TPU v7x, 32 devices: a whole 2x2x4 slice. The times are simulated.
32 devices in a mesh: fsdp: 4 (over z), ctx: 4 (over x, core), tp: 2 (over y).
Axes of the slice: x: 2, y: 2, z: 4, core: 2. Of those that a mesh axis runs over, the one named last changes fastest.
Arguments:
- tokens: bfloat16 [4, 2048, 1536], P('fsdp', 'ctx'), may hold values from -25 to 25
- lengths: int32 [4], P('fsdp'), may hold values from 512 to 2048, as said below
- routes: int32 [4, 2048, 8], P('fsdp', 'ctx'), may hold values from 0 to 15, all different within a row
- visit_order: int32 [4, 4, 4096], P('fsdp', 'ctx'), may hold values from 0 to 4095, each once within a row
- cotangent: bfloat16 [4, 2048, 1536], P('fsdp', 'ctx'), may hold values from -6 to 6
- first_gain: bfloat16 [1536], P('fsdp'), may hold values from 0.099609375 to 1.8984375
- query_weight: bfloat16 [1536, 1536], P('fsdp', 'tp'), may hold values from -0.15625 to 0.15625
- key_matrix: bfloat16 [1536, 512], P('fsdp', 'tp'), may hold values from -0.15625 to 0.15625
- value_matrix: bfloat16 [1536, 512], P('fsdp', 'tp'), may hold values from -0.15625 to 0.15625
- output_weight: bfloat16 [1536, 1536], P('tp', 'fsdp'), may hold values from -3.5 to 3.5
- second_gain: bfloat16 [1536], P('fsdp'), may hold values from 0.099609375 to 1.8984375
- router_weight: bfloat16 [1536, 16], P('fsdp'), may hold values from -0.078125 to 0.078125
- gate_weight: bfloat16 [16, 1536, 512], P('fsdp', None, 'tp'), may hold values from -0.15625 to 0.15625
- up_weight: bfloat16 [16, 1536, 512], P('fsdp', None, 'tp'), may hold values from -0.15625 to 0.15625
- down_weight: bfloat16 [16, 512, 1536], P('fsdp', 'tp'), may hold values from -0.75 to 0.75
Outputs:
- layer_out: bfloat16 [4, 2048, 1536], P('fsdp', 'ctx')
- grad_tokens: float32 [4, 2048, 1536], P('fsdp', 'ctx')
- grad_first_gain: float32 [1536], P('fsdp')
- grad_query_weight: float32 [1536, 1536], P('fsdp', 'tp')
- grad_key_weight: float32 [1536, 512], P('fsdp', 'tp')
- grad_value_weight: float32 [1536, 512], P('fsdp', 'tp')
- grad_output_weight: float32 [1536, 1536], P('tp', 'fsdp')
- grad_second_gain: float32 [1536], P('fsdp')
- grad_router_weight: float32 [1536, 16], P('fsdp')
- grad_gate_weight: float32 [16, 1536, 512], P('fsdp', None, 'tp')
- grad_up_weight: float32 [16, 1536, 512], P('fsdp', None, 'tp')
- grad_down_weight: float32 [16, 512, 1536], P('fsdp', 'tp')
Inputs may be any that keep to these rules, and one draw needn't show every extreme that they name: `lengths`: in every draw some sequence has length 2048. `routes`: the 8 experts of a token are different. `visit_order`: for each sequence and block, the entries are a permutation of the block's pair numbers.
All inputs are finite; a program needn't handle non-finite values.
Results may differ from a plain program's by a relative error of at most 0.028.
Values may be sent and summed in bfloat16 or wider, within the bound.
No kernel may reach another device: no remote copies, remote signals or barrier semaphores. Data moves between devices by JAX's collectives and lax.ppermute only.
A program may use at most 256 MiB of HBM per device.

v0:
```python
import math

import jax
import jax.numpy as jnp
from jax import lax
from jax.sharding import PartitionSpec as P

HEAD_SIZE = 64
TOPK = 8
E = 16
SCORE_BLOCK = 512
CAP = 256


EPSILON = 1e-06


def tensor_total(partial_value):
    return lax.psum(partial_value.astype(jnp.bfloat16), "tp").astype(jnp.float32)


def normalize(values):
    inverse_rms = lax.rsqrt(jnp.mean(values * values, axis=-1, keepdims=True) + EPSILON)
    return (inverse_rms, values * inverse_rms)


def norm_backward(grad_scaled, gain, inverse_rms, normed):
    scaled = grad_scaled * gain
    return inverse_rms * (scaled - normed * jnp.mean(scaled * normed, axis=-1, keepdims=True))


def rotation_tables(positions):
    half_dim = HEAD_SIZE // 2
    frequency = jnp.exp(
        jnp.arange(half_dim, dtype=jnp.float32) * (-2.0 * math.log(10000.0) / HEAD_SIZE)
    )
    angles = positions.astype(jnp.float32)[:, None] * frequency[None, :]
    return (jnp.cos(angles)[:, None, :], jnp.sin(angles)[:, None, :])


def rotate(values, cosine_table, sine_table, inverse):
    row_count = values.shape[0]
    head_count = values.shape[1] // HEAD_SIZE
    shaped = values.reshape(row_count, head_count, HEAD_SIZE)
    first_half = shaped[:, :, : HEAD_SIZE // 2]
    second_half = shaped[:, :, HEAD_SIZE // 2 :]
    if inverse:
        joined = jnp.concatenate(
            [
                first_half * cosine_table + second_half * sine_table,
                second_half * cosine_table - first_half * sine_table,
            ],
            axis=-1,
        )
    else:
        joined = jnp.concatenate(
            [
                first_half * cosine_table - second_half * sine_table,
                second_half * cosine_table + first_half * sine_table,
            ],
            axis=-1,
        )
    return joined.reshape(row_count, head_count * HEAD_SIZE)


def plan_pairs(route_rows, ranked, live_rows):
    pair_count = route_rows.shape[0] * route_rows.shape[1]
    pair_expert = route_rows.reshape(-1)
    pair_live = jnp.repeat(live_rows, route_rows.shape[1])
    ranked_expert = pair_expert[ranked]
    ranked_live = pair_live[ranked]
    expert_hits = (
        (ranked_expert[:, None] == jnp.arange(E, dtype=jnp.int32)[None, :]) & ranked_live[:, None]
    ).astype(jnp.int32)
    earlier = jnp.cumsum(expert_hits, axis=0) - expert_hits
    slot_place = jnp.sum(earlier * expert_hits, axis=1)
    is_kept = ranked_live & (slot_place < CAP)
    slot_index = jnp.where(is_kept, ranked_expert * CAP + slot_place, E * CAP)
    slot_pair = (
        jnp.full((E * CAP + 1,), pair_count, jnp.int32).at[slot_index].set(ranked)[: E * CAP]
    )
    pair_slot = jnp.full((pair_count,), E * CAP, jnp.int32).at[ranked].set(slot_index)
    return (slot_pair, pair_slot)


def experts_forward(expert_input, gate_used, up_used, down_used):
    split_view = expert_input.reshape(
        -1, gate_used.shape[0], expert_input.shape[1], expert_input.shape[2]
    )
    gate_pre = jnp.einsum(
        "secd,edf->secf", split_view, gate_used, preferred_element_type=jnp.float32
    )
    up_pre = jnp.einsum("secd,edf->secf", split_view, up_used, preferred_element_type=jnp.float32)
    hidden_mid = (jax.nn.silu(gate_pre) * up_pre).astype(jnp.bfloat16)
    produced = jnp.einsum(
        "secf,efd->secd", hidden_mid, down_used, preferred_element_type=jnp.float32
    ).astype(jnp.bfloat16)
    return (produced.reshape(expert_input.shape), gate_pre, up_pre, hidden_mid)


def experts_backward(
    expert_input, slot_grad, gate_pre, up_pre, hidden_mid, gate_used, up_used, down_used
):
    split_view = expert_input.reshape(
        -1, gate_used.shape[0], expert_input.shape[1], expert_input.shape[2]
    )
    grad_view = slot_grad.reshape(split_view.shape)
    hidden_grad = jnp.einsum(
        "secd,efd->secf", grad_view, down_used, preferred_element_type=jnp.float32
    )
    sigmoid_gate = jax.nn.sigmoid(gate_pre)
    gate_grad = (
        hidden_grad * up_pre * sigmoid_gate * (1.0 + gate_pre * (1.0 - sigmoid_gate))
    ).astype(jnp.bfloat16)
    up_grad = (hidden_grad * gate_pre * sigmoid_gate).astype(jnp.bfloat16)
    input_grad = (
        jnp.einsum("secf,edf->secd", gate_grad, gate_used, preferred_element_type=jnp.float32)
        + jnp.einsum("secf,edf->secd", up_grad, up_used, preferred_element_type=jnp.float32)
    ).astype(jnp.bfloat16)
    grad_gate_part = jnp.einsum(
        "secd,secf->edf", split_view, gate_grad, preferred_element_type=jnp.float32
    )
    grad_up_part = jnp.einsum(
        "secd,secf->edf", split_view, up_grad, preferred_element_type=jnp.float32
    )
    grad_down_part = jnp.einsum(
        "secf,secd->efd", hidden_mid, grad_view, preferred_element_type=jnp.float32
    )
    return (input_grad.reshape(slot_grad.shape), grad_gate_part, grad_up_part, grad_down_part)


def block_scores(query_block, query_start, key_head_rows, key_index, length):
    block_rows = jnp.arange(SCORE_BLOCK, dtype=jnp.int32)
    key_start = key_index * SCORE_BLOCK
    key_block = lax.dynamic_slice_in_dim(key_head_rows, key_start, SCORE_BLOCK, 0)
    scores = jnp.einsum(
        "qhgd,khd->hgqk", query_block, key_block, preferred_element_type=jnp.float32
    ) * HEAD_SIZE ** (-0.5)
    key_pos = key_start + block_rows
    allowed = (key_pos[None, :] <= query_start + block_rows[:, None]) & (key_pos[None, :] < length)
    return (jnp.where(allowed, scores, -jnp.inf), key_start, key_block)


def attention_forward(query_rows, keys_all, every_value, first_row, length):
    row_count = query_rows.shape[0]
    kv_heads = keys_all.shape[1] // HEAD_SIZE
    heads_per_group = query_rows.shape[1] // HEAD_SIZE // kv_heads
    block_count = row_count // SCORE_BLOCK
    query_block_list = query_rows.reshape(
        block_count, SCORE_BLOCK, kv_heads, heads_per_group, HEAD_SIZE
    )
    key_head_rows = keys_all.reshape(-1, kv_heads, HEAD_SIZE)
    value_head_rows = every_value.reshape(-1, kv_heads, HEAD_SIZE)

    def one_block(item):
        block_index, query_block = item
        query_start = first_row + block_index * SCORE_BLOCK
        key_count = jnp.minimum(
            query_start // SCORE_BLOCK + 1, (length + SCORE_BLOCK - 1) // SCORE_BLOCK
        )

        def first_pass(key_index, carry):
            running_max, running_sum = carry
            scores, key_start, key_block = block_scores(
                query_block, query_start, key_head_rows, key_index, length
            )
            new_max = jnp.maximum(running_max, jnp.max(scores, axis=-1))
            running_sum = running_sum * jnp.exp(running_max - new_max) + jnp.sum(
                jnp.exp(scores - new_max[..., None]), axis=-1
            )
            return (new_max, running_sum)

        start_max = jnp.full((kv_heads, heads_per_group, SCORE_BLOCK), -jnp.inf, jnp.float32)
        start_sum = jnp.zeros((kv_heads, heads_per_group, SCORE_BLOCK), jnp.float32)
        running_max, running_sum = lax.fori_loop(0, key_count, first_pass, (start_max, start_sum))
        log_total = running_max + jnp.log(running_sum)

        def second_pass(key_index, output_sum):
            scores, key_start, key_block = block_scores(
                query_block, query_start, key_head_rows, key_index, length
            )
            probs = jnp.exp(scores - log_total[..., None]).astype(jnp.bfloat16)
            value_block = lax.dynamic_slice_in_dim(value_head_rows, key_start, SCORE_BLOCK, 0)
            return output_sum + jnp.einsum(
                "hgqk,khd->qhgd", probs, value_block, preferred_element_type=jnp.float32
            )

        start_out = jnp.zeros((SCORE_BLOCK, kv_heads, heads_per_group, HEAD_SIZE), jnp.float32)
        attended = lax.fori_loop(0, key_count, second_pass, start_out)
        return (attended, log_total)

    attended, log_total = lax.map(
        one_block, (jnp.arange(block_count, dtype=jnp.int32), query_block_list)
    )
    return (attended.reshape(row_count, -1), log_total)


def attention_backward(
    query_rows, keys_all, every_value, grad_attended, attended, log_total, first_row, length
):
    row_count = query_rows.shape[0]
    kv_heads = keys_all.shape[1] // HEAD_SIZE
    heads_per_group = query_rows.shape[1] // HEAD_SIZE // kv_heads
    block_count = row_count // SCORE_BLOCK
    score_scale = HEAD_SIZE ** (-0.5)
    query_block_list = query_rows.reshape(
        block_count, SCORE_BLOCK, kv_heads, heads_per_group, HEAD_SIZE
    )
    grad_blocks = grad_attended.reshape(
        block_count, SCORE_BLOCK, kv_heads, heads_per_group, HEAD_SIZE
    )
    key_head_rows = keys_all.reshape(-1, kv_heads, HEAD_SIZE)
    value_head_rows = every_value.reshape(-1, kv_heads, HEAD_SIZE)
    row_delta = jnp.sum(
        grad_attended.astype(jnp.float32).reshape(
            block_count, SCORE_BLOCK, kv_heads, heads_per_group, HEAD_SIZE
        )
        * attended.reshape(block_count, SCORE_BLOCK, kv_heads, heads_per_group, HEAD_SIZE),
        axis=-1,
    )
    row_delta = jnp.transpose(row_delta, (0, 2, 3, 1))

    def one_block(carry, item):
        block_index, query_block, grad_block, delta_block, total_block = item
        query_start = first_row + block_index * SCORE_BLOCK
        key_count = jnp.minimum(
            query_start // SCORE_BLOCK + 1, (length + SCORE_BLOCK - 1) // SCORE_BLOCK
        )

        def key_step(key_index, inner):
            grad_query, grad_keys, grad_values = inner
            scores, key_start, key_block = block_scores(
                query_block, query_start, key_head_rows, key_index, length
            )
            probs = jnp.exp(scores - total_block[..., None])
            value_block = lax.dynamic_slice_in_dim(value_head_rows, key_start, SCORE_BLOCK, 0)
            grad_probs = jnp.einsum(
                "qhgd,khd->hgqk", grad_block, value_block, preferred_element_type=jnp.float32
            )
            grad_scores = (probs * (grad_probs - delta_block[..., None])).astype(jnp.bfloat16)
            grad_query = (
                grad_query
                + jnp.einsum(
                    "hgqk,khd->qhgd", grad_scores, key_block, preferred_element_type=jnp.float32
                )
                * score_scale
            )
            key_part = (
                jnp.einsum(
                    "hgqk,qhgd->khd", grad_scores, query_block, preferred_element_type=jnp.float32
                )
                * score_scale
            )
            value_part = jnp.einsum(
                "hgqk,qhgd->khd",
                probs.astype(jnp.bfloat16),
                grad_block,
                preferred_element_type=jnp.float32,
            )
            grad_keys = lax.dynamic_update_slice_in_dim(
                grad_keys,
                lax.dynamic_slice_in_dim(grad_keys, key_start, SCORE_BLOCK, 0) + key_part,
                key_start,
                0,
            )
            grad_values = lax.dynamic_update_slice_in_dim(
                grad_values,
                lax.dynamic_slice_in_dim(grad_values, key_start, SCORE_BLOCK, 0) + value_part,
                key_start,
                0,
            )
            return (grad_query, grad_keys, grad_values)

        start_query = jnp.zeros((SCORE_BLOCK, kv_heads, heads_per_group, HEAD_SIZE), jnp.float32)
        grad_query, grad_keys, grad_values = lax.fori_loop(
            0, key_count, key_step, (start_query, carry[0], carry[1])
        )
        return ((grad_keys, grad_values), grad_query)

    start_keys = jnp.zeros(key_head_rows.shape, jnp.float32)
    (grad_keys, grad_values), grad_query = lax.scan(
        one_block,
        (start_keys, start_keys),
        (
            jnp.arange(block_count, dtype=jnp.int32),
            query_block_list,
            grad_blocks,
            row_delta,
            log_total,
        ),
    )
    return (
        grad_query.reshape(row_count, -1),
        grad_keys.reshape(keys_all.shape[0], -1),
        grad_values.reshape(keys_all.shape[0], -1),
    )


def local(
    tokens,
    lengths,
    routes,
    visit_order,
    cotangent,
    first_gain,
    query_weight,
    key_matrix,
    value_matrix,
    output_weight,
    second_gain,
    router_weight,
    gate_weight,
    up_weight,
    down_weight,
):
    row_count = tokens.shape[1]
    width = tokens.shape[2]
    first_row = lax.axis_index("ctx") * row_count
    positions = first_row + jnp.arange(row_count, dtype=jnp.int32)
    length = lengths[0]
    live_rows = positions < length
    valid = live_rows.astype(jnp.float32)[:, None]
    gain_first, query_full, key_full, value_full, output_full, gain_second, router_full = (
        lax.all_gather(first_gain, "fsdp", axis=0, tiled=True),
        lax.all_gather(query_weight, "fsdp", axis=0, tiled=True),
        lax.all_gather(key_matrix, "fsdp", axis=0, tiled=True),
        lax.all_gather(value_matrix, "fsdp", axis=0, tiled=True),
        lax.all_gather(output_weight, "fsdp", axis=1, tiled=True),
        lax.all_gather(second_gain, "fsdp", axis=0, tiled=True),
        lax.all_gather(router_weight, "fsdp", axis=0, tiled=True),
    )
    gain_first = gain_first.astype(jnp.float32)
    gain_second = gain_second.astype(jnp.float32)
    inputs = tokens[0].astype(jnp.float32)
    inverse_one, normed_one = normalize(inputs)
    hidden_one = (normed_one * gain_first).astype(jnp.bfloat16)
    cosine_table, sine_table = rotation_tables(positions)
    query_rows = rotate(
        jnp.dot(hidden_one, query_full, preferred_element_type=jnp.float32),
        cosine_table,
        sine_table,
        False,
    ).astype(jnp.bfloat16)
    keys_local = rotate(
        jnp.dot(hidden_one, key_full, preferred_element_type=jnp.float32),
        cosine_table,
        sine_table,
        False,
    ).astype(jnp.bfloat16)
    values_local = jnp.dot(hidden_one, value_full, preferred_element_type=jnp.float32).astype(
        jnp.bfloat16
    )
    keys_all, every_value = (
        lax.all_gather(keys_local, "ctx", axis=0, tiled=True),
        lax.all_gather(values_local, "ctx", axis=0, tiled=True),
    )
    attended, log_total = attention_forward(query_rows, keys_all, every_value, first_row, length)
    attended_low = attended.astype(jnp.bfloat16)
    residual = inputs + tensor_total(
        jnp.dot(attended_low, output_full, preferred_element_type=jnp.float32)
    )
    inverse_two, normed_two = normalize(residual)
    hidden_two = (normed_two * gain_second).astype(jnp.bfloat16)
    logits = jnp.dot(hidden_two, router_full, preferred_element_type=jnp.float32)
    route_rows = routes[0]
    route_onehot = (route_rows[:, :, None] == jnp.arange(E, dtype=jnp.int32)[None, None, :]).astype(
        jnp.float32
    )
    gate_weights = jax.nn.softmax(jnp.sum(route_onehot * logits[:, None, :], axis=-1), axis=-1)
    slot_pair, pair_slot = plan_pairs(route_rows, visit_order[0, 0], live_rows)
    slot_token = slot_pair // TOPK
    hidden_pad = jnp.concatenate([hidden_two, jnp.zeros((1, width), jnp.bfloat16)], axis=0)
    dispatched = hidden_pad[slot_token].reshape(E, CAP, width)
    gate_pad = jnp.concatenate([gate_weights.reshape(-1), jnp.zeros((1,), jnp.float32)], axis=0)
    slot_gate = gate_pad[slot_pair]
    gate_used, up_used, down_used = (
        lax.all_gather(gate_weight, "fsdp", axis=0, tiled=True),
        lax.all_gather(up_weight, "fsdp", axis=0, tiled=True),
        lax.all_gather(down_weight, "fsdp", axis=0, tiled=True),
    )
    expert_out, gate_pre, up_pre, hidden_mid = experts_forward(
        dispatched, gate_used, up_used, down_used
    )
    out_pad = jnp.concatenate(
        [expert_out.reshape(E * CAP, width), jnp.zeros((1, width), jnp.bfloat16)], axis=0
    )
    pair_out = out_pad[pair_slot].reshape(row_count, TOPK, width).astype(jnp.float32)
    mixture = tensor_total(jnp.sum(gate_weights[:, :, None] * pair_out, axis=1))
    layer_out = (valid * (residual + mixture)).astype(jnp.bfloat16)[None]
    grad_out = cotangent[0].astype(jnp.float32) * valid
    grad_out_pad = jnp.concatenate([grad_out, jnp.zeros((1, width), jnp.float32)], axis=0)
    slot_grad = (
        (grad_out_pad[slot_token] * slot_gate[:, None]).astype(jnp.bfloat16).reshape(E, CAP, width)
    )
    gate_grad_part = jnp.sum(grad_out[:, None, :] * pair_out, axis=-1)
    input_grad, grad_gate_full, grad_up_full, grad_down_full = experts_backward(
        dispatched, slot_grad, gate_pre, up_pre, hidden_mid, gate_used, up_used, down_used
    )
    grad_gate_w, grad_up_w, grad_down_w = (
        lax.psum_scatter(
            grad_gate_full.astype(jnp.bfloat16), "fsdp", scatter_dimension=0, tiled=True
        ).astype(jnp.float32),
        lax.psum_scatter(
            grad_up_full.astype(jnp.bfloat16), "fsdp", scatter_dimension=0, tiled=True
        ).astype(jnp.float32),
        lax.psum_scatter(
            grad_down_full.astype(jnp.bfloat16), "fsdp", scatter_dimension=0, tiled=True
        ).astype(jnp.float32),
    )
    input_pad = jnp.concatenate(
        [input_grad.reshape(E * CAP, width), jnp.zeros((1, width), jnp.bfloat16)], axis=0
    )
    hidden_grad_part = jnp.sum(
        input_pad[pair_slot].reshape(row_count, TOPK, width).astype(jnp.float32), axis=1
    )
    hidden_grad, gate_grad = (
        lax.psum(hidden_grad_part.astype(jnp.bfloat16), "tp").astype(jnp.float32),
        lax.psum(gate_grad_part.astype(jnp.bfloat16), "tp").astype(jnp.float32),
    )
    logit_route_grad = gate_weights * (
        gate_grad - jnp.sum(gate_weights * gate_grad, axis=-1, keepdims=True)
    )
    logit_grad = jnp.sum(logit_route_grad[:, :, None] * route_onehot, axis=1).astype(jnp.bfloat16)
    hidden_grad = hidden_grad + jnp.einsum(
        "re,de->rd", logit_grad, router_full, preferred_element_type=jnp.float32
    )
    grad_router_w = jnp.einsum(
        "rd,re->de", hidden_two, logit_grad, preferred_element_type=jnp.float32
    )
    grad_second_w = jnp.sum(hidden_grad * normed_two, axis=0)
    residual_grad = grad_out + norm_backward(hidden_grad, gain_second, inverse_two, normed_two)
    branch_grad = residual_grad.astype(jnp.bfloat16)
    grad_output_w = jnp.einsum(
        "rh,rd->hd", attended_low, branch_grad, preferred_element_type=jnp.float32
    )
    attended_grad = jnp.einsum(
        "rd,hd->rh", branch_grad, output_full, preferred_element_type=jnp.float32
    ).astype(jnp.bfloat16)
    grad_query_rot, grad_keys_all, grad_values_all = attention_backward(
        query_rows, keys_all, every_value, attended_grad, attended, log_total, first_row, length
    )
    grad_keys_rot, grad_values_local = (
        lax.psum_scatter(
            grad_keys_all.astype(jnp.bfloat16), "ctx", scatter_dimension=0, tiled=True
        ).astype(jnp.float32),
        lax.psum_scatter(
            grad_values_all.astype(jnp.bfloat16), "ctx", scatter_dimension=0, tiled=True
        ).astype(jnp.float32),
    )
    query_raw_grad = rotate(grad_query_rot, cosine_table, sine_table, True).astype(jnp.bfloat16)
    key_raw_grad = rotate(grad_keys_rot, cosine_table, sine_table, True).astype(jnp.bfloat16)
    value_raw_grad = grad_values_local.astype(jnp.bfloat16)
    grad_query_w = jnp.einsum(
        "rd,rf->df", hidden_one, query_raw_grad, preferred_element_type=jnp.float32
    )
    grad_key_w = jnp.einsum(
        "rd,rf->df", hidden_one, key_raw_grad, preferred_element_type=jnp.float32
    )
    grad_value_w = jnp.einsum(
        "rd,rf->df", hidden_one, value_raw_grad, preferred_element_type=jnp.float32
    )
    first_grad_part = (
        jnp.einsum("rf,df->rd", query_raw_grad, query_full, preferred_element_type=jnp.float32)
        + jnp.einsum("rf,df->rd", key_raw_grad, key_full, preferred_element_type=jnp.float32)
        + jnp.einsum("rf,df->rd", value_raw_grad, value_full, preferred_element_type=jnp.float32)
    )
    first_grad = tensor_total(first_grad_part)
    grad_first_w = jnp.sum(first_grad * normed_one, axis=0)
    grad_inputs = residual_grad + norm_backward(first_grad, gain_first, inverse_one, normed_one)
    shard_first, shard_query, shard_key, shard_value, shard_output, shard_second, shard_router = (
        lax.psum_scatter(
            grad_first_w.astype(jnp.bfloat16), "fsdp", scatter_dimension=0, tiled=True
        ).astype(jnp.float32),
        lax.psum_scatter(
            grad_query_w.astype(jnp.bfloat16), "fsdp", scatter_dimension=0, tiled=True
        ).astype(jnp.float32),
        lax.psum_scatter(
            grad_key_w.astype(jnp.bfloat16), "fsdp", scatter_dimension=0, tiled=True
        ).astype(jnp.float32),
        lax.psum_scatter(
            grad_value_w.astype(jnp.bfloat16), "fsdp", scatter_dimension=0, tiled=True
        ).astype(jnp.float32),
        lax.psum_scatter(
            grad_output_w.astype(jnp.bfloat16), "fsdp", scatter_dimension=1, tiled=True
        ).astype(jnp.float32),
        lax.psum_scatter(
            grad_second_w.astype(jnp.bfloat16), "fsdp", scatter_dimension=0, tiled=True
        ).astype(jnp.float32),
        lax.psum_scatter(
            grad_router_w.astype(jnp.bfloat16), "fsdp", scatter_dimension=0, tiled=True
        ).astype(jnp.float32),
    )
    summed = (
        lax.psum(shard_first.astype(jnp.bfloat16), "ctx").astype(jnp.float32),
        lax.psum(shard_query.astype(jnp.bfloat16), "ctx").astype(jnp.float32),
        lax.psum(shard_key.astype(jnp.bfloat16), "ctx").astype(jnp.float32),
        lax.psum(shard_value.astype(jnp.bfloat16), "ctx").astype(jnp.float32),
        lax.psum(shard_output.astype(jnp.bfloat16), "ctx").astype(jnp.float32),
        lax.psum(shard_second.astype(jnp.bfloat16), "ctx").astype(jnp.float32),
        lax.psum(shard_router.astype(jnp.bfloat16), "ctx").astype(jnp.float32),
        lax.psum(grad_gate_w.astype(jnp.bfloat16), "ctx").astype(jnp.float32),
        lax.psum(grad_up_w.astype(jnp.bfloat16), "ctx").astype(jnp.float32),
        lax.psum(grad_down_w.astype(jnp.bfloat16), "ctx").astype(jnp.float32),
    )
    return (
        layer_out,
        grad_inputs[None],
        summed[0],
        summed[1],
        summed[2],
        summed[3],
        summed[4],
        summed[5],
        summed[6],
        summed[7],
        summed[8],
        summed[9],
    )


def solution(mesh):
    placed = (
        P("fsdp", "ctx", None),
        P("fsdp"),
        P("fsdp", "ctx", None),
        P("fsdp", "ctx", None),
        P("fsdp", "ctx", None),
        P("fsdp"),
        P("fsdp", "tp"),
        P("fsdp", "tp"),
        P("fsdp", "tp"),
        P("tp", "fsdp"),
        P("fsdp"),
        P("fsdp", None),
        P("fsdp", None, "tp"),
        P("fsdp", None, "tp"),
        P("fsdp", "tp", None),
    )
    return jax.shard_map(
        local,
        mesh=mesh,
        in_specs=placed,
        out_specs=(
            P("fsdp", "ctx", None),
            P("fsdp", "ctx", None),
            P("fsdp"),
            P("fsdp", "tp"),
            P("fsdp", "tp"),
            P("fsdp", "tp"),
            P("tp", "fsdp"),
            P("fsdp"),
            P("fsdp", None),
            P("fsdp", None, "tp"),
            P("fsdp", None, "tp"),
            P("fsdp", "tp", None),
        ),
        check_vma=False,
    )
```

profile of v0, /device:TPU:1, one launch (start us, length us, event | category | flops | bytes accessed | tf_op | source)
XLA Modules:
  0.0 2400.2 jit_solution(3122014991507985553)
XLA Ops:
  63.5 49.4 %all-gather.14.cloned.1.call-done = bf16[1536,768]{1,0:T(8,128)(2,1)} async-done(((bf16[384,768]{1,0:T(8,128)(2,1)}), bf16[1536,768]{1,0:T(8,128)(2,1)}) %all-gather.14.cloned.1.call-update) | async-done | bytes 2359312 | tf_op jit(solution)/shard_map/all_gather | solution.py:325
  158.0 24.3 %all-gather.16.cloned.1.call-done = bf16[768,1536]{1,0:T(8,128)(2,1)} async-done(((bf16[768,384]{1,0:T(8,128)(2,1)}), bf16[768,1536]{1,0:T(8,128)(2,1)}) %all-gather.16.cloned.1.call-update) | async-done | bytes 2359312 | tf_op jit(solution)/shard_map/all_gather | solution.py:328
  198.8 23.0 gather_fusion.1
  221.9 25.6 %gather_fusion = pred[4096]{0:T(1024)(128)(4,1)S(1)} fusion(pred[4096]{0:T(1024)(128)(4,1)S(1)} %reshape.500, s32[4096]{0:T(1024)S(1)} %broadcast_clamp_fusion), kind=kCustom, calls=%fused_computation | custom fusion | bytes 24576 | tf_op jit(solution)/shard_map/gather | solution.py:71
  286.3 20.7 gather_fusion.4
  351.5 23.0 gather_fusion.5
  374.6 86.1 %all-gather.18.cloned.1.call-done = bf16[16,1536,256]{2,1,0:T(8,128)(2,1)} async-done(((bf16[4,1536,256]{2,1,0:T(8,128)(2,1)}), bf16[16,1536,256]{2,1,0:T(8,128)(2,1)}) %all-gather.18.cloned.1.call-update) | async-done | bytes 12582928 | tf_op jit(solution)/shard_map/all_gather | solution.py:377
  475.0 203.7 %all-gather.20.cloned.1.call-done = bf16[16,1536,256]{2,1,0:T(8,128)(2,1)} async-done(((bf16[4,1536,256]{2,1,0:T(8,128)(2,1)}), bf16[16,1536,256]{2,1,0:T(8,128)(2,1)}) %all-gather.20.cloned.1.call-update) | async-done | bytes 12582928 | tf_op jit(solution)/shard_map/all_gather | solution.py:378
  693.1 203.7 %all-gather.22.cloned.1.call-done = bf16[16,256,1536]{2,1,0:T(8,128)(2,1)} async-done(((bf16[4,256,1536]{2,1,0:T(8,128)(2,1)}), bf16[16,256,1536]{2,1,0:T(8,128)(2,1)}) %all-gather.22.cloned.1.call-update) | async-done | bytes 12582928 | tf_op jit(solution)/shard_map/all_gather | solution.py:379
  896.8 24.4 %fusion.65 = (bf16[1,16,256,256]{3,2,1,0:T(8,128)(2,1)}, bf16[1,16,256,256]{3,2,1,0:T(8,128)(2,1)S(1)}, bf16[1,16,256,256]{3,2,1,0:T(8,128)(2,1)}) fusion(f32[16,256,256]{2,1,0:T(8,128)} %fusion.138, f32[16,256,256]{2,1,0:T(8,128)} %fusion.139, bf16[16,256,1536]{2,1,0:T(8,128)(2,1)} %all-gather.22.cloned.1.call-done, f32[16,256,1536]{2,1,0:T(8,128)} %bitcast.404, ...), kind=kOutput, calls=%fused_computation.92 | convolution fusion | flops 3250585600 | bytes 52445184 | tf_op jit(solution)/shard_map/secd,efd->secf/dot_general | solution.py:108
  988.1 31.5 %gather_fusion.3 = bf16[4096,1536]{1,0:T(8,128)(2,1)} fusion(bf16[4097,1536]{1,0:T(8,128)(2,1)} %concatenate.32, s32[4096]{0:T(1024)S(1)} %copy-done.48), kind=kCustom, calls=%fused_computation.3 | custom fusion | bytes 25182208 | tf_op jit(solution)/shard_map/gather | solution.py:387
  1019.6 31.5 %gather_fusion.6 = bf16[4096,1536]{1,0:T(8,128)(2,1)} fusion(bf16[4097,1536]{1,0:T(8,128)(2,1)} %concatenate.35, s32[4096]{0:T(1024)S(1)} %copy-done.48), kind=kCustom, calls=%fused_computation.6 | custom fusion | bytes 25182208 | tf_op jit(solution)/shard_map/gather | solution.py:414
  1087.1 26.2 %all-reduce.17.cloned.1.call-done = bf16[512,1536]{1,0:T(8,128)(2,1)} async-done(((bf16[512,1536]{1,0:T(8,128)(2,1)}), bf16[512,1536]{1,0:T(8,128)(2,1)}) %all-reduce.17.cloned.1.call-update) | async-done | bytes 1572880 | tf_op jit(solution)/shard_map/psum | solution.py:417
  1127.3 42.0 %while.61 = (s32[]{:T(128)}, f32[512,4,3,64]{0,3,2,1:T(8,128)}, f32[2048,4,64]{0,2,1:T(8,128)}, f32[2048,4,64]{0,2,1:T(8,128)}, s32[]{:T(128)}, /*index=5*/bf16[...) while((s32[]{:T(128)}, f32[512,4,3,64]{0,3,2,1:T(8,128)}, ...), condition=%wide.region_28.29_spmd, body=%wide.region_27.28_spmd.sunk | while | flops 2046429184 | bytes 83445040 | solution.py:275
  1183.4 54.8 %reduce-scatter.15.cloned.1.call-done = bf16[512,256]{0,1:T(8,128)(2,1)} async-done(((bf16[2048,256]{0,1:T(8,128)(2,1)}), bf16[512,256]{0,1:T(8,128)(2,1)}) %reduce-scatter.15.cloned.1.call-update) | async-done | bytes 262160 | tf_op jit(solution)/shard_map/reduce_scatter | solution.py:443
  1241.1 25.3 %reduce-scatter.17.cloned.1.call-done = bf16[512,256]{0,1:T(8,128)(2,1)} async-done(((bf16[2048,256]{0,1:T(8,128)(2,1)}), bf16[512,256]{0,1:T(8,128)(2,1)}) %reduce-scatter.17.cloned.1.call-update) | async-done | bytes 262160 | tf_op jit(solution)/shard_map/reduce_scatter | solution.py:446
  1341.1 25.3 %reduce-scatter.23.cloned.1.call-done = bf16[384,256]{1,0:T(8,128)(2,1)} async-done(((bf16[1536,256]{1,0:T(8,128)(2,1)}), bf16[384,256]{1,0:T(8,128)(2,1)}) %reduce-scatter.23.cloned.1.call-update) | async-done | bytes 196624 | tf_op jit(solution)/shard_map/reduce_scatter | solution.py:480
  1366.4 51.2 %reduce-scatter.19.cloned.1.call-done = bf16[384,768]{1,0:T(8,128)(2,1)} async-done(((bf16[1536,768]{1,0:T(8,128)(2,1)}), bf16[384,768]{1,0:T(8,128)(2,1)}) %reduce-scatter.19.cloned.1.call-update) | async-done | bytes 589840 | tf_op jit(solution)/shard_map/reduce_scatter | solution.py:474
  1417.6 213.8 %reduce-scatter.25.cloned.1.call-done = bf16[4,1536,256]{2,1,0:T(8,128)(2,1)} async-done(((bf16[16,1536,256]{2,1,0:T(8,128)(2,1)}), bf16[4,1536,256]{2,1,0:T(8,128)(2,1)}) %reduce-scatter.25.cloned.1.call-update) | async-done | bytes 3145744 | tf_op jit(solution)/shard_map/reduce_scatter | solution.py:400
  1631.4 215.1 %reduce-scatter.27.cloned.1.call-done = bf16[4,1536,256]{2,1,0:T(8,128)(2,1)} async-done(((bf16[16,1536,256]{2,1,0:T(8,128)(2,1)}), bf16[4,1536,256]{2,1,0:T(8,128)(2,1)}) %reduce-scatter.27.cloned.1.call-update) | async-done | bytes 3145744 | tf_op jit(solution)/shard_map/reduce_scatter | solution.py:403
  1846.5 215.1 %reduce-scatter.29.cloned.1.call-done = bf16[4,256,1536]{2,1,0:T(8,128)(2,1)} async-done(((bf16[16,256,1536]{2,1,0:T(8,128)(2,1)}), bf16[4,256,1536]{2,1,0:T(8,128)(2,1)}) %reduce-scatter.29.cloned.1.call-update) | async-done | bytes 3145744 | tf_op jit(solution)/shard_map/reduce_scatter | solution.py:406
  2063.5 21.4 reduce-scatter.33.cloned.1.call-done
  2085.9 88.0 %all-reduce.21.cloned.1.call-done = (bf16[512,1536]{1,0:T(8,128)(2,1)}, bf16[512,1536]{1,0:T(8,128)(2,1)}) async-done(((bf16[512,1536]{1,0:T(8,128)(2,1)}, bf16[512,1536]{1,0:T(8,128)(2,1)}), (bf16[512,1536]{1,0:T(8,128)(2,1)}, bf16[512,1536]{1,0:T(8,128)(2,1)})) %all-reduce.21.cloned.1.call-update) | async-done | bytes 3145744 | tf_op jit(solution)/shard_map/psum | solution.py:19
  2205.8 169.5 %all-reduce.19.cloned.1.call-done = (bf16[384,768]{1,0:T(8,128)(2,1)}, bf16[384,256]{1,0:T(8,128)(2,1)}, bf16[384,256]{1,0:T(8,128)(2,1)}, bf16[768,384]{1,0:T(8...) async-done(((bf16[384,768]{1,0:T(8,128)(2,1)}, bf16[384,256]{1,0:T(8,128)(2,1)}, ...) | async-done | bytes 11010064 | tf_op jit(solution)/shard_map/psum | solution.py:495
  (365 shorter events, 555.3 us)
Async XLA Ops:
  7.2 54.0 %all-gather.10.cloned.1.call-start = ((), (), s32[]{:S(2)}) async-start(), calls=%async_computation.10 | async-start | bytes 1310720 | tf_op jit(solution)/shard_map/all_gather | solution.py:355
  40.2 72.6 %all-gather.14.cloned.1.call-start = ((), (), s32[]{:S(2)}) async-start(), calls=%async_computation.12 | async-start | bytes 2949120 | tf_op jit(solution)/shard_map/all_gather | solution.py:325
  41.0 90.0 %all-gather.12.cloned.1.call-start = ((), (), s32[]{:S(2)}) async-start(), calls=%async_computation.11 | async-start | bytes 1310720 | tf_op jit(solution)/shard_map/all_gather | solution.py:354
  57.5 124.9 %all-gather.16.cloned.1.call-start = ((), (), s32[]{:S(2)}) async-start(), calls=%async_computation.13 | async-start | bytes 2949120 | tf_op jit(solution)/shard_map/all_gather | solution.py:328
  58.0 268.1 %all-reduce.15.cloned.1.call-start = ((), (), s32[]{:S(2)}) async-start(), calls=%async_computation.14 | async-start | bytes 3145728 | tf_op jit(solution)/shard_map/psum | solution.py:19
  186.6 274.0 %all-gather.18.cloned.1.call-start = ((), (), s32[]{:S(2)}) async-start(), calls=%async_computation.15 | async-start | bytes 15728640 | tf_op jit(solution)/shard_map/all_gather | solution.py:377
  187.3 491.5 %all-gather.20.cloned.1.call-start = ((), (), s32[]{:S(2)}) async-start(), calls=%async_computation.16 | async-start | bytes 15728640 | tf_op jit(solution)/shard_map/all_gather | solution.py:378
  188.0 708.8 %all-gather.22.cloned.1.call-start = ((), (), s32[]{:S(2)}) async-start(), calls=%async_computation.17 | async-start | bytes 15728640 | tf_op jit(solution)/shard_map/all_gather | solution.py:379
  188.8 924.5 %all-reduce.17.cloned.1.call-start = ((), (), s32[]{:S(2)}) async-start(), calls=%async_computation.18 | async-start | bytes 3145728 | tf_op jit(solution)/shard_map/psum | solution.py:417
  374.6 522.2 %copy-start.43 = (f32[16,256]{1,0:T(8,128)}, f32[16,256]{1,0:T(8,128)S(1)}, u32[]{:S(2)}) copy-start(f32[16,256]{1,0:T(8,128)S(1)} %mul.451) | copy-start | bytes 49156
  1063.5 174.7 %reduce-scatter.15.cloned.1.call-start = ((), (), s32[]{:S(2)}) async-start(), calls=%async_computation.19 | async-start | bytes 1310720 | tf_op jit(solution)/shard_map/reduce_scatter | solution.py:443
  1172.0 94.4 %reduce-scatter.17.cloned.1.call-start = ((), (), s32[]{:S(2)}) async-start(), calls=%async_computation.20 | async-start | bytes 1310720 | tf_op jit(solution)/shard_map/reduce_scatter | solution.py:446
  1175.0 144.8 %reduce-scatter.31.cloned.1.call-start = ((), (), s32[]{:S(2)}) async-start(), calls=%async_computation.27 | async-start | bytes 2949120
  1183.3 157.8 %reduce-scatter.21.cloned.1.call-start = ((), (), s32[]{:S(2)}) async-start(), calls=%async_computation.22 | async-start | bytes 983040 | tf_op jit(solution)/shard_map/reduce_scatter | solution.py:477
  1241.1 125.3 %reduce-scatter.23.cloned.1.call-start = ((), (), s32[]{:S(2)}) async-start(), calls=%async_computation.23 | async-start | bytes 983040 | tf_op jit(solution)/shard_map/reduce_scatter | solution.py:480
  1269.1 148.5 %reduce-scatter.19.cloned.1.call-start = ((), (), s32[]{:S(2)}) async-start(), calls=%async_computation.21 | async-start | bytes 2949120 | tf_op jit(solution)/shard_map/reduce_scatter | solution.py:474
  1273.4 358.0 %reduce-scatter.25.cloned.1.call-start = ((), (), s32[]{:S(2)}) async-start(), calls=%async_computation.24 | async-start | bytes 15728640 | tf_op jit(solution)/shard_map/reduce_scatter | solution.py:400
  1283.9 562.6 %reduce-scatter.27.cloned.1.call-start = ((), (), s32[]{:S(2)}) async-start(), calls=%async_computation.25 | async-start | bytes 15728640 | tf_op jit(solution)/shard_map/reduce_scatter | solution.py:403
  1294.1 767.6 %reduce-scatter.29.cloned.1.call-start = ((), (), s32[]{:S(2)}) async-start(), calls=%async_computation.26 | async-start | bytes 15728640 | tf_op jit(solution)/shard_map/reduce_scatter | solution.py:406
  1310.5 774.4 %reduce-scatter.33.cloned.1.call-start = ((), (), s32[]{:S(2)}) async-start(), calls=%async_computation.28 | async-start | bytes 491520
  1313.2 860.7 %all-reduce.21.cloned.1.call-start = ((), (), s32[]{:S(2)}) async-start(), calls=%async_computation.30 | async-start | bytes 6291456 | tf_op jit(solution)/shard_map/psum | solution.py:19
  1319.7 1055.5 %all-reduce.19.cloned.1.call-start = ((), (), s32[]{:S(2)}) async-start(), calls=%async_computation.29 | async-start | bytes 22020096 | tf_op jit(solution)/shard_map/psum | solution.py:495
  2061.7 139.1 %copy-start.12 = (bf16[512,1536]{1,0:T(8,128)(2,1)S(1)}, bf16[512,1536]{1,0:T(8,128)(2,1)}, u32[]{:S(2)}) copy-start(bf16[512,1536]{1,0:T(8,128)(2,1)} %all-reduce.15.cloned.1.call-done) | copy-start | bytes 4718596
  2061.7 139.1 %copy-start.61 = (f32[512]{0:T(512)S(1)}, f32[512]{0:T(512)}, u32[]{:S(2)}) copy-start(f32[512]{0:T(512)} %copy-done.59) | copy-start | bytes 6148
  (70 other events, 1595.8 us)
Sparse Core Ops, SparseCore 0:
  40.3 20.8 all-gather.9
  62.8 50.0 all-gather.13
  115.0 15.9 all-gather.11
  132.5 49.8 all-gather.15
  186.7 53.1 all-reduce.14
  241.4 219.1 all-gather.17
  462.3 216.4 all-gather.19
  680.4 216.3 all-gather.21
  1063.6 49.6 all-reduce.16
  1172.2 65.9 reduce-scatter.14
  1241.5 24.8 reduce-scatter.16
  1269.1 47.8 reduce-scatter.30
  1319.4 21.6 reduce-scatter.20
  1343.8 22.5 reduce-scatter.22
  1369.1 48.4 reduce-scatter.18
  1419.8 211.5 reduce-scatter.24
  1633.6 212.8 reduce-scatter.26
  1848.7 212.8 reduce-scatter.28
  2064.5 20.3 reduce-scatter.32
  2088.4 85.4 all-reduce.20
  2177.7 197.4 all-reduce.18
where the time goes:
time: 2410 us; the launch traced here: 2400 us
  waiting for transfers between devices  1710 us (71%)
  local copies, waits for them, and re-layouts  263 us (11%)
  matrix products  221 us (9%)
  blocking collectives  96.3 us (4%)
  other arithmetic  92.1 us (4%)
    reduce_scatter x1, waiting for transfers between devices, local(): lax.psum_scatter(grad_down_full.astype(jnp.bfloat16), 'fsdp', scatter_dim...  215 us
    reduce_scatter x1, waiting for transfers between devices, local(): lax.psum_scatter(grad_up_full.astype(jnp.bfloat16), 'fsdp', scatter_dimen...  215 us
    reduce_scatter x1, waiting for transfers between devices, local(): lax.psum_scatter(grad_gate_full.astype(jnp.bfloat16), 'fsdp', scatter_dim...  214 us
    all_gather x1, waiting for transfers between devices, local(): lax.all_gather(up_weight, 'fsdp', axis=0, tiled=True)  204 us
    all_gather x1, waiting for transfers between devices, local(): lax.all_gather(down_weight, 'fsdp', axis=0, tiled=True)  204 us
    psum x1, waiting for transfers between devices, local(): lax.psum(shard_query.astype(jnp.bfloat16), 'ctx').astype(jnp.float32)  169 us
    psum x2, waiting for transfers between devices, tensor_total(): lax.psum(partial_value.astype(jnp.bfloat16), 'tp').astype(jnp.float32)  88 us
    all_gather x1, waiting for transfers between devices, local(): lax.all_gather(gate_weight, 'fsdp', axis=0, tiled=True)  86.1 us
  transfers between devices with their start and end apart: 21, of which 19 were waited for; matrix products, arithmetic and copies ran while one was open for 13% of the time, Pallas kernels for 0%

commit v1 on v0

v1 whole, which is shorter than its diff:
```python
import functools
import math

import jax
import jax.numpy as jnp
from jax import lax
from jax.experimental import pallas as pl
from jax.experimental.pallas import tpu as pltpu
from jax.sharding import Mesh
from jax.sharding import PartitionSpec as P

HEAD = 64
TOPK = 8
E = 16
CAP = 256
EPSILON = 1e-06
BF = jnp.bfloat16
F32 = jnp.float32
NEG = -1e30
FAR = 1e6


def dot(a, b, ca, cb):
    return lax.dot_general(a, b, (((ca,), (cb,)), ((), ())), preferred_element_type=F32)


def shift(v, axis, n, by=1):
    return lax.ppermute(v, axis, [(i, (i + by) % n) for i in range(n)])


def swap(v, axis):
    return lax.ppermute(v, axis, [(0, 1), (1, 0)])


def pick(v, index, parts, dim):
    size = v.shape[dim] // parts
    return lax.dynamic_slice_in_dim(v, index * size, size, dim)


def put(buffer, v, start, dim):
    return lax.dynamic_update_slice_in_dim(buffer, v, start, dim)


def ring_reduce(part, axis, n):
    me = lax.axis_index(axis)
    moving = part((me + n - 1) % n).astype(BF)
    for s in range(2, n):
        moving = (shift(moving, axis, n).astype(F32) + part((me + n - s) % n)).astype(BF)
    return shift(moving, axis, n).astype(F32) + part(me)


def core_halves(v, dim):
    core = lax.axis_index("core")
    mine = pick(v, core, 2, dim)
    theirs = pick(v, 1 - core, 2, dim)
    return mine.astype(F32) + swap(theirs.astype(BF), "core").astype(F32)


def core_join(v, dim):
    other = swap(v, "core")
    first = lax.axis_index("core") == 0
    return jnp.concatenate([jnp.where(first, v, other), jnp.where(first, other, v)], axis=dim)


def ring_gather(v, axis, n, dim):
    me = lax.axis_index(axis)
    size = v.shape[dim]
    shape = list(v.shape)
    shape[dim] = size * n
    out = put(jnp.zeros(shape, v.dtype), v, me * size, dim)
    moving = v
    for s in range(1, n):
        moving = shift(moving, axis, n)
        out = put(out, moving, ((me + n - s) % n) * size, dim)
    return out


def ctx_total(v, n_cx):
    half = core_halves(v, 0).astype(BF)
    part = ring_reduce(lambda j: pick(half, j, n_cx, 0).astype(F32), "cx", n_cx).astype(BF)
    return core_join(ring_gather(part, "cx", n_cx, 0), 0)


def normalize(values):
    inverse = lax.rsqrt(jnp.mean(values * values, axis=-1, keepdims=True) + EPSILON)
    return inverse, values * inverse


def norm_backward(grad, gain, inverse, normed):
    scaled = grad * gain
    return inverse * (scaled - normed * jnp.mean(scaled * normed, axis=-1, keepdims=True))


def rotate(v, cos, sin, inverse):
    rows = v.shape[1]
    shaped = v.reshape(-1, 2, HEAD // 2, rows)
    a, b = shaped[:, 0], shaped[:, 1]
    if inverse:
        out = jnp.stack([a * cos + b * sin, b * cos - a * sin], axis=1)
    else:
        out = jnp.stack([a * cos - b * sin, b * cos + a * sin], axis=1)
    return out.reshape(-1, rows)


def keep_plan(routes, order, live):
    rows = routes.shape[0]
    pairs = rows * TOPK
    token, choice = order // TOPK, order % TOPK
    rank = jnp.arange(pairs, dtype=jnp.int32)
    at_token = (jnp.arange(rows, dtype=jnp.int32)[:, None] == token[None, :]).astype(BF)
    at_choice = jnp.arange(TOPK, dtype=jnp.int32)[:, None] == choice[None, :]
    high = jnp.where(at_choice, (rank // 64)[None, :], 0).astype(BF)
    low = jnp.where(at_choice, (rank % 64)[None, :], 0).astype(BF)
    place = dot(jnp.concatenate([high, low], axis=0), at_token, 1, 1)
    place = place[:TOPK] * 64.0 + place[TOPK:]
    routes_t = routes.T
    hits = routes_t[:, None, :] == jnp.arange(E, dtype=jnp.int32)[None, :, None]
    routed = jnp.any(hits, axis=0)
    place_e = jnp.sum(jnp.where(hits, place[:, None, :], 0.0), axis=0)
    place_e = jnp.where(routed & live[None, :], place_e, FAR)
    earlier = jnp.sum(
        (place_e.T[:, :, None] < place_e[None, :, :]).astype(F32), axis=0
    )
    kept = routed & live[None, :] & (earlier < CAP)
    return routed, kept


def softmax_block(q, k, last, base, first_row, length):
    s = lax.dot_general(k, q, (((0,), (0,)), ((), ())), preferred_element_type=F32)
    if last:
        key = base + lax.broadcasted_iota(jnp.int32, s.shape, 0)
        query = first_row + lax.broadcasted_iota(jnp.int32, s.shape, 1)
        s = jnp.where((key <= query) & (key < length), s, NEG)
    return s


def attend_kernel(group, info_ref, q_ref, kv_ref, o_ref, lse_ref):
    count, first_row, length = info_ref[0], info_ref[1], info_ref[2]
    rows = q_ref.shape[1]
    keys = kv_ref.shape[3]
    for h in range(group):
        q = q_ref[h * HEAD : (h + 1) * HEAD, :]

        def step(j, carry, last):
            top, total, acc = carry
            k = kv_ref[j, 0]
            v = kv_ref[j, 1]
            s = softmax_block(q, k, last, j * keys, first_row, length)
            new_top = jnp.maximum(top, jnp.max(s, axis=0, keepdims=True))
            p = jnp.exp(s - new_top)
            fade = jnp.exp(top - new_top)
            total = total * fade + jnp.sum(p, axis=0, keepdims=True)
            acc = acc * fade + jnp.dot(v, p.astype(BF), preferred_element_type=F32)
            return new_top, total, acc

        carry = (
            jnp.full((1, rows), NEG, F32),
            jnp.zeros((1, rows), F32),
            jnp.zeros((HEAD, rows), F32),
        )
        carry = lax.fori_loop(0, count - 1, functools.partial(step, last=False), carry)
        top, total, acc = step(count - 1, carry, True)
        o_ref[h * HEAD : (h + 1) * HEAD, :] = (acc / total).astype(BF)
        lse_ref[0, h : h + 1, :] = top + jnp.log(total)


def attend(q, kv, info, group):
    rows = q.shape[1]
    n_ctx, _, depth, keys = kv.shape
    heads = depth // HEAD
    return pl.pallas_call(
        functools.partial(attend_kernel, group),
        name="attend",
        grid_spec=pltpu.PrefetchScalarGridSpec(
            num_scalar_prefetch=1,
            grid=(heads,),
            in_specs=[
                pl.BlockSpec((group * HEAD, rows), lambda g, i: (g, 0)),
                pl.BlockSpec((n_ctx, 2, HEAD, keys), lambda g, i: (0, 0, g, 0)),
            ],
            out_specs=[
                pl.BlockSpec((group * HEAD, rows), lambda g, i: (g, 0)),
                pl.BlockSpec((1, 8, rows), lambda g, i: (g, 0, 0)),
            ],
        ),
        out_shape=[
            jax.ShapeDtypeStruct(q.shape, BF),
            jax.ShapeDtypeStruct((heads, 8, rows), F32),
        ],
        compiler_params=pltpu.CompilerParams(vmem_limit_bytes=48 << 20),
        cost_estimate=pl.CostEstimate(
            flops=4 * q.shape[0] * rows * n_ctx * keys,
            transcendentals=q.shape[0] // HEAD * rows * n_ctx * keys,
            bytes_accessed=4 * q.size + 2 * kv.size,
        ),
    )(info, q, kv)


def attend_back_kernel(group, info_ref, q_ref, kv_ref, o_ref, do_ref, lse_ref, dq_ref, dkv_ref):
    count, first_row, length = info_ref[0], info_ref[1], info_ref[2]
    n_ctx = kv_ref.shape[0]
    keys = kv_ref.shape[3]
    delta = []
    for h in range(group):
        part = slice(h * HEAD, (h + 1) * HEAD)
        delta.append(
            jnp.sum(do_ref[part, :].astype(F32) * o_ref[part, :].astype(F32), axis=0, keepdims=True)
        )
    dq_ref[...] = jnp.zeros_like(dq_ref)

    def step(j, last):
        k = kv_ref[j, 0]
        v = kv_ref[j, 1]
        dk = jnp.zeros((keys, HEAD), F32)
        dv = jnp.zeros((keys, HEAD), F32)
        for h in range(group):
            part = slice(h * HEAD, (h + 1) * HEAD)
            q = q_ref[part, :]
            do = do_ref[part, :]
            s = softmax_block(q, k, last, j * keys, first_row, length)
            p = jnp.exp(s - lse_ref[0, h : h + 1, :])
            dp = lax.dot_general(v, do, (((0,), (0,)), ((), ())), preferred_element_type=F32)
            ds = (p * (dp - delta[h])).astype(BF)
            pb = p.astype(BF)
            dv += lax.dot_general(pb, do, (((1,), (1,)), ((), ())), preferred_element_type=F32)
            dk += lax.dot_general(ds, q, (((1,), (1,)), ((), ())), preferred_element_type=F32)
            dq_ref[part, :] += jnp.dot(k, ds, preferred_element_type=F32)
        dkv_ref[j, 0] = dk.T.astype(BF)
        dkv_ref[j, 1] = dv.T.astype(BF)

    @pl.loop(0, count - 1)
    def _(j):
        step(j, False)

    step(count - 1, True)

    @pl.loop(count, n_ctx)
    def _(j):
        dkv_ref[j] = jnp.zeros(dkv_ref.shape[1:], BF)


def attend_back(q, kv, o, do, lse, info, group):
    rows = q.shape[1]
    n_ctx, _, depth, keys = kv.shape
    heads = depth // HEAD
    wide = pl.BlockSpec((group * HEAD, rows), lambda g, i: (g, 0))
    blocks = pl.BlockSpec((n_ctx, 2, HEAD, keys), lambda g, i: (0, 0, g, 0))
    return pl.pallas_call(
        functools.partial(attend_back_kernel, group),
        name="attend_back",
        grid_spec=pltpu.PrefetchScalarGridSpec(
            num_scalar_prefetch=1,
            grid=(heads,),
            in_specs=[
                wide,
                blocks,
                wide,
                wide,
                pl.BlockSpec((1, 8, rows), lambda g, i: (g, 0, 0)),
            ],
            out_specs=[wide, blocks],
        ),
        out_shape=[
            jax.ShapeDtypeStruct(q.shape, F32),
            jax.ShapeDtypeStruct(kv.shape, BF),
        ],
        compiler_params=pltpu.CompilerParams(vmem_limit_bytes=48 << 20),
        cost_estimate=pl.CostEstimate(
            flops=10 * q.shape[0] * rows * n_ctx * keys,
            transcendentals=q.shape[0] // HEAD * rows * n_ctx * keys,
            bytes_accessed=10 * q.size + 4 * kv.size,
        ),
    )(info, q, kv, o, do, lse)


def local(
    sizes,
    tokens,
    lengths,
    routes,
    visit_order,
    cotangent,
    first_gain,
    query_weight,
    key_matrix,
    value_matrix,
    output_weight,
    second_gain,
    router_weight,
    gate_weight,
    up_weight,
    down_weight,
):
    n_z, n_cx = sizes
    n_ctx = 2 * n_cx
    z = lax.axis_index("fsdp")
    cx = lax.axis_index("cx")
    core = lax.axis_index("core")
    tp = lax.axis_index("tp")
    ctx = cx * 2 + core
    rows, width = tokens.shape[1:]
    half = rows // 2
    shard = query_weight.shape[0]
    q_width = query_weight.shape[1]
    kv_width = key_matrix.shape[1]
    group = q_width // kv_width
    held = gate_weight.shape[0]
    hidden = gate_weight.shape[2]
    first_row = ctx * rows
    length = lengths[0]
    positions = first_row + jnp.arange(rows, dtype=jnp.int32)
    live = positions < length
    valid = live.astype(F32)[:, None]

    small = jnp.concatenate(
        [first_gain[None], second_gain[None], router_weight.T], axis=0
    )
    small_full = put(jnp.zeros((2 + E, width), BF), small, z * shard, 1)
    for s in range(1, n_z):
        small_full = put(small_full, shift(small, "fsdp", n_z, s), ((z + n_z - s) % n_z) * shard, 1)
    gain_first = small_full[0:1].astype(F32)
    gain_second = small_full[1:2].astype(F32)
    router = small_full[2:]

    w_mine = jnp.concatenate([query_weight, key_matrix, value_matrix], axis=1)
    w_full = put(jnp.zeros((width, w_mine.shape[1]), BF), w_mine, z * shard, 0)
    moving = pick(w_mine, core, 2, 0)
    piece = shard // 2
    for s in range(1, n_z):
        moving = shift(moving, "fsdp", n_z)
        start = ((z + n_z - s) % n_z) * shard
        w_full = put(w_full, moving, start + core * piece, 0)
        w_full = put(w_full, swap(moving, "core"), start + (1 - core) * piece, 0)

    grad_out = (cotangent[0].astype(F32) * valid).astype(BF)
    grad_half = pick(grad_out, tp, 2, 0)
    grad_chunks = []
    moving = grad_half
    for s in range(n_z):
        if s:
            moving = shift(moving, "fsdp", n_z)
        grad_chunks.append(jnp.concatenate([moving, swap(moving, "tp")], axis=0))

    o_full = put(jnp.zeros((q_width, width), BF), output_weight, z * shard, 1)
    moving = pick(output_weight, core, 2, 0)
    o_piece = q_width // 2
    for s in range(1, n_z):
        moving = shift(moving, "fsdp", n_z)
        start = ((z + n_z - s) % n_z) * shard
        both = lax.dynamic_update_slice(o_full, moving, (core * o_piece, start))
        o_full = lax.dynamic_update_slice(both, swap(moving, "core"), ((1 - core) * o_piece, start))

    routed, kept = keep_plan(routes[0], visit_order[0, 0], live)

    inputs = tokens[0].astype(F32)
    inverse_one, normed_one = normalize(inputs)
    hidden_one = (normed_one * gain_first).astype(BF)
    frequency = jnp.exp(
        jnp.arange(HEAD // 2, dtype=F32) * (-2.0 * math.log(10000.0) / HEAD)
    )
    angles = frequency[:, None] * positions.astype(F32)[None, :]
    cos, sin = jnp.cos(angles), jnp.sin(angles)
    projected = dot(w_full, hidden_one, 0, 1)
    scale = HEAD**-0.5
    query = (rotate(projected[:q_width], cos, sin, False).astype(BF) * scale).astype(BF)
    key = rotate(projected[q_width : q_width + kv_width], cos, sin, False).astype(BF)
    value = projected[q_width + kv_width :].astype(BF)
    kv_mine = jnp.stack([key, value])[None]
    kv = jnp.zeros((n_ctx,) + kv_mine.shape[1:], BF)
    moving = kv_mine
    for s in range(n_cx):
        if s:
            moving = shift(moving, "cx", n_cx)
        source = ((cx + n_cx - s) % n_cx) * 2
        kv = put(kv, moving, source + core, 0)
        kv = put(kv, swap(moving, "core"), source + 1 - core, 0)
    count = jnp.minimum(ctx + 1, (length + rows - 1) // rows)
    info = jnp.stack([count, first_row, length])
    attended, lse = attend(query, kv, info, group)

    far = dot(pick(attended, 1 - tp, 2, 1), o_full, 0, 0).astype(BF)
    near = dot(pick(attended, tp, 2, 1), o_full, 0, 0)
    residual = pick(tokens[0], tp, 2, 0).astype(F32) + near + swap(far, "tp").astype(F32)
    inverse_two, normed_two = normalize(residual)
    hidden_two = (normed_two * gain_second).astype(BF)
    logits = dot(router, hidden_two, 1, 1)
    routed_half = pick(routed, tp, 2, 1)
    kept_half = pick(kept, tp, 2, 1).astype(F32)
    masked = jnp.where(routed_half, logits, NEG)
    raised = jnp.where(
        routed_half, jnp.exp(masked - jnp.max(masked, axis=0, keepdims=True)), 0.0
    )
    gates = raised / jnp.sum(raised, axis=0, keepdims=True)
    weights = gates * kept_half

    gate_up = jnp.concatenate(
        [gate_weight[e] for e in range(held)] + [up_weight[e] for e in range(held)], axis=1
    )
    down = down_weight.reshape(held * hidden, width)
    mid = held * hidden
    h2_chunks, acts, grads, mix_parts, back_parts, gate_parts = [], [], [], [], [], []
    moving, moving_w = hidden_two, weights
    for s in range(n_z):
        if s:
            moving = shift(moving, "fsdp", n_z)
            moving_w = shift(moving_w, "fsdp", n_z)
        block = jnp.concatenate([moving, swap(moving, "tp")], axis=0)
        block_w = jnp.concatenate([moving_w, swap(moving_w, "tp")], axis=1)
        mine_w = lax.dynamic_slice_in_dim(block_w, z * held, held, 0).T
        spread = jnp.broadcast_to(mine_w[:, :, None], (rows, held, hidden)).reshape(rows, mid)
        both = dot(block, gate_up, 1, 0)
        g, u = both[:, :mid], both[:, mid:]
        sig = jax.nn.sigmoid(g)
        silu = g * sig
        act = silu * u
        weighted = (act * spread).astype(BF)
        mix_parts.append(dot(weighted, down, 1, 0).astype(BF))
        dact = dot(grad_chunks[s], down, 1, 1)
        gate_grad = jnp.sum((act * dact).reshape(rows, held, hidden), axis=-1).T
        gate_parts.append(put(jnp.zeros((E, rows), F32), gate_grad, z * held, 0))
        dhid = dact * spread
        dg = (dhid * u * sig * (1.0 + g * (1.0 - sig))).astype(BF)
        du = (dhid * silu).astype(BF)
        dgu = jnp.concatenate([dg, du], axis=1)
        back_parts.append(dot(dgu, gate_up, 1, 1).astype(BF))
        h2_chunks.append(block)
        acts.append(weighted)
        grads.append(dgu)

    def home(parts, dim):
        halves = []
        for part in parts:
            size = part.shape[dim] // 2
            mine = lax.slice_in_dim(part, 0, size, axis=dim).astype(F32)
            theirs = lax.slice_in_dim(part, size, 2 * size, axis=dim)
            halves.append(mine + swap(theirs, "tp").astype(F32))
        moving = halves[1].astype(part.dtype)
        for s in range(2, n_z):
            moving = (shift(moving, "fsdp", n_z).astype(F32) + halves[s]).astype(part.dtype)
        return shift(moving, "fsdp", n_z).astype(F32) + halves[0]

    hidden_grad = home(back_parts, 0)
    gate_grad = home(gate_parts, 1) * kept_half
    mixture = home(mix_parts, 0)

    h2_all = jnp.concatenate(h2_chunks, axis=0)
    grad_gate_up = dot(h2_all, jnp.concatenate(grads, axis=0), 0, 0).astype(BF)
    grad_down = dot(
        jnp.concatenate(acts, axis=0), jnp.concatenate(grad_chunks, axis=0), 0, 0
    ).astype(BF)
    grad_gate_up = ctx_total(grad_gate_up, n_cx)
    grad_down = ctx_total(grad_down, n_cx)

    valid_half = pick(valid, tp, 2, 0)
    out_half = (valid_half * (residual + mixture)).astype(BF)
    out_other = swap(out_half, "tp")
    lead = tp == 0
    layer_out = jnp.concatenate(
        [jnp.where(lead, out_half, out_other), jnp.where(lead, out_other, out_half)], axis=0
    )

    logit_grad = (
        gates * (gate_grad - jnp.sum(gates * gate_grad, axis=0, keepdims=True))
    ).astype(BF)
    hidden_grad = hidden_grad + dot(logit_grad, router, 0, 0)
    grad_router = dot(logit_grad, hidden_two, 1, 0)
    grad_second = jnp.sum(hidden_grad * normed_two, axis=0, keepdims=True)
    branch_half = (
        grad_half.astype(F32) + norm_backward(hidden_grad, gain_second, inverse_two, normed_two)
    ).astype(BF)
    branch_other = swap(branch_half, "tp")
    branch = jnp.concatenate(
        [jnp.where(lead, branch_half, branch_other), jnp.where(lead, branch_other, branch_half)],
        axis=0,
    )

    attended_grad = dot(o_full, branch, 1, 1).astype(BF)
    grad_query_rot, grad_kv = attend_back(
        query, kv, attended, attended_grad, lse, info, group
    )
    grad_output = dot(attended, branch, 1, 0).astype(BF)
    by_core = grad_kv.reshape((n_cx, 2) + grad_kv.shape[1:])
    kv_sum = (
        lax.dynamic_index_in_dim(by_core, core, 1, False).astype(F32)
        + swap(lax.dynamic_index_in_dim(by_core, 1 - core, 1, False), "core").astype(F32)
    ).astype(BF)
    kv_grad = ring_reduce(
        lambda j: lax.dynamic_index_in_dim(kv_sum, j, 0, False).astype(F32), "cx", n_cx
    )
    query_grad = (rotate(grad_query_rot, cos, sin, True) * scale).astype(BF)
    key_grad = rotate(kv_grad[0], cos, sin, True).astype(BF)
    value_grad = kv_grad[1].astype(BF)
    grad_all = jnp.concatenate([query_grad, key_grad, value_grad], axis=0)
    first_part = dot(grad_all, w_full, 0, 1)
    grad_first = jnp.sum(first_part * normed_one, axis=0, keepdims=True)
    first_low = first_part.astype(BF)
    first_grad = first_low.astype(F32) + swap(first_low, "tp").astype(F32)
    grad_inputs = branch.astype(F32) + norm_backward(
        first_grad, gain_first, inverse_one, normed_one
    )
    grad_w = dot(hidden_one, grad_all, 0, 1).astype(BF)

    def owner_rows(v):
        blocks = v.reshape(n_z, v.shape[0] // n_z, v.shape[1])
        mine = core_halves(blocks, 1).astype(BF)
        mine = ring_reduce(lambda j: pick(mine, j, n_cx, 1).astype(F32), "cx", n_cx).astype(BF)
        mine = ring_reduce(
            lambda j: lax.dynamic_index_in_dim(mine, j, 0, False).astype(F32), "fsdp", n_z
        ).astype(BF)
        return core_join(ring_gather(mine, "cx", n_cx, 0), 0)

    def owner_columns(v):
        mine = core_halves(v, 0).astype(BF)
        mine = ring_reduce(lambda j: pick(mine, j, n_cx, 0).astype(F32), "cx", n_cx).astype(BF)
        mine = ring_reduce(lambda j: pick(mine, j, n_z, 1).astype(F32), "fsdp", n_z).astype(BF)
        return core_join(ring_gather(mine, "cx", n_cx, 0), 0)

    grad_w = owner_rows(grad_w).astype(F32)
    grad_output = owner_columns(grad_output).astype(F32)

    small_grad = jnp.concatenate([grad_first, grad_second, grad_router], axis=0)
    small_grad = small_grad + swap(small_grad, "tp")
    small_grad = small_grad + swap(small_grad, "core")
    total = small_grad
    moving = small_grad
    for s in range(1, n_cx):
        moving = shift(moving, "cx", n_cx)
        total = total + moving
    me = z
    moving = pick(total, (me + n_z - 1) % n_z, n_z, 1)
    for s in range(2, n_z):
        moving = shift(moving, "fsdp", n_z) + pick(total, (me + n_z - s) % n_z, n_z, 1)
    small_mine = shift(moving, "fsdp", n_z) + pick(total, me, n_z, 1)

    def experts_of(v):
        return jnp.stack(
            [v[:, e * hidden : (e + 1) * hidden] for e in range(held)]
        ).astype(F32)

    return (
        layer_out[None],
        grad_inputs[None],
        small_mine[0],
        grad_w[:, :q_width],
        grad_w[:, q_width : q_width + kv_width],
        grad_w[:, q_width + kv_width :],
        grad_output,
        small_mine[1],
        small_mine[2:].T,
        experts_of(grad_gate_up[:, :mid]),
        experts_of(grad_gate_up[:, mid:]),
        grad_down.reshape(held, hidden, width).astype(F32),
    )


def solution(mesh):
    n_z, n_ctx, n_tp = mesh.shape["fsdp"], mesh.shape["ctx"], mesh.shape["tp"]
    named = Mesh(
        mesh.devices.reshape(n_z, n_ctx // 2, 2, n_tp), ("fsdp", "cx", "core", "tp")
    )
    ctx = ("cx", "core")
    placed = (
        P("fsdp", ctx, None),
        P("fsdp"),
        P("fsdp", ctx, None),
        P("fsdp", ctx, None),
        P("fsdp", ctx, None),
        P("fsdp"),
        P("fsdp", "tp"),
        P("fsdp", "tp"),
        P("fsdp", "tp"),
        P("tp", "fsdp"),
        P("fsdp"),
        P("fsdp", None),
        P("fsdp", None, "tp"),
        P("fsdp", None, "tp"),
        P("fsdp", "tp", None),
    )
    return jax.shard_map(
        functools.partial(local, (n_z, n_ctx // 2)),
        mesh=named,
        in_specs=placed,
        out_specs=(
            P("fsdp", ctx, None),
            P("fsdp", ctx, None),
            P("fsdp"),
            P("fsdp", "tp"),
            P("fsdp", "tp"),
            P("fsdp", "tp"),
            P("tp", "fsdp"),
            P("fsdp"),
            P("fsdp", None),
            P("fsdp", None, "tp"),
            P("fsdp", None, "tp"),
            P("fsdp", "tp", None),
        ),
        check_vma=False,
    )
```

time: 2410 us -> 835 us (0.35)
  waiting for transfers between devices: 1710 us -> 284 us
  starting transfers between devices: 1.03 us -> 162 us
  local copies, waits for them, and re-layouts: 263 us -> 132 us
  blocking collectives: 96.3 us -> 0 us
  matrix products: 221 us -> 132 us
  Pallas kernels: 0 us -> 37.6 us
    reduce_scatter x8 -> x0, waiting for transfers between devices: 820 us -> none  [the longest x1 215 us: local(): lax.psum_scatter(grad_down_full.astype(jnp.bfloat16), 'fsdp', scatter_dim...]
    all_gather x7 -> x0, waiting for transfers between devices: 580 us -> none  [the longest x1 204 us: local(): lax.all_gather(up_weight, 'fsdp', axis=0, tiled=True)]
    ppermute x0 -> x94, waiting for transfers between devices: none -> 284 us  [the longest x47 198 us: shift(): return lax.ppermute(v, axis, [(i, (i + by) % n) for i in range(n)])]
    psum x4 -> x0, waiting for transfers between devices: 284 us -> none  [the longest x1 169 us: local(): lax.psum(shard_query.astype(jnp.bfloat16), 'ctx').astype(jnp.float32)]
    gather x7 -> x0, local copies, waits for them, and re-layouts: 175 us -> none  [the longest x1 31.5 us: local(): out_pad[pair_slot].reshape(row_count, TOPK, width).astype(jnp.float32)]
    ppermute x0 -> x94, starting transfers between devices: none -> 162 us  [the longest x47 98 us: shift(): return lax.ppermute(v, axis, [(i, (i + by) % n) for i in range(n)])]
    dot_general x38 -> x29, matrix products: 221 us -> 132 us  [dot(): lax.dot_general(a, b, (((ca,), (cb,)), ((), ())), preferred_element_type=...]
    all_gather x5 -> x0, blocking collectives: 69.4 us -> none  [the longest x1 18.4 us: local(): lax.all_gather(router_weight, 'fsdp', axis=0, tiled=True)]
  transfers between devices with their start and end apart: 21 -> 94, of which waited for: 19 -> 33; matrix products, arithmetic and copies ran while one was open for 13% -> 38% of each run, Pallas kernels for 0% -> 5%
where the time goes in v1:
time: 835 us; the launch traced here: 825 us
  waiting for transfers between devices  284 us (34%)
  starting transfers between devices  162 us (19%)
  local copies, waits for them, and re-layouts  132 us (16%)
  matrix products  132 us (16%)
  other arithmetic  73 us (9%)
  Pallas kernels  37.6 us (5%)
    ppermute x47, waiting for transfers between devices, shift(): return lax.ppermute(v, axis, [(i, (i + by) % n) for i in range(n)])  198 us
    dot_general x29, matrix products, dot(): lax.dot_general(a, b, (((ca,), (cb,)), ((), ())), preferred_element_type=...  132 us
    ppermute x47, starting transfers between devices, shift(): return lax.ppermute(v, axis, [(i, (i + by) % n) for i in range(n)])  98 us
    ppermute x47, waiting for transfers between devices, swap(): return lax.ppermute(v, axis, [(0, 1), (1, 0)])  86.8 us
    ppermute x47, starting transfers between devices, swap(): return lax.ppermute(v, axis, [(0, 1), (1, 0)])  63.7 us
    unnamed x243, local copies, waits for them, and re-layouts  51.9 us
    pallas_call x1, Pallas kernels, attend_back(): pl.pallas_call(functools.partial(attend_back_kernel, group), name='attend...  20 us
    pallas_call x1, Pallas kernels, attend(): pl.pallas_call(functools.partial(attend_kernel, group), name='attend', gr...  17.6 us
  transfers between devices with their start and end apart: 94, of which 33 were waited for; matrix products, arithmetic and copies ran while one was open for 38% of the time, Pallas kernels for 5%

profile of v1, /device:TPU:1, one launch (start us, length us, event | category | flops | bytes accessed | tf_op | source)
XLA Modules:
  0.0 824.6 jit_solution(8514705200541449180)
XLA Ops:
  62.2 15.4 %collective-permute-done.4 = bf16[192,1280]{1,0:T(8,128)(2,1)S(1)} collective-permute-done((bf16[192,1280]{1,0:T(8,128)(2,1)}, bf16[192,1280]{1,0:T(8,128)(2,1)S(1)}, u32[]{:S(2)}, u32[]{:S(2)}) %collective-permute-start.4) | collective-permute-done | bytes 491552 | tf_op jit(solution)/shard_map/ppermute | solution.py:28
  140.1 17.6 %attend.1 = (bf16[768,512]{1,0:T(8,128)(2,1)S(1)}, f32[4,8,512]{2,1,0:T(8,128)S(1)}) custom-call(s32[3]{0:T(128)S(1)} %pad_add_fusion.info_ref, bf16[768,512]{1,0:T(8,128)(2,1)S(1)} %bitcast.173, bf16[4,2,256,512]{3,2,1,0:T(8,128)(2,1)S(1)} %constant_dynamic-update-slice_fusion.32.kv_ref), custom_call_target="tpu_custom_call" | custom-call | flops 3221225472 | bytes 3670016 | tf_op jit(solution)/shard_map/attend/pallas_call | solution.py:171
  166.4 12.0 %collective-permute-done.18 = bf16[256,1536]{1,0:T(8,128)(2,1)S(1)} collective-permute-done((bf16[256,1536]{1,0:T(8,128)(2,1)S(1)}, bf16[256,1536]{1,0:T(8,128)(2,1)S(1)}, u32[]{:S(2)}, u32[]{:S(2)}) %collective-permute-start.18) | collective-permute-done | bytes 786464 | tf_op jit(solution)/shard_map/ppermute | solution.py:32
  184.9 10.2 %collective-permute-done.50 = bf16[256,1536]{1,0:T(8,128)(2,1)S(1)} collective-permute-done((bf16[256,1536]{1,0:T(8,128)(2,1)S(1)}, bf16[256,1536]{1,0:T(8,128)(2,1)S(1)}, u32[]{:S(2)}, u32[]{:S(2)}) %collective-permute-start.50) | collective-permute-done | bytes 786464 | tf_op jit(solution)/shard_map/ppermute | solution.py:32
  198.3 13.8 %collective-permute-done.37 = bf16[256,1536]{1,0:T(8,128)(2,1)S(1)} collective-permute-done((bf16[256,1536]{1,0:T(8,128)(2,1)S(1)}, bf16[256,1536]{1,0:T(8,128)(2,1)S(1)}, u32[]{:S(2)}, u32[]{:S(2)}) %collective-permute-start.37) | collective-permute-done | bytes 786464 | tf_op jit(solution)/shard_map/ppermute | solution.py:32
  261.1 13.0 %collective-permute-done.55 = f32[16,256]{1,0:T(8,128)S(1)} collective-permute-done((f32[16,256]{1,0:T(8,128)S(1)}, f32[16,256]{1,0:T(8,128)S(1)}, u32[]{:S(2)}, u32[]{:S(2)}) %collective-permute-start.55) | collective-permute-done | bytes 16416 | tf_op jit(solution)/shard_map/ppermute | solution.py:32
  364.9 8.3 %collective-permute-done.28 = f32[16,256]{1,0:T(8,128)S(1)} collective-permute-done((f32[16,256]{1,0:T(8,128)S(1)}, f32[16,256]{1,0:T(8,128)S(1)}, u32[]{:S(2)}, u32[]{:S(2)}) %collective-permute-start.28) | collective-permute-done | bytes 16416 | tf_op jit(solution)/shard_map/ppermute | solution.py:32
  378.4 7.4 convolution_convert_fusion.4
  393.2 14.1 %collective-permute-done.34 = f32[16,256]{1,0:T(8,128)S(1)} collective-permute-done((f32[16,256]{1,0:T(8,128)S(1)}, f32[16,256]{1,0:T(8,128)S(1)}, u32[]{:S(2)}, u32[]{:S(2)}) %collective-permute-start.34) | collective-permute-done | bytes 16416 | tf_op jit(solution)/shard_map/ppermute | solution.py:32
  413.6 10.2 %fusion.33 = bf16[1024,1536]{1,0:T(8,128)(2,1)S(1)} fusion(bf16[2048,1536]{1,0:T(8,128)(2,1)} %constant_dynamic-update-slice_fusion.11, bf16[512,1024]{1,0:T(8,128)(2,1)S(1)} %get-tuple-element.67, bf16[512,1024]{1,0:T(8,128)(2,1)S(1)} %copy-done.72, bf16[512,1024]{1,0:T(8,128)(2,1)S(1)} %copy-done.67, bf16[512,1024]{1,0:T(8,128)(2,1)S(1)} %copy-done.61), kind=kOutput, calls=%fused_computation.52 | convolution fusion | flops 6460801024 | bytes 13631488 | tf_op jit(solution)/shard_map/dot_general | solution.py:24
  423.9 24.3 %fusion.17 = bf16[1536,2048]{1,0:T(8,128)(2,1)S(1)} fusion(bf16[2048,1536]{1,0:T(8,128)(2,1)} %constant_dynamic-update-slice_fusion.3, bf16[512,1024]{1,0:T(8,128)(2,1)} %get-tuple-element.52, bf16[512,1024]{1,0:T(8,128)(2,1)} %get-tuple-element.51, bf16[512,1024]{1,0:T(8,128)(2,1)} %copy-done.70, bf16[512,1024]{1,0:T(8,128)(2,1)S(1)} %copy-done.69, ...), kind=kOutput, calls=%fused_computation.33 | convolution fusion | flops 12955156480 | bytes 20971520 | tf_op jit(solution)/shard_map/dot_general | solution.py:24
  464.4 16.8 %collective-permute-done.44 = bf16[256,1536]{1,0:T(8,128)(2,1)S(1)} collective-permute-done((bf16[256,1536]{1,0:T(8,128)(2,1)S(1)}, bf16[256,1536]{1,0:T(8,128)(2,1)S(1)}, u32[]{:S(2)}, u32[]{:S(2)}) %collective-permute-start.44) | collective-permute-done | bytes 786464 | tf_op jit(solution)/shard_map/ppermute | solution.py:28
  483.9 13.7 %collective-permute-done.24 = bf16[256,1536]{1,0:T(8,128)(2,1)S(1)} collective-permute-done((bf16[256,1536]{1,0:T(8,128)(2,1)S(1)}, bf16[256,1536]{1,0:T(8,128)(2,1)S(1)}, u32[]{:S(2)}, u32[]{:S(2)}) %collective-permute-start.24) | collective-permute-done | bytes 786464 | tf_op jit(solution)/shard_map/ppermute | solution.py:28
  501.2 17.0 %collective-permute-done.48 = bf16[256,1536]{1,0:T(8,128)(2,1)S(1)} collective-permute-done((bf16[256,1536]{1,0:T(8,128)(2,1)S(1)}, bf16[256,1536]{1,0:T(8,128)(2,1)S(1)}, u32[]{:S(2)}, u32[]{:S(2)}) %collective-permute-start.48) | collective-permute-done | bytes 786464 | tf_op jit(solution)/shard_map/ppermute | solution.py:28
  518.2 16.6 %collective-permute-start.91 = (bf16[256,1536]{1,0:T(8,128)(2,1)S(1)}, bf16[256,1536]{1,0:T(8,128)(2,1)S(1)}, u32[]{:S(2)}, u32[]{:S(2)}) collective-permute-start(bf16[256,1536]{1,0:T(8,128)(2,1)S(1)} %constant_dynamic-slice_fusion.1), channel_id=1, source_target_pairs={{0,4},{4,0},{1,5},{5,1},{2,6},{6,2},{3,7},{7,3},{8,12},{12,8},{9,1... | collective-permute-start | bytes 2359304 | tf_op jit(solution)/shard_map/ppermute | solution.py:28
  537.5 11.4 %collective-permute-done.91 = bf16[256,1536]{1,0:T(8,128)(2,1)S(1)} collective-permute-done((bf16[256,1536]{1,0:T(8,128)(2,1)S(1)}, bf16[256,1536]{1,0:T(8,128)(2,1)S(1)}, u32[]{:S(2)}, u32[]{:S(2)}) %collective-permute-start.91) | collective-permute-done | bytes 786464 | tf_op jit(solution)/shard_map/ppermute | solution.py:28
  556.4 15.9 %collective-permute-done.36 = bf16[256,1536]{1,0:T(8,128)(2,1)S(1)} collective-permute-done((bf16[256,1536]{1,0:T(8,128)(2,1)S(1)}, bf16[256,1536]{1,0:T(8,128)(2,1)S(1)}, u32[]{:S(2)}, u32[]{:S(2)}) %collective-permute-start.36) | collective-permute-done | bytes 786464 | tf_op jit(solution)/shard_map/ppermute | solution.py:28
  578.2 16.4 %collective-permute-start.87 = (bf16[384,2048]{1,0:T(8,128)(2,1)}, bf16[384,2048]{1,0:T(8,128)(2,1)}, u32[]{:S(2)}, u32[]{:S(2)}) collective-permute-start(bf16[384,2048]{1,0:T(8,128)(2,1)} %constant_dynamic-slice_fusion.3), channel_id=1, source_target_pairs={{0,4},{4,0},{1,5},{5,1},{2,6},{6,2},{3,7},{7,3},{8,12},{12,8},{9,1... | collective-permute-start | bytes 4718600 | tf_op jit(solution)/shard_map/ppermute | solution.py:28
  599.0 20.0 %attend_back.1 = (f32[768,512]{1,0:T(8,128)S(1)}, bf16[4,2,256,512]{3,2,1,0:T(8,128)(2,1)S(1)}) custom-call(s32[3]{0:T(128)S(1)} %pad_add_fusion.info_ref, bf16[768,512]{1,0:T(8,128)(2,1)S(1)} %bitcast.174, bf16[4,2,256,512]{3,2,1,0:T(8,128)(2,1)} %copy-done.1, bf16[768,512]{1,0:T(8,128)(2,1)S(1)} %copy-done.5, ...), custom_call_target="tpu_custom_call" | custom-call | flops 8053063680 | bytes 8126464 | tf_op jit(solution)/shard_map/attend_back/pallas_call | solution.py:248
  630.9 20.7 %collective-permute-start.88 = (bf16[384,2048]{1,0:T(8,128)(2,1)}, bf16[384,2048]{1,0:T(8,128)(2,1)}, u32[]{:S(2)}, u32[]{:S(2)}) collective-permute-start(bf16[384,2048]{1,0:T(8,128)(2,1)} %get-tuple-element.33), channel_id=1, source_target_pairs={{0,4},{4,0},{1,5},{5,1},{2,6},{6,2},{3,7},{7,3},{8,12},{12,8},{9,1... | collective-permute-start | bytes 4718600 | tf_op jit(solution)/shard_map/ppermute | solution.py:28
  653.9 43.5 %collective-permute-done.64 = bf16[2,256,512]{2,1,0:T(8,128)(2,1)S(1)} collective-permute-done((bf16[2,256,512]{2,1,0:T(8,128)(2,1)S(1)}, bf16[2,256,512]{2,1,0:T(8,128)(2,1)S(1)}, u32[]{:S(2)}, u32[]{:S(2)}) %collective-permute-start.64) | collective-permute-done | bytes 524320 | tf_op jit(solution)/shard_map/ppermute | solution.py:28
  700.0 10.0 %collective-permute-done.80 = bf16[192,1536]{1,0:T(8,128)(2,1)S(1)} collective-permute-done((bf16[192,1536]{1,0:T(8,128)(2,1)S(1)}, bf16[192,1536]{1,0:T(8,128)(2,1)S(1)}, u32[]{:S(2)}, u32[]{:S(2)}) %collective-permute-start.80) | collective-permute-done | bytes 589856 | tf_op jit(solution)/shard_map/ppermute | solution.py:28
  738.7 12.6 %collective-permute-done.65 = bf16[512,1536]{1,0:T(8,128)(2,1)S(1)} collective-permute-done((bf16[512,1536]{1,0:T(8,128)(2,1)S(1)}, bf16[512,1536]{1,0:T(8,128)(2,1)S(1)}, u32[]{:S(2)}, u32[]{:S(2)}) %collective-permute-start.65) | collective-permute-done | bytes 1572896 | tf_op jit(solution)/shard_map/ppermute | solution.py:32
  762.7 16.0 %collective-permute-done.68 = f32[18,1536]{1,0:T(8,128)S(1)} collective-permute-done((f32[18,1536]{1,0:T(8,128)S(1)}, f32[18,1536]{1,0:T(8,128)S(1)}, u32[]{:S(2)}, u32[]{:S(2)}) %collective-permute-start.68) | collective-permute-done | bytes 110624 | tf_op jit(solution)/shard_map/ppermute | solution.py:28
  (637 shorter events, 443.7 us)
Async XLA Ops:
  3.7 38.6 %collective-permute-start.7 = (bf16[18,384]{1,0:T(8,128)(2,1)}, bf16[18,384]{1,0:T(8,128)(2,1)}, u32[]{:S(2)}, u32[]{:S(2)}) collective-permute-start(bf16[18,384]{1,0:T(8,128)(2,1)} %get-tuple-element.97), channel_id=1, source_target_pairs={{0,16},{8,24},{16,0},{24,8},{1,17},{9,25},{17,1},{25,9},{2,18},{10... | collective-permute-start | bytes 41480 | tf_op jit(solution)/shard_map/ppermute | solution.py:28
  11.8 46.0 %collective-permute-start.12 = (bf16[384,384]{1,0:T(8,128)(2,1)}, bf16[384,384]{1,0:T(8,128)(2,1)}, u32[]{:S(2)}, u32[]{:S(2)}) collective-permute-start(bf16[384,384]{1,0:T(8,128)(2,1)} %constant_dynamic-slice_fusion.13), channel_id=1, source_target_pairs={{0,8},{8,16},{16,24},{24,0},{1,9},{9,17},{17,25},{25,1},{2,10},{10... | collective-permute-start | bytes 884744 | tf_op jit(solution)/shard_map/ppermute | solution.py:28
  38.4 48.1 %collective-permute-start.41 = (bf16[256,1536]{1,0:T(8,128)(2,1)}, bf16[256,1536]{1,0:T(8,128)(2,1)}, u32[]{:S(2)}, u32[]{:S(2)}) collective-permute-start(bf16[256,1536]{1,0:T(8,128)(2,1)} %get-tuple-element.31), channel_id=1, source_target_pairs={{0,8},{8,16},{16,24},{24,0},{1,9},{9,17},{17,25},{25,1},{2,10},{10... | collective-permute-start | bytes 2359304 | tf_op jit(solution)/shard_map/ppermute | solution.py:28
  57.9 59.8 %collective-permute-start.53 = (bf16[256,1536]{1,0:T(8,128)(2,1)}, bf16[256,1536]{1,0:T(8,128)(2,1)}, u32[]{:S(2)}, u32[]{:S(2)}) collective-permute-start(bf16[256,1536]{1,0:T(8,128)(2,1)} %get-tuple-element.31), channel_id=1, source_target_pairs={{0,1},{1,0},{2,3},{3,2},{4,5},{5,4},{6,7},{7,6},{8,9},{9,8},{10,11... | collective-permute-start | bytes 2359304 | tf_op jit(solution)/shard_map/ppermute | solution.py:32
  86.4 48.6 %collective-permute-start.45 = (bf16[256,1536]{1,0:T(8,128)(2,1)}, bf16[256,1536]{1,0:T(8,128)(2,1)}, u32[]{:S(2)}, u32[]{:S(2)}) collective-permute-start(bf16[256,1536]{1,0:T(8,128)(2,1)} %collective-permute-done.41), channel_id=1, source_target_pairs={{0,8},{8,16},{16,24},{24,0},{1,9},{9,17},{17,25},{25,1},{2,10},{10... | collective-permute-start | bytes 2359304 | tf_op jit(solution)/shard_map/ppermute | solution.py:28
  117.6 44.3 %collective-permute-start.42 = (bf16[256,1536]{1,0:T(8,128)(2,1)}, bf16[256,1536]{1,0:T(8,128)(2,1)S(1)}, u32[]{:S(2)}, u32[]{:S(2)}) collective-permute-start(bf16[256,1536]{1,0:T(8,128)(2,1)} %collective-permute-done.41), channel_id=1, source_target_pairs={{0,1},{1,0},{2,3},{3,2},{4,5},{5,4},{6,7},{7,6},{8,9},{9,8},{10,11... | collective-permute-start | bytes 2359304 | tf_op jit(solution)/shard_map/ppermute | solution.py:32
  197.1 40.0 %collective-permute-start.20 = (bf16[256,1536]{1,0:T(8,128)(2,1)}, bf16[256,1536]{1,0:T(8,128)(2,1)}, u32[]{:S(2)}, u32[]{:S(2)}) collective-permute-start(bf16[256,1536]{1,0:T(8,128)(2,1)} %collective-permute-done.19), channel_id=1, source_target_pairs={{0,1},{1,0},{2,3},{3,2},{4,5},{5,4},{6,7},{7,6},{8,9},{9,8},{10,11... | collective-permute-start | bytes 2359304 | tf_op jit(solution)/shard_map/ppermute | solution.py:32
  229.7 91.4 %collective-permute-start.61 = (f32[16,256]{1,0:T(8,128)}, f32[16,256]{1,0:T(8,128)}, u32[]{:S(2)}, u32[]{:S(2)}) collective-permute-start(f32[16,256]{1,0:T(8,128)} %slice.343), channel_id=1, source_target_pairs={{0,1},{1,0},{2,3},{3,2},{4,5},{5,4},{6,7},{7,6},{8,9},{9,8},{10,11... | collective-permute-start | bytes 49160 | tf_op jit(solution)/shard_map/ppermute | solution.py:32
  358.3 99.0 %collective-permute-start.43 = (bf16[256,1536]{1,0:T(8,128)(2,1)}, bf16[256,1536]{1,0:T(8,128)(2,1)}, u32[]{:S(2)}, u32[]{:S(2)}) collective-permute-start(bf16[256,1536]{1,0:T(8,128)(2,1)} %slice.329), channel_id=1, source_target_pairs={{0,1},{1,0},{2,3},{3,2},{4,5},{5,4},{6,7},{7,6},{8,9},{9,8},{10,11... | collective-permute-start | bytes 2359304 | tf_op jit(solution)/shard_map/ppermute | solution.py:32
  363.0 97.7 %collective-permute-start.23 = (bf16[256,1536]{1,0:T(8,128)(2,1)}, bf16[256,1536]{1,0:T(8,128)(2,1)}, u32[]{:S(2)}, u32[]{:S(2)}) collective-permute-start(bf16[256,1536]{1,0:T(8,128)(2,1)} %slice.315), channel_id=1, source_target_pairs={{0,1},{1,0},{2,3},{3,2},{4,5},{5,4},{6,7},{7,6},{8,9},{9,8},{10,11... | collective-permute-start | bytes 2359304 | tf_op jit(solution)/shard_map/ppermute | solution.py:32
  386.8 77.2 %collective-permute-start.47 = (bf16[256,1536]{1,0:T(8,128)(2,1)}, bf16[256,1536]{1,0:T(8,128)(2,1)}, u32[]{:S(2)}, u32[]{:S(2)}) collective-permute-start(bf16[256,1536]{1,0:T(8,128)(2,1)} %slice.331), channel_id=1, source_target_pairs={{0,1},{1,0},{2,3},{3,2},{4,5},{5,4},{6,7},{7,6},{8,9},{9,8},{10,11... | collective-permute-start | bytes 2359304 | tf_op jit(solution)/shard_map/ppermute | solution.py:32
  392.2 91.3 %collective-permute-start.29 = (bf16[256,1536]{1,0:T(8,128)(2,1)}, bf16[256,1536]{1,0:T(8,128)(2,1)}, u32[]{:S(2)}, u32[]{:S(2)}) collective-permute-start(bf16[256,1536]{1,0:T(8,128)(2,1)} %slice.319), channel_id=1, source_target_pairs={{0,1},{1,0},{2,3},{3,2},{4,5},{5,4},{6,7},{7,6},{8,9},{9,8},{10,11... | collective-permute-start | bytes 2359304 | tf_op jit(solution)/shard_map/ppermute | solution.py:32
  457.2 41.9 %collective-permute-start.90 = (bf16[512,1536]{1,0:T(8,128)(2,1)S(1)}, bf16[512,1536]{1,0:T(8,128)(2,1)S(1)}, u32[]{:S(2)}, u32[]{:S(2)}) collective-permute-start(bf16[512,1536]{1,0:T(8,128)(2,1)S(1)} %constant_dynamic-slice_fusion.2), channel_id=1, source_target_pairs={{0,2},{2,0},{1,3},{3,1},{4,6},{6,4},{5,7},{7,5},{8,10},{10,8},{9,1... | collective-permute-start | bytes 4718600 | tf_op jit(solution)/shard_map/ppermute | solution.py:32
  481.2 53.9 %collective-permute-start.35 = (bf16[256,1536]{1,0:T(8,128)(2,1)S(1)}, bf16[256,1536]{1,0:T(8,128)(2,1)S(1)}, u32[]{:S(2)}, u32[]{:S(2)}) collective-permute-start(bf16[256,1536]{1,0:T(8,128)(2,1)S(1)} %slice.323), channel_id=1, source_target_pairs={{0,1},{1,0},{2,3},{3,2},{4,5},{5,4},{6,7},{7,6},{8,9},{9,8},{10,11... | collective-permute-start | bytes 2359304 | tf_op jit(solution)/shard_map/ppermute | solution.py:32
  483.5 92.0 %collective-permute-start.86 = (bf16[768,2048]{1,0:T(8,128)(2,1)S(1)}, bf16[768,2048]{1,0:T(8,128)(2,1)S(1)}, u32[]{:S(2)}, u32[]{:S(2)}) collective-permute-start(bf16[768,2048]{1,0:T(8,128)(2,1)S(1)} %constant_dynamic-slice_fusion.4), channel_id=1, source_target_pairs={{0,2},{2,0},{1,3},{3,1},{4,6},{6,4},{5,7},{7,5},{8,10},{10,8},{9,1... | collective-permute-start | bytes 9437192 | tf_op jit(solution)/shard_map/ppermute | solution.py:32
  500.4 48.9 %collective-permute-start.54 = (bf16[256,1536]{1,0:T(8,128)(2,1)S(1)}, bf16[256,1536]{1,0:T(8,128)(2,1)S(1)}, u32[]{:S(2)}, u32[]{:S(2)}) collective-permute-start(bf16[256,1536]{1,0:T(8,128)(2,1)S(1)} %copy-done.77), channel_id=1, source_target_pairs={{0,1},{1,0},{2,3},{3,2},{4,5},{5,4},{6,7},{7,6},{8,9},{9,8},{10,11... | collective-permute-start | bytes 2359304 | tf_op jit(solution)/shard_map/ppermute | solution.py:32
  549.3 45.2 %collective-permute-start.92 = (bf16[256,1536]{1,0:T(8,128)(2,1)S(1)}, bf16[256,1536]{1,0:T(8,128)(2,1)S(1)}, u32[]{:S(2)}, u32[]{:S(2)}) collective-permute-start(bf16[256,1536]{1,0:T(8,128)(2,1)S(1)} %get-tuple-element.29), channel_id=1, source_target_pairs={{0,4},{4,0},{1,5},{5,1},{2,6},{6,2},{3,7},{7,3},{8,12},{12,8},{9,1... | collective-permute-start | bytes 2359304 | tf_op jit(solution)/shard_map/ppermute | solution.py:28
  575.4 45.8 %collective-permute-start.40 = (bf16[256,1536]{1,0:T(8,128)(2,1)}, bf16[256,1536]{1,0:T(8,128)(2,1)}, u32[]{:S(2)}, u32[]{:S(2)}) collective-permute-start(bf16[256,1536]{1,0:T(8,128)(2,1)} %get-tuple-element.78), channel_id=1, source_target_pairs={{0,1},{1,0},{2,3},{3,2},{4,5},{5,4},{6,7},{7,6},{8,9},{9,8},{10,11... | collective-permute-start | bytes 2359304 | tf_op jit(solution)/shard_map/ppermute | solution.py:32
  578.2 49.0 %collective-permute-start.87 = (bf16[384,2048]{1,0:T(8,128)(2,1)}, bf16[384,2048]{1,0:T(8,128)(2,1)}, u32[]{:S(2)}, u32[]{:S(2)}) collective-permute-start(bf16[384,2048]{1,0:T(8,128)(2,1)} %constant_dynamic-slice_fusion.3), channel_id=1, source_target_pairs={{0,4},{4,0},{1,5},{5,1},{2,6},{6,2},{3,7},{7,3},{8,12},{12,8},{9,1... | collective-permute-start | bytes 4718600 | tf_op jit(solution)/shard_map/ppermute | solution.py:28
  594.6 129.0 %collective-permute-start.93 = (bf16[512,1536]{1,0:T(8,128)(2,1)S(1)}, bf16[512,1536]{1,0:T(8,128)(2,1)}, u32[]{:S(2)}, u32[]{:S(2)}) collective-permute-start(bf16[512,1536]{1,0:T(8,128)(2,1)S(1)} %constant_dynamic-update-slice_fusion.19), channel_id=1, source_target_pairs={{0,2},{2,0},{1,3},{3,1},{4,6},{6,4},{5,7},{7,5},{8,10},{10,8},{9,1... | collective-permute-start | bytes 4718600 | tf_op jit(solution)/shard_map/ppermute | solution.py:32
  630.9 128.7 %collective-permute-start.88 = (bf16[384,2048]{1,0:T(8,128)(2,1)}, bf16[384,2048]{1,0:T(8,128)(2,1)}, u32[]{:S(2)}, u32[]{:S(2)}) collective-permute-start(bf16[384,2048]{1,0:T(8,128)(2,1)} %get-tuple-element.33), channel_id=1, source_target_pairs={{0,4},{4,0},{1,5},{5,1},{2,6},{6,2},{3,7},{7,3},{8,12},{12,8},{9,1... | collective-permute-start | bytes 4718600 | tf_op jit(solution)/shard_map/ppermute | solution.py:28
  652.0 45.4 %collective-permute-start.64 = (bf16[2,256,512]{2,1,0:T(8,128)(2,1)S(1)}, bf16[2,256,512]{2,1,0:T(8,128)(2,1)S(1)}, u32[]{:S(2)}, u32[]{:S(2)}) collective-permute-start(bf16[2,256,512]{2,1,0:T(8,128)(2,1)S(1)} %dynamic-slice_bitcast_fusion.1), channel_id=1, source_target_pairs={{0,4},{4,0},{1,5},{5,1},{2,6},{6,2},{3,7},{7,3},{8,12},{12,8},{9,1... | collective-permute-start | bytes 1572872 | tf_op jit(solution)/shard_map/ppermute | solution.py:28
  652.4 57.6 %collective-permute-start.80 = (bf16[192,1536]{1,0:T(8,128)(2,1)S(1)}, bf16[192,1536]{1,0:T(8,128)(2,1)S(1)}, u32[]{:S(2)}, u32[]{:S(2)}) collective-permute-start(bf16[192,1536]{1,0:T(8,128)(2,1)S(1)} %constant_dynamic-slice_fusion.6), channel_id=1, source_target_pairs={{0,4},{4,0},{1,5},{5,1},{2,6},{6,2},{3,7},{7,3},{8,12},{12,8},{9,1... | collective-permute-start | bytes 1769480 | tf_op jit(solution)/shard_map/ppermute | solution.py:28
  761.2 52.6 %collective-permute-start.89 = (bf16[768,2048]{1,0:T(8,128)(2,1)S(1)}, bf16[768,2048]{1,0:T(8,128)(2,1)S(1)}, u32[]{:S(2)}, u32[]{:S(2)}) collective-permute-start(bf16[768,2048]{1,0:T(8,128)(2,1)S(1)} %constant_dynamic-update-slice_fusion.21), channel_id=1, source_target_pairs={{0,2},{2,0},{1,3},{3,1},{4,6},{6,4},{5,7},{7,5},{8,10},{10,8},{9,1... | collective-permute-start | bytes 9437192 | tf_op jit(solution)/shard_map/ppermute | solution.py:32
  (180 other events, 2890.8 us)

commit v2 on v1

v2 whole, which is shorter than its diff:
```python
import functools
import math

import jax
import jax.numpy as jnp
from jax import lax
from jax.experimental import pallas as pl
from jax.experimental.pallas import tpu as pltpu
from jax.sharding import Mesh
from jax.sharding import PartitionSpec as P

HEAD = 64
TOPK = 8
E = 16
CAP = 256
EPSILON = 1e-06
BF = jnp.bfloat16
F32 = jnp.float32
NEG = -1e30
FAR = 1e6


def dot(a, b, ca, cb):
    return lax.dot_general(a, b, (((ca,), (cb,)), ((), ())), preferred_element_type=F32)


def shift(v, axis, n, by=1):
    return lax.ppermute(v, axis, [(i, (i + by) % n) for i in range(n)])


def swap(v, axis):
    return lax.ppermute(v, axis, [(0, 1), (1, 0)])


def pick(v, index, parts, dim):
    size = v.shape[dim] // parts
    return lax.dynamic_slice_in_dim(v, index * size, size, dim)


def put(buffer, v, start, dim):
    return lax.dynamic_update_slice_in_dim(buffer, v, start, dim)


def after(v, *others):
    return lax.optimization_barrier((v,) + others)[0]


def direct_reduce(part, axis, n):
    me = lax.axis_index(axis)
    total = part(me)
    for s in range(1, n):
        total = total + shift(part((me + s) % n).astype(BF), axis, n, s).astype(F32)
    return total


def ring_reduce(part, axis, n, *others):
    me = lax.axis_index(axis)
    moving = part((me + n - 1) % n).astype(BF)
    for s in range(2, n):
        moving = (shift(moving, axis, n).astype(F32) + part((me + n - s) % n)).astype(BF)
    moving = shift(moving, axis, n)
    if others:
        moving = after(moving, *others)
    return moving.astype(F32) + part(me)


def core_halves(v, dim):
    core = lax.axis_index("core")
    mine = pick(v, core, 2, dim)
    theirs = pick(v, 1 - core, 2, dim)
    return mine.astype(F32) + swap(theirs.astype(BF), "core").astype(F32)


def core_join(v, dim):
    other = swap(v, "core")
    first = lax.axis_index("core") == 0
    return jnp.concatenate([jnp.where(first, v, other), jnp.where(first, other, v)], axis=dim)


def ring_gather(v, axis, n, dim):
    me = lax.axis_index(axis)
    size = v.shape[dim]
    shape = list(v.shape)
    shape[dim] = size * n
    out = put(jnp.zeros(shape, v.dtype), v, me * size, dim)
    moving = v
    for s in range(1, n):
        moving = shift(moving, axis, n)
        out = put(out, moving, ((me + n - s) % n) * size, dim)
    return out


def ctx_total(v, n_cx):
    half = core_halves(v, 0).astype(BF)
    part = ring_reduce(lambda j: pick(half, j, n_cx, 0).astype(F32), "cx", n_cx).astype(BF)
    return core_join(ring_gather(part, "cx", n_cx, 0), 0)


def normalize(values):
    inverse = lax.rsqrt(jnp.mean(values * values, axis=-1, keepdims=True) + EPSILON)
    return inverse, values * inverse


def norm_backward(grad, gain, inverse, normed):
    scaled = grad * gain
    return inverse * (scaled - normed * jnp.mean(scaled * normed, axis=-1, keepdims=True))


def rotate(v, cos, sin, inverse):
    rows = v.shape[1]
    shaped = v.reshape(-1, 2, HEAD // 2, rows)
    a, b = shaped[:, 0], shaped[:, 1]
    if inverse:
        out = jnp.stack([a * cos + b * sin, b * cos - a * sin], axis=1)
    else:
        out = jnp.stack([a * cos - b * sin, b * cos + a * sin], axis=1)
    return out.reshape(-1, rows)


def keep_plan(routes, order, live):
    rows = routes.shape[0]
    pairs = rows * TOPK
    token, choice = order // TOPK, order % TOPK
    rank = jnp.arange(pairs, dtype=jnp.int32)
    at_token = (jnp.arange(rows, dtype=jnp.int32)[:, None] == token[None, :]).astype(BF)
    at_choice = jnp.arange(TOPK, dtype=jnp.int32)[:, None] == choice[None, :]
    high = jnp.where(at_choice, (rank // 64)[None, :], 0).astype(BF)
    low = jnp.where(at_choice, (rank % 64)[None, :], 0).astype(BF)
    place = dot(at_token, jnp.concatenate([high, low], axis=0), 1, 1)
    place = place[:, :TOPK] * 64.0 + place[:, TOPK:]
    hits = routes[:, :, None] == jnp.arange(E, dtype=jnp.int32)[None, None, :]
    routed = jnp.any(hits, axis=1)
    place_e = jnp.sum(jnp.where(hits, place[:, :, None], 0.0), axis=1)
    place_e = jnp.where(routed & live[:, None], place_e, FAR)
    across = place_e.T
    earlier = jnp.sum((place_e[:, :, None] < across[None, :, :]).astype(F32), axis=0).T
    kept = routed & live[:, None] & (earlier < CAP)
    return routed, kept


def assemble(info_ref, own_ref, got_ref, other_ref, full_ref):
    z, core = info_ref[0], info_ref[1]
    rows = own_ref.shape[0]
    piece = rows // 2
    n_z = got_ref.shape[0] + 1
    full_ref[pl.ds(pl.multiple_of(z * rows, piece), rows), :] = own_ref[...]
    for s in range(1, n_z):
        start = ((z + n_z - s) % n_z) * rows
        mine = pl.multiple_of(start + core * piece, piece)
        theirs = pl.multiple_of(start + (1 - core) * piece, piece)
        full_ref[pl.ds(mine, piece), :] = got_ref[s - 1]
        full_ref[pl.ds(theirs, piece), :] = other_ref[s - 1]


def project_kernel(turned, scale, info_ref, own_ref, got_ref, other_ref, x_ref, cos_ref, sin_ref, out_ref, full_ref):
    assemble(info_ref, own_ref, got_ref, other_ref, full_ref)
    flat = jnp.dot(x_ref[...], full_ref[...], preferred_element_type=F32).T
    cos, sin = cos_ref[...], sin_ref[...]
    quarter = HEAD // 2
    for start in range(0, turned, HEAD):
        a = flat[start : start + quarter, :]
        b = flat[start + quarter : start + HEAD, :]
        out_ref[start : start + quarter, :] = ((a * cos - b * sin).astype(BF) * scale).astype(BF)
        out_ref[start + quarter : start + HEAD, :] = ((b * cos + a * sin).astype(BF) * scale).astype(BF)
    if turned < flat.shape[0]:
        out_ref[turned:, :] = flat[turned:, :].astype(BF)


def project(info, own, got, other, x, cos, sin, turned, scale):
    columns = own.shape[1]
    rows, width = x.shape
    return pl.pallas_call(
        functools.partial(project_kernel, turned, scale),
        name="project",
        grid_spec=pltpu.PrefetchScalarGridSpec(num_scalar_prefetch=1, grid=(1,),
            in_specs=[pl.BlockSpec(v.shape, lambda i, n, k=v.ndim: (0,) * k) for v in (own, got, other, x, cos, sin)],
            out_specs=[
                pl.BlockSpec((columns, rows), lambda i, n: (0, 0)),
                pl.BlockSpec((width, columns), lambda i, n: (0, 0)),
            ],
        ),
        out_shape=[
            jax.ShapeDtypeStruct((columns, rows), BF),
            jax.ShapeDtypeStruct((width, columns), BF),
        ],
        compiler_params=pltpu.CompilerParams(vmem_limit_bytes=40 << 20),
        cost_estimate=pl.CostEstimate(
            flops=2 * rows * width * columns,
            transcendentals=0,
            bytes_accessed=4 * width * columns + 2 * rows * (width + columns),
        ),
    )(info, own, got, other, x, cos, sin)


def assembled(info, own, got, other):
    rows, columns = own.shape
    full = (rows * (got.shape[0] + 1), columns)
    return pl.pallas_call(
        assemble,
        name="assembled",
        grid_spec=pltpu.PrefetchScalarGridSpec(num_scalar_prefetch=1, grid=(1,),
            in_specs=[pl.BlockSpec(v.shape, lambda i, n, k=v.ndim: (0,) * k) for v in (own, got, other)],
            out_specs=pl.BlockSpec(full, lambda i, n: (0, 0)),
        ),
        out_shape=jax.ShapeDtypeStruct(full, BF),
        compiler_params=pltpu.CompilerParams(vmem_limit_bytes=32 << 20),
        cost_estimate=pl.CostEstimate(flops=0, transcendentals=0, bytes_accessed=4 * rows * columns * 4),
    )(info, own, got, other)


def softmax_block(q, k, last, base, first_row, length):
    s = lax.dot_general(k, q, (((0,), (0,)), ((), ())), preferred_element_type=F32)
    if last:
        key = base + lax.broadcasted_iota(jnp.int32, s.shape, 0)
        query = first_row + lax.broadcasted_iota(jnp.int32, s.shape, 1)
        s = jnp.where((key <= query) & (key < length), s, NEG)
    return s


def slot_of(block, ctx, n_ctx):
    n_cx = n_ctx // 2
    steps = (ctx // 2 + n_cx - block // 2) % n_cx
    return ((ctx + block) % 2) * n_cx + steps


def attend_kernel(group, info_ref, q_ref, kv_ref, o_ref, lse_ref):
    count, first_row, length, ctx = info_ref[0], info_ref[1], info_ref[2], info_ref[3]
    rows = q_ref.shape[1]
    n_ctx = kv_ref.shape[0]
    keys = kv_ref.shape[3]
    for h in range(group):
        q = q_ref[h * HEAD : (h + 1) * HEAD, :]

        def step(j, carry, last):
            top, total, acc = carry
            slot = slot_of(j, ctx, n_ctx)
            k = kv_ref[slot, 0]
            v = kv_ref[slot, 1]
            s = softmax_block(q, k, last, j * keys, first_row, length)
            new_top = jnp.maximum(top, jnp.max(s, axis=0, keepdims=True))
            p = jnp.exp(s - new_top)
            fade = jnp.exp(top - new_top)
            total = total * fade + jnp.sum(p, axis=0, keepdims=True)
            acc = acc * fade + jnp.dot(v, p.astype(BF), preferred_element_type=F32)
            return new_top, total, acc

        carry = (
            jnp.full((1, rows), NEG, F32),
            jnp.zeros((1, rows), F32),
            jnp.zeros((HEAD, rows), F32),
        )
        carry = lax.fori_loop(0, count - 1, functools.partial(step, last=False), carry)
        top, total, acc = step(count - 1, carry, True)
        o_ref[h * HEAD : (h + 1) * HEAD, :] = (acc / total).astype(BF)
        lse_ref[0, h : h + 1, :] = top + jnp.log(total)


def attend(q, kv, info, group, start, heads):
    rows = q.shape[1]
    n_ctx, _, depth, keys = kv.shape
    return pl.pallas_call(
        functools.partial(attend_kernel, group),
        name="attend",
        grid_spec=pltpu.PrefetchScalarGridSpec(
            num_scalar_prefetch=1,
            grid=(heads,),
            in_specs=[
                pl.BlockSpec((group * HEAD, rows), lambda g, i: (start + g, 0)),
                pl.BlockSpec((n_ctx, 2, HEAD, keys), lambda g, i: (0, 0, start + g, 0)),
            ],
            out_specs=[
                pl.BlockSpec((group * HEAD, rows), lambda g, i: (g, 0)),
                pl.BlockSpec((1, 8, rows), lambda g, i: (g, 0, 0)),
            ],
        ),
        out_shape=[
            jax.ShapeDtypeStruct((heads * group * HEAD, rows), BF),
            jax.ShapeDtypeStruct((heads, 8, rows), F32),
        ],
        compiler_params=pltpu.CompilerParams(vmem_limit_bytes=48 << 20),
        cost_estimate=pl.CostEstimate(
            flops=4 * heads * group * HEAD * rows * n_ctx * keys,
            transcendentals=heads * group * rows * n_ctx * keys,
            bytes_accessed=2 * q.size + kv.size,
        ),
    )(info, q, kv)


def attend_back_kernel(group, info_ref, q_ref, kv_ref, o_ref, do_ref, lse_ref, dq_ref, dkv_ref):
    count, first_row, length, ctx = info_ref[0], info_ref[1], info_ref[2], info_ref[3]
    n_ctx = kv_ref.shape[0]
    keys = kv_ref.shape[3]
    delta = []
    for h in range(group):
        part = slice(h * HEAD, (h + 1) * HEAD)
        delta.append(
            jnp.sum(do_ref[part, :].astype(F32) * o_ref[part, :].astype(F32), axis=0, keepdims=True)
        )
    dq_ref[...] = jnp.zeros_like(dq_ref)

    def step(j, last):
        slot = slot_of(j, ctx, n_ctx)
        k = kv_ref[slot, 0]
        v = kv_ref[slot, 1]
        dk = jnp.zeros((keys, HEAD), F32)
        dv = jnp.zeros((keys, HEAD), F32)
        for h in range(group):
            part = slice(h * HEAD, (h + 1) * HEAD)
            q = q_ref[part, :]
            do = do_ref[part, :]
            s = softmax_block(q, k, last, j * keys, first_row, length)
            p = jnp.exp(s - lse_ref[0, h : h + 1, :])
            dp = lax.dot_general(v, do, (((0,), (0,)), ((), ())), preferred_element_type=F32)
            ds = (p * (dp - delta[h])).astype(BF)
            pb = p.astype(BF)
            dv += lax.dot_general(pb, do, (((1,), (1,)), ((), ())), preferred_element_type=F32)
            dk += lax.dot_general(ds, q, (((1,), (1,)), ((), ())), preferred_element_type=F32)
            dq_ref[part, :] += jnp.dot(k, ds, preferred_element_type=F32)
        dkv_ref[slot, 0] = dk.T.astype(BF)
        dkv_ref[slot, 1] = dv.T.astype(BF)

    @pl.loop(0, count - 1)
    def _(j):
        step(j, False)

    step(count - 1, True)

    @pl.loop(count, n_ctx)
    def _(j):
        dkv_ref[slot_of(j, ctx, n_ctx)] = jnp.zeros(dkv_ref.shape[1:], BF)


def attend_back(q, kv, o, do, lse, info, group):
    rows = q.shape[1]
    n_ctx, _, depth, keys = kv.shape
    heads = depth // HEAD
    wide = pl.BlockSpec((group * HEAD, rows), lambda g, i: (g, 0))
    blocks = pl.BlockSpec((n_ctx, 2, HEAD, keys), lambda g, i: (0, 0, g, 0))
    return pl.pallas_call(
        functools.partial(attend_back_kernel, group),
        name="attend_back",
        grid_spec=pltpu.PrefetchScalarGridSpec(
            num_scalar_prefetch=1,
            grid=(heads,),
            in_specs=[
                wide,
                blocks,
                wide,
                wide,
                pl.BlockSpec((1, 8, rows), lambda g, i: (g, 0, 0)),
            ],
            out_specs=[wide, blocks],
        ),
        out_shape=[
            jax.ShapeDtypeStruct(q.shape, F32),
            jax.ShapeDtypeStruct(kv.shape, BF),
        ],
        compiler_params=pltpu.CompilerParams(vmem_limit_bytes=48 << 20),
        cost_estimate=pl.CostEstimate(
            flops=10 * q.shape[0] * rows * n_ctx * keys,
            transcendentals=q.shape[0] // HEAD * rows * n_ctx * keys,
            bytes_accessed=10 * q.size + 4 * kv.size,
        ),
    )(info, q, kv, o, do, lse)


def expert_kernel(aliased, info_ref, near_in, far_in, near_do, far_do, gate_ref, up_ref, down_ref, *refs):
    if aliased:
        refs = refs[1:]
    near_out, far_out, mix_out, act_out, dg_out, du_out = refs[:6]
    rows_x, rows_do, shares_in, mix_sum, back_sum, shares_out = refs[6:]
    e = pl.program_id(0)
    half, width = near_do.shape[2:]
    rows = 2 * half

    @pl.when(e == 0)
    def _():
        rows_x[:half, :] = near_in[:, :width]
        rows_x[half:, :] = far_in[:, :width]
        rows_do[:half, :] = near_do[0, 0]
        rows_do[half:, :] = far_do[0, 0]
        shares_in[:half, :] = near_in[:, width:].astype(F32)
        shares_in[half:, :] = far_in[:, width:].astype(F32)

    lanes = lax.broadcasted_iota(jnp.int32, (rows, 128), 1)
    x = rows_x[...]
    do = rows_do[...]
    per, _, hidden = gate_ref.shape
    mix = back = share = None
    for i in range(per):
        chosen = info_ref[0] + e * per + i
        gate, up, down = gate_ref[i], up_ref[i], down_ref[i]
        weight = jnp.sum(
            jnp.where((lanes == chosen) | (lanes == chosen + E), shares_in[...], 0.0),
            axis=1,
            keepdims=True,
        )
        g = jnp.dot(x, gate, preferred_element_type=F32)
        u = jnp.dot(x, up, preferred_element_type=F32)
        dact = dot(do, down, 1, 1)
        sig = jax.nn.sigmoid(g)
        silu = g * sig
        act = silu * u
        share_i = jnp.where(lanes == chosen, jnp.sum(act * dact, axis=1, keepdims=True), 0.0)
        dhid = dact * weight
        part = slice(i * hidden, (i + 1) * hidden)
        act_out[:, part] = (act * weight).astype(BF)
        dg_out[:, part] = (dhid * u * (sig * (1.0 + g * (1.0 - sig)))).astype(BF)
        du_out[:, part] = (dhid * silu).astype(BF)
        mix_i = jnp.dot(act_out[:, part], down, preferred_element_type=F32)
        back_i = dot(dg_out[:, part], gate, 1, 1) + dot(du_out[:, part], up, 1, 1)
        mix = mix_i if mix is None else mix + mix_i
        back = back_i if back is None else back + back_i
        share = share_i if share is None else share + share_i

    @pl.when(e == 0)
    def _():
        mix_sum[...] = mix
        back_sum[...] = back
        shares_out[...] = share

    @pl.when(e > 0)
    def _():
        mix_sum[...] += mix
        back_sum[...] += back
        shares_out[...] += share

    @pl.when(e == pl.num_programs(0) - 1)
    def _():
        near_out[:, :width] = back_sum[:half, :].astype(BF)
        near_out[:, width:] = shares_out[:half, :].astype(BF)
        far_out[:, :width] = back_sum[half:, :].astype(BF)
        far_out[:, width:] = shares_out[half:, :].astype(BF)
        tp = info_ref[1]
        mix_out[0, tp] = mix_sum[:half, :].astype(BF)
        mix_out[0, 1 - tp] = mix_sum[half:, :].astype(BF)


def experts(info, near, far, do_near, do_far, n_z, gate, up, down, mix_all):
    half, wide = near.shape
    width = do_near.shape[3]
    held, _, hidden = gate.shape
    rows = 2 * half
    whole = lambda shape: pl.BlockSpec(shape, lambda e, i: (0, 0))
    per = 1
    each = lambda shape: pl.BlockSpec((per,) + shape, lambda e, i: (e, 0, 0))
    column = pl.BlockSpec((rows, per * hidden), lambda e, i: (0, e))
    mid = jax.ShapeDtypeStruct((rows, held * hidden), BF)
    message = jax.ShapeDtypeStruct((half, wide), BF)
    aliased = mix_all is not None
    return pl.pallas_call(
        functools.partial(expert_kernel, aliased),
        name="experts",
        grid_spec=pltpu.PrefetchScalarGridSpec(
            num_scalar_prefetch=1,
            grid=(held // per,),
            in_specs=[
                whole((half, wide)),
                whole((half, wide)),
                pl.BlockSpec((1, 1, half, width), lambda e, i: (i[3], i[4], 0, 0)),
                pl.BlockSpec((1, 1, half, width), lambda e, i: (i[5], i[4], 0, 0)),
                each((width, hidden)),
                each((width, hidden)),
                each((hidden, width)),
            ]
            + [pl.BlockSpec(memory_space=pl.ANY)] * aliased,
            out_specs=[
                whole((half, wide)),
                whole((half, wide)),
                pl.BlockSpec((1, 2, half, width), lambda e, i: (i[2], 0, 0, 0)),
                column,
                column,
                column,
            ],
            scratch_shapes=[
                pltpu.VMEM((rows, width), BF),
                pltpu.VMEM((rows, width), BF),
                pltpu.VMEM((rows, 128), F32),
                pltpu.VMEM((rows, width), F32),
                pltpu.VMEM((rows, width), F32),
                pltpu.VMEM((rows, 128), F32),
            ],
        ),
        out_shape=[
            message,
            message,
            jax.ShapeDtypeStruct((n_z, 2, half, width), BF),
            mid,
            mid,
            mid,
        ],
        input_output_aliases={8: 2} if aliased else {},
        compiler_params=pltpu.CompilerParams(vmem_limit_bytes=56 << 20),
        cost_estimate=pl.CostEstimate(
            flops=12 * rows * width * held * hidden,
            transcendentals=rows * held * hidden,
            bytes_accessed=6 * held * hidden * width + 16 * rows * width,
        ),
    )(info, near, far, do_near, do_far, gate, up, down, *([mix_all] if aliased else []))


def weight_grad_kernel(count, info_ref, *refs):
    lefts = refs[:count]
    rights = refs[count:-2]
    out, turned = refs[-2:]
    size = lefts[0].shape[0]

    @pl.when(pl.program_id(0) == 0)
    def _():
        for i, left in enumerate(lefts):
            turned[:, i * size : (i + 1) * size] = left[:, : turned.shape[0]].T

    half = len(rights) // 2
    for i, blocks in enumerate((rights[:half], rights[half:])):
        out[0, i] = jnp.dot(
            turned[...],
            jnp.concatenate([block[...] for block in blocks], axis=0),
            preferred_element_type=F32,
        ).astype(BF)


def weight_grads(info, chunks, firsts, seconds, held, width):
    size, wide = chunks[0].shape
    rows, mid = firsts[0].shape
    hidden = mid // held
    at = 1 + len(firsts)
    column = pl.BlockSpec((rows, hidden), lambda e, i: (0, i[at + e]))
    return pl.pallas_call(
        functools.partial(weight_grad_kernel, len(chunks)),
        name="weight_grads",
        grid_spec=pltpu.PrefetchScalarGridSpec(
            num_scalar_prefetch=1,
            grid=(held,),
            in_specs=[
                pl.BlockSpec((size, wide), lambda e, i: (0, 0), pipeline_mode=pl.Buffered(1))
                for _ in chunks
            ]
            + [column for _ in firsts + seconds],
            out_specs=pl.BlockSpec((1, 2, width, hidden), lambda e, i: (e, 0, 0, 0)),
            scratch_shapes=[pltpu.VMEM((width, size * len(chunks)), BF)],
        ),
        out_shape=jax.ShapeDtypeStruct((held, 2, width, hidden), BF),
        compiler_params=pltpu.CompilerParams(vmem_limit_bytes=58 << 20),
        cost_estimate=pl.CostEstimate(
            flops=4 * len(firsts) * rows * width * mid,
            transcendentals=0,
            bytes_accessed=4 * len(firsts) * rows * (width + mid),
        ),
    )(info, *chunks, *firsts, *seconds)


def down_grad_kernel(count, info_ref, *refs):
    rights = refs[: 2 * count]
    lefts = refs[2 * count : 3 * count]
    total = None
    for i, left in enumerate(lefts):
        right = jnp.concatenate([rights[2 * i][0, 0], rights[2 * i + 1][0, 0]], axis=0)
        term = dot(left[...], right, 0, 0)
        total = term if total is None else total + term
    refs[-1][0] = total.astype(BF)


def down_grads(info, do_all, acts, held):
    _, n_z, size, width = do_all.shape
    rows, mid = acts[0].shape
    hidden = mid // held
    at = 1 + n_z
    chunk = lambda other, s: pl.BlockSpec(
        (1, 1, size, width),
        lambda e, i: ((1 - i[0]) if other else i[0], i[1 + s], 0, 0),
        pipeline_mode=pl.Buffered(1),
    )
    return pl.pallas_call(
        functools.partial(down_grad_kernel, n_z),
        name="down_grads",
        grid_spec=pltpu.PrefetchScalarGridSpec(
            num_scalar_prefetch=1,
            grid=(held,),
            in_specs=[chunk(other, s) for s in range(n_z) for other in (False, True)]
            + [pl.BlockSpec((rows, hidden), lambda e, i: (0, i[at + e])) for _ in acts],
            out_specs=pl.BlockSpec((1, hidden, width), lambda e, i: (e, 0, 0)),
        ),
        out_shape=jax.ShapeDtypeStruct((held, hidden, width), BF),
        compiler_params=pltpu.CompilerParams(vmem_limit_bytes=56 << 20),
        cost_estimate=pl.CostEstimate(
            flops=2 * len(acts) * rows * width * mid,
            transcendentals=0,
            bytes_accessed=2 * len(acts) * rows * (width + mid),
        ),
    )(info, *([do_all] * (2 * n_z)), *acts)


def place_kernel(count, info_ref, *refs):
    for i, ref in enumerate(refs[:count]):

        @pl.when(pl.program_id(0) == i)
        def _():
            for k, out in enumerate(refs[count:]):
                out[0] = ref[0, k].astype(F32)


def place(info, parts):
    kinds = parts[0][0].shape[1]
    shape = parts[0][0].shape[2:]
    return pl.pallas_call(
        functools.partial(place_kernel, len(parts)),
        name="place",
        grid_spec=pltpu.PrefetchScalarGridSpec(
            num_scalar_prefetch=1,
            grid=(len(parts),),
            in_specs=[
                pl.BlockSpec((1, kinds) + shape, lambda e, i, k=k: (k, 0, 0, 0)) for _, k in parts
            ],
            out_specs=[pl.BlockSpec((1,) + shape, lambda e, i: (i[e], 0, 0))] * kinds,
        ),
        out_shape=[jax.ShapeDtypeStruct((len(parts),) + shape, F32)] * kinds,
        compiler_params=pltpu.CompilerParams(vmem_limit_bytes=48 << 20),
        cost_estimate=pl.CostEstimate(
            flops=0, transcendentals=0, bytes_accessed=6 * kinds * len(parts) * math.prod(shape)
        ),
    )(info, *[array for array, _ in parts])


def local(
    sizes,
    tokens,
    lengths,
    routes,
    visit_order,
    cotangent,
    first_gain,
    query_weight,
    key_matrix,
    value_matrix,
    output_weight,
    second_gain,
    router_weight,
    gate_weight,
    up_weight,
    down_weight,
):
    n_z, n_cx = sizes
    n_ctx = 2 * n_cx
    z = lax.axis_index("fsdp")
    cx = lax.axis_index("cx")
    core = lax.axis_index("core")
    tp = lax.axis_index("tp")
    ctx = cx * 2 + core
    rows, width = tokens.shape[1:]
    half = rows // 2
    shard = query_weight.shape[0]
    q_width = query_weight.shape[1]
    kv_width = key_matrix.shape[1]
    group = q_width // kv_width
    held = gate_weight.shape[0]
    hidden = gate_weight.shape[2]
    first_row = ctx * rows
    length = lengths[0]
    positions = first_row + jnp.arange(rows, dtype=jnp.int32)
    live = positions < length
    valid = live.astype(F32)[:, None]

    small = jnp.concatenate(
        [first_gain[None], second_gain[None], router_weight.T], axis=0
    )
    small_full = put(jnp.zeros((2 + E, width), BF), small, z * shard, 1)
    for s in range(1, n_z):
        small_full = put(small_full, shift(small, "fsdp", n_z, s), ((z + n_z - s) % n_z) * shard, 1)
    gain_first = small_full[0:1].astype(F32)
    gain_second = small_full[1:2].astype(F32)
    router = small_full[2:]

    grad_half = (pick(cotangent[0], tp, 2, 0).astype(F32) * pick(valid, tp, 2, 0)).astype(BF)
    grad_other = swap(grad_half, "tp")

    def bring(own):
        piece = pick(own, core, 2, 0)
        return own, [shift(piece, "fsdp", n_z, s) for s in range(1, n_z)]

    def spread(own, got):
        got = jnp.stack(got)
        return own, got, swap(got, "core")

    kv_pieces = spread(*bring(jnp.concatenate([key_matrix, value_matrix], axis=1)))
    q_own, q_got = bring(after(query_weight, kv_pieces[1]))
    here = jnp.stack([z, core]).astype(jnp.int32)

    routed, kept = keep_plan(routes[0], visit_order[0, 0], live)

    inputs = tokens[0].astype(F32)
    inverse_one, normed_one = normalize(inputs)
    hidden_one = (normed_one * gain_first).astype(BF)
    frequency = jnp.exp(
        jnp.arange(HEAD // 2, dtype=F32) * (-2.0 * math.log(10000.0) / HEAD)
    )
    angles = frequency[:, None] * positions.astype(F32)[None, :]
    cos, sin = jnp.cos(angles), jnp.sin(angles)
    scale = HEAD**-0.5
    kv_mine, w_kv = project(here, *kv_pieces, hidden_one, cos, sin, kv_width, 1.0)
    kv_mine = kv_mine.reshape(1, 2, kv_width, rows)
    near_kv = [kv_mine]
    for s in range(1, n_cx):
        near_kv.append(shift(near_kv[-1], "cx", n_cx))
    near_kv = jnp.concatenate(near_kv, axis=0)
    q_pieces = spread(q_own, [after(v, near_kv) for v in q_got])
    o_own, o_got = bring(after(output_weight.T, q_pieces[1]))
    grad_all = lax.all_gather(after(grad_half, q_pieces[1]), ("tp", "fsdp"))
    grad_all = grad_all.reshape(2, n_z, half, width)
    query, w_q = project(here, *q_pieces, hidden_one, cos, sin, q_width, scale)
    kv = jnp.concatenate([near_kv, swap(near_kv, "core")], axis=0)
    count = jnp.minimum(ctx + 1, (length + rows - 1) // rows)
    info = jnp.stack([count, first_row, length, ctx])
    kv_heads = kv_width // HEAD
    split = [(0, kv_heads // 2), (kv_heads // 2, kv_heads - kv_heads // 2)]
    early, early_lse = attend(after(query, grad_other), kv, info, group, *split[0])
    o_pieces = spread(o_own, [after(v, early) for v in o_got])
    later, later_lse = attend(after(query, early), kv, info, group, *split[1])
    attended = jnp.concatenate([early, later], axis=0)
    lse = jnp.concatenate([early_lse, later_lse], axis=0)
    o_full = assembled(here, *[after(v, later) for v in o_pieces])

    far = dot(pick(attended, 1 - tp, 2, 1), o_full, 0, 1).astype(BF)
    near = dot(pick(attended, tp, 2, 1), o_full, 0, 1)
    residual = pick(tokens[0], tp, 2, 0).astype(F32) + near + swap(far, "tp").astype(F32)
    inverse_two, normed_two = normalize(residual)
    hidden_two = (normed_two * gain_second).astype(BF)
    logits = dot(hidden_two, router, 1, 1)
    routed_half = pick(routed, tp, 2, 0)
    kept_half = pick(kept, tp, 2, 0).astype(F32)
    masked = jnp.where(routed_half, logits, NEG)
    raised = jnp.where(
        routed_half, jnp.exp(masked - jnp.max(masked, axis=1, keepdims=True)), 0.0
    )
    gates = raised / jnp.sum(raised, axis=1, keepdims=True)
    weights = gates * kept_half

    high = weights.astype(BF)
    low = (weights - high.astype(F32)).astype(BF)
    message = jnp.concatenate(
        [hidden_two, high, low, jnp.zeros((half, 128 - 2 * E), BF)], axis=1
    )
    blocks = [(z + n_z - s) % n_z for s in range(n_z)]
    near = [message]
    far = [swap(message, "tp")]
    coming = shift(message, "fsdp", n_z)
    done, mix_all, moving, joined = [], None, None, ()
    for s in range(n_z):
        first = near[s]
        if s + 1 < n_z:
            near.append(after(coming, *[d[0] for d in done[-1:]]))
            far.append(swap(near[-1], "tp"))
            first = after(first, near[-1])
            if s + 2 < n_z:
                coming = shift(near[-1], "fsdp", n_z)
        first = after(first, *joined)
        if s:
            info_s = [z * held, tp, blocks[s], tp, blocks[s], 1 - tp]
            rows_do = (grad_all, grad_all)
        else:
            info_s = [z * held, tp, blocks[s], 0, 0, 0]
            rows_do = (grad_half[None, None], grad_other[None, None])
        done.append(
            experts(
                jnp.stack([jnp.asarray(v, jnp.int32) for v in info_s]),
                first,
                far[s],
                *rows_do,
                n_z,
                gate_weight,
                up_weight,
                down_weight,
                mix_all,
            )
        )
        mix_all = done[s][2]
        if s > 1:
            part = done[s - 1][0].astype(F32) + swap(done[s - 1][1], "tp").astype(F32)
            if s > 2:
                part = shift(moving, "fsdp", n_z).astype(F32) + part
            moving = part.astype(BF)
            joined = (moving,)
    last = swap(done[-1][1], "tp")
    by_ctx = held == n_ctx and n_cx == 2
    if by_ctx:
        slots = [(1 - core) * 2 + 1 - cx, (1 - core) * 2 + cx, core * 2 + 1 - cx, core * 2 + cx]
    else:
        slots = list(range(held))
    order = jnp.stack([jnp.asarray(v, jnp.int32) for v in [tp] + blocks + slots])
    grad_pair = weight_grads(
        order,
        [v for s in range(n_z) for v in (near[s], far[s])],
        [done[s][4] for s in range(n_z)],
        [after(done[s][5], moving) for s in range(n_z)],
        held,
        width,
    )
    part = done[-1][0].astype(F32) + after(last, grad_pair).astype(F32)
    moving = (shift(moving, "fsdp", n_z).astype(F32) + part).astype(BF)
    own = done[0][0].astype(F32) + swap(after(done[0][1], last), "tp").astype(F32)
    grad_down = down_grads(
        order, grad_all, [after(done[s][3], moving) for s in range(n_z)], held
    )[:, None]
    back = shift(moving, "fsdp", n_z)

    half_held = held // 2

    def core_stage(v, *others):
        both = v[half_held:].astype(F32) + after(swap(v[:half_held], "core"), *others).astype(F32)
        return both, both[:1].astype(BF)

    if by_ctx:
        pair_half, pair_far = core_stage(grad_pair, grad_down)
        back, own = after(back, pair_far), after(own, pair_far)
        pair_far = swap(pair_far, "cx")
    back = back.astype(F32) + own
    hidden_grad = back[:, :width]
    gate_grad = back[:, width : width + E] * kept_half

    mixture = lax.psum_scatter(
        after(mix_all, back).reshape(2 * n_z * half, width),
        ("fsdp", "tp"),
        scatter_dimension=0,
        tiled=True,
    )

    logit_grad = (
        gates * (gate_grad - jnp.sum(gates * gate_grad, axis=1, keepdims=True))
    ).astype(BF)
    hidden_grad = hidden_grad + dot(logit_grad, router, 1, 0)
    grad_router = dot(logit_grad, hidden_two, 0, 0)
    grad_second = jnp.sum(hidden_grad * normed_two, axis=0, keepdims=True)
    branch_half = (
        grad_half.astype(F32) + norm_backward(hidden_grad, gain_second, inverse_two, normed_two)
    ).astype(BF)
    lead = tp == 0
    branch_other = swap(branch_half, "tp")
    if by_ctx:
        down_half, down_far = core_stage(grad_down)
        branch_other = after(branch_other, down_far)
        down_far = swap(down_far, "cx")
    branch = jnp.concatenate(
        [jnp.where(lead, branch_half, branch_other), jnp.where(lead, branch_other, branch_half)],
        axis=0,
    )

    attended_grad = dot(o_full, branch, 0, 1).astype(BF)
    grad_output = dot(attended, branch, 1, 0).astype(BF)
    attended_grad = after(attended_grad, grad_output)

    grad_query_rot, grad_kv = attend_back(
        query, kv, attended, attended_grad, lse, info, group
    )
    kv_sum = grad_kv[:n_cx].astype(F32) + swap(grad_kv[n_cx:], "core").astype(F32)
    kv_moving = kv_sum[1].astype(BF)
    for s in range(2, n_cx):
        kv_moving = (shift(kv_moving, "cx", n_cx).astype(F32) + kv_sum[s]).astype(BF)
    kv_grad = shift(kv_moving, "cx", n_cx).astype(F32) + kv_sum[0]
    query_grad = (rotate(grad_query_rot, cos, sin, True) * scale).astype(BF)
    key_grad = rotate(kv_grad[0], cos, sin, True).astype(BF)
    value_grad = kv_grad[1].astype(BF)
    grad_both = jnp.concatenate([key_grad, value_grad], axis=0)
    first_part = dot(query_grad, w_q, 0, 1) + dot(grad_both, w_kv, 0, 1)
    grad_first = jnp.sum(first_part * normed_one, axis=0, keepdims=True)
    first_low = first_part.astype(BF)
    first_other = swap(first_low, "tp")
    if by_ctx:
        down_total = (down_half[1:] + after(down_far, first_low).astype(F32)).astype(BF)
        pair_total = (pair_half[1:] + after(pair_far, first_low).astype(F32)).astype(BF)
    grad_q = dot(hidden_one, query_grad, 0, 1).astype(BF)
    grad_kv_w = dot(hidden_one, grad_both, 0, 1).astype(BF)

    def owned(v, dim, *others):
        if dim:
            mine = core_halves(v, 0).astype(BF)
            part = lambda j: pick(mine, j, n_z, 1)
        else:
            mine = core_halves(v.reshape(n_z, v.shape[0] // n_z, v.shape[1]), 1).astype(BF)
            part = lambda j: lax.dynamic_index_in_dim(mine, j, 0, False)
        total = part(z).astype(F32)
        for s in range(1, n_z):
            total = total + after(shift(part((z + s) % n_z), "fsdp", n_z, s), *others).astype(F32)
        everyone = ring_gather(total.astype(BF)[None], "cx", n_cx, 0)
        return core_join(jnp.sum(everyone.astype(F32), axis=0).astype(BF), 0)

    grad_q = owned(grad_q, 0, first_low).astype(F32)
    grad_kv_w = owned(grad_kv_w, 0).astype(F32)
    grad_output = owned(grad_output, 1, first_low).astype(F32)

    valid_half = pick(valid, tp, 2, 0)
    out_half = (valid_half * (residual + after(mixture, grad_kv).astype(F32))).astype(BF)
    out_other = swap(out_half, "tp")
    layer_out = jnp.concatenate(
        [jnp.where(lead, out_half, out_other), jnp.where(lead, out_other, out_half)], axis=0
    )

    def ctx_sum_generic(v):
        kinds, a, b = v.shape[1:]
        total = ctx_total(v.reshape(-1, b), n_cx).reshape(v.shape).astype(F32)
        return [total[:, k] for k in range(kinds)]

    def ctx_sum_end(total):
        both = jnp.concatenate([swap(total, "cx"), total], axis=0)
        others = swap(both, "core")
        return place(
            jnp.stack(slots).astype(jnp.int32), [(others, 0), (others, 1), (both, 0), (both, 1)]
        )

    if by_ctx:
        (grad_down,) = ctx_sum_end(down_total)
        grad_gate, grad_up = ctx_sum_end(pair_total)
    else:
        (grad_down,) = ctx_sum_generic(grad_down)
        grad_gate, grad_up = ctx_sum_generic(grad_pair)

    small_grad = jnp.concatenate([grad_first, grad_second, grad_router], axis=0)
    small_grad = small_grad + swap(small_grad, "tp")
    small_grad = small_grad + swap(small_grad, "core")
    everyone = ring_gather(small_grad[None], "cx", n_cx, 0)
    total = jnp.sum(everyone, axis=0)
    small_mine = pick(total, z, n_z, 1)
    for s in range(1, n_z):
        small_mine = small_mine + shift(pick(total, (z + s) % n_z, n_z, 1), "fsdp", n_z, s)

    first_grad = first_low.astype(F32) + after(first_other, small_mine).astype(F32)
    grad_inputs = branch.astype(F32) + norm_backward(
        first_grad, gain_first, inverse_one, normed_one
    )

    return (
        layer_out[None],
        grad_inputs[None],
        small_mine[0],
        grad_q,
        grad_kv_w[:, :kv_width],
        grad_kv_w[:, kv_width:],
        grad_output,
        small_mine[1],
        small_mine[2:].T,
        grad_gate,
        grad_up,
        grad_down,
    )


def solution(mesh):
    n_z, n_ctx, n_tp = mesh.shape["fsdp"], mesh.shape["ctx"], mesh.shape["tp"]
    named = Mesh(
        mesh.devices.reshape(n_z, n_ctx // 2, 2, n_tp), ("fsdp", "cx", "core", "tp")
    )
    ctx = ("cx", "core")
    placed = (
        P("fsdp", ctx, None),
        P("fsdp"),
        P("fsdp", ctx, None),
        P("fsdp", ctx, None),
        P("fsdp", ctx, None),
        P("fsdp"),
        P("fsdp", "tp"),
        P("fsdp", "tp"),
        P("fsdp", "tp"),
        P("tp", "fsdp"),
        P("fsdp"),
        P("fsdp", None),
        P("fsdp", None, "tp"),
        P("fsdp", None, "tp"),
        P("fsdp", "tp", None),
    )
    return jax.shard_map(
        functools.partial(local, (n_z, n_ctx // 2)),
        mesh=named,
        in_specs=placed,
        out_specs=(
            P("fsdp", ctx, None),
            P("fsdp", ctx, None),
            P("fsdp"),
            P("fsdp", "tp"),
            P("fsdp", "tp"),
            P("fsdp", "tp"),
            P("tp", "fsdp"),
            P("fsdp"),
            P("fsdp", None),
            P("fsdp", None, "tp"),
            P("fsdp", None, "tp"),
            P("fsdp", "tp", None),
        ),
        check_vma=False,
    )
```

time: 835 us -> 669 us (0.80)
  Pallas kernels: 37.6 us -> 169 us
  matrix products: 132 us -> 17.7 us
  waiting for transfers between devices: 284 us -> 197 us
  local copies, waits for them, and re-layouts: 132 us -> 48 us
  between operations: 4 us -> 16.2 us
  starting transfers between devices: 162 us -> 150 us
  other arithmetic: 73 us -> 61.4 us
    pallas_call x0 -> x11, Pallas kernels: none -> 131 us  [the longest x4 78.9 us: experts(): pl.pallas_call(functools.partial(expert_kernel, aliased), name='experts',...]
    dot_general x29 -> x12, matrix products: 132 us -> 17.7 us  [dot(): lax.dot_general(a, b, (((ca,), (cb,)), ((), ())), preferred_element_type=...]
    ppermute x47 -> x36, waiting for transfers between devices: 198 us -> 124 us  [shift(): return lax.ppermute(v, axis, [(i, (i + by) % n) for i in range(n)])]
    ppermute x47 -> x34, starting transfers between devices: 63.7 us -> 33.7 us  [swap(): return lax.ppermute(v, axis, [(0, 1), (1, 0)])]
    unnamed x243 -> x123, local copies, waits for them, and re-layouts: 51.9 us -> 22.7 us
    dynamic_update_slice x6 -> x0, local copies, waits for them, and re-layouts: 26.6 us -> none  [the longest x3 13.6 us: local(): lax.dynamic_update_slice(both, swap(moving, 'core'), ((1 - core) * o_piec...]
    ppermute x47 -> x36, starting transfers between devices: 98 us -> 116 us  [shift(): return lax.ppermute(v, axis, [(i, (i + by) % n) for i in range(n)])]
    ppermute x47 -> x34, waiting for transfers between devices: 86.8 us -> 73.3 us  [swap(): return lax.ppermute(v, axis, [(0, 1), (1, 0)])]
  transfers between devices with their start and end apart: 94 -> 72, of which waited for: 33 -> 20; matrix products, arithmetic and copies ran while one was open for 38% -> 15% of each run, Pallas kernels for 5% -> 25%
where the time goes in v2:
time: 669 us; the launch traced here: 660 us
  waiting for transfers between devices  197 us (29%)
  Pallas kernels  169 us (25%)
  starting transfers between devices  150 us (22%)
  other arithmetic  61.4 us (9%)
  local copies, waits for them, and re-layouts  48 us (7%)
  matrix products  17.7 us (3%)
  between operations  16.2 us (2%)
    ppermute x36, waiting for transfers between devices, shift(): return lax.ppermute(v, axis, [(i, (i + by) % n) for i in range(n)])  124 us
    ppermute x36, starting transfers between devices, shift(): return lax.ppermute(v, axis, [(i, (i + by) % n) for i in range(n)])  116 us
    pallas_call x4, Pallas kernels, experts(): pl.pallas_call(functools.partial(expert_kernel, aliased), name='experts',...  78.9 us
    ppermute x34, waiting for transfers between devices, swap(): return lax.ppermute(v, axis, [(0, 1), (1, 0)])  73.3 us
    ppermute x34, starting transfers between devices, swap(): return lax.ppermute(v, axis, [(0, 1), (1, 0)])  33.7 us
    unnamed x123, local copies, waits for them, and re-layouts  22.7 us
    pallas_call x1, Pallas kernels, weight_grads(): pl.pallas_call(functools.partial(weight_grad_kernel, len(chunks)), name='...  21.8 us
    pallas_call x1, Pallas kernels, attend_back(): pl.pallas_call(functools.partial(attend_back_kernel, group), name='attend...  20 us
  transfers between devices with their start and end apart: 72, of which 20 were waited for; matrix products, arithmetic and copies ran while one was open for 15% of the time, Pallas kernels for 25%

profile of v2, /device:TPU:1, one launch (start us, length us, event | category | flops | bytes accessed | tf_op | source)
XLA Modules:
  0.0 659.8 jit_solution(3301331715893745999)
XLA Ops:
  23.7 9.2 %collective-permute-done.1 = bf16[192,512]{1,0:T(8,128)(2,1)S(1)} collective-permute-done((bf16[192,512]{1,0:T(8,128)(2,1)S(1)}, bf16[192,512]{1,0:T(8,128)(2,1)S(1)}, u32[]{:S(2)}, u32[]{:S(2)}) %collective-permute-start.1) | collective-permute-done | bytes 196640 | tf_op jit(solution)/shard_map/ppermute | solution.py:28
  55.0 11.0 %collective-permute-done.9 = bf16[192,768]{1,0:T(8,128)(2,1)S(1)} collective-permute-done((bf16[192,768]{1,0:T(8,128)(2,1)}, bf16[192,768]{1,0:T(8,128)(2,1)S(1)}, u32[]{:S(2)}, u32[]{:S(2)}) %collective-permute-start.9) | collective-permute-done | bytes 294944 | tf_op jit(solution)/shard_map/ppermute | solution.py:28
  91.2 9.3 %attend.2 = (bf16[384,512]{1,0:T(8,128)(2,1)S(1)}, f32[2,8,512]{2,1,0:T(8,128)S(1)}) custom-call(s32[4]{0:T(128)S(1)} %pad_add_fusion.info_ref, bf16[768,512]{1,0:T(8,128)(2,1)S(1)} %get-tuple-element.101.q_ref, bf16[4,2,256,512]{3,2,1,0:T(8,128)(2,1)S(1)} %pad_maximum_fusion.1.kv_ref), custom_call_target="tpu_custom_call" | custom-call | flops 1610612736 | bytes 1835008 | tf_op jit(solution)/shard_map/attend/pallas_call | solution.py:261
  100.6 13.9 %collective-permute-done.15 = bf16[192,768]{1,0:T(8,128)(2,1)S(1)} collective-permute-done((bf16[192,768]{1,0:T(8,128)(2,1)S(1)}, bf16[192,768]{1,0:T(8,128)(2,1)S(1)}, u32[]{:S(2)}, u32[]{:S(2)}) %collective-permute-start.15) | collective-permute-done | bytes 294944 | tf_op jit(solution)/shard_map/ppermute | solution.py:28
  118.6 9.2 %attend.3 = (bf16[384,512]{1,0:T(8,128)(2,1)S(1)}, f32[2,8,512]{2,1,0:T(8,128)S(1)}) custom-call(s32[4]{0:T(128)S(1)} %pad_add_fusion.info_ref, bf16[768,512]{1,0:T(8,128)(2,1)S(1)} %copy-done.18, bf16[4,2,256,512]{3,2,1,0:T(8,128)(2,1)S(1)} %copy-done.5), custom_call_target="tpu_custom_call" | custom-call | flops 1610612736 | bytes 1835008 | tf_op jit(solution)/shard_map/attend/pallas_call | solution.py:261
  135.4 29.5 %collective-permute-done.18 = bf16[256,1536]{1,0:T(8,128)(2,1)} collective-permute-done((bf16[256,1536]{1,0:T(8,128)(2,1)}, bf16[256,1536]{1,0:T(8,128)(2,1)}, u32[]{:S(2)}, u32[]{:S(2)}) %collective-permute-start.18) | collective-permute-done | bytes 786464 | tf_op jit(solution)/shard_map/ppermute | solution.py:32
  172.6 21.6 %collective-permute-start.19 = (bf16[256,1664]{1,0:T(8,128)(2,1)}, bf16[256,1664]{1,0:T(8,128)(2,1)}, u32[]{:S(2)}, u32[]{:S(2)}) collective-permute-start(bf16[256,1664]{1,0:T(8,128)(2,1)} %concatenate.58.near_in.refs_0_), channel_id=1, source_target_pairs={{0,8},{8,16},{16,24},{24,0},{1,9},{9,17},{17,25},{25,1},{2,10},{10... | collective-permute-start | bytes 2555912 | tf_op jit(solution)/shard_map/ppermute | solution.py:28
  199.5 22.4 %collective-permute-done.19.near_in.refs_2_ = bf16[256,1664]{1,0:T(8,128)(2,1)} collective-permute-done((bf16[256,1664]{1,0:T(8,128)(2,1)}, bf16[256,1664]{1,0:T(8,128)(2,1)}, u32[]{:S(2)}, u32[]{:S(2)}) %collective-permute-start.19) | collective-permute-done | bytes 852000 | tf_op jit(solution)/shard_map/ppermute | solution.py:28
  222.2 19.7 %experts.4 = (bf16[256,1664]{1,0:T(8,128)(2,1)}, bf16[256,1664]{1,0:T(8,128)(2,1)}, bf16[4,2,256,1536]{3,2,1,0:T(8,128)(2,1)}, bf16[512,1024]{1,0:T(8,128)(2,1)}...) custom-call(s32[6]{0:T(128)} %stack.172.info_ref, bf16[256,1664]{1,0:T(8,128)(2,1)} %concatenate.58.near_in.refs_0_, ...), custom_call_target="tpu_custom_call" | custom-call | flops 9663676416 | bytes 22020096 | tf_op jit(solution)/shard_map/experts/pallas_call | solution.py:451
  246.8 19.5 %experts.5 = (bf16[256,1664]{1,0:T(8,128)(2,1)}, bf16[256,1664]{1,0:T(8,128)(2,1)}, bf16[4,2,256,1536]{3,2,1,0:T(8,128)(2,1)}, bf16[512,1024]{1,0:T(8,128)(2,1)}...) custom-call(s32[6]{0:T(128)} %stack.174.info_ref, ...), custom_call_target="tpu_custom_call", output_to_operand_aliasing={{2}: (8, {})} | custom-call | flops 9663676416 | bytes 22020096 | tf_op jit(solution)/shard_map/experts/pallas_call | solution.py:451
  270.0 19.6 %experts.6 = (bf16[256,1664]{1,0:T(8,128)(2,1)}, bf16[256,1664]{1,0:T(8,128)(2,1)}, bf16[4,2,256,1536]{3,2,1,0:T(8,128)(2,1)}, bf16[512,1024]{1,0:T(8,128)(2,1)}...) custom-call(s32[6]{0:T(128)} %stack.176.info_ref, ...), custom_call_target="tpu_custom_call", output_to_operand_aliasing={{2}: (8, {})} | custom-call | flops 9663676416 | bytes 22020096 | tf_op jit(solution)/shard_map/experts/pallas_call | solution.py:451
  290.0 16.0 %collective-permute-done.24 = bf16[256,1664]{1,0:T(8,128)(2,1)S(1)} collective-permute-done((bf16[256,1664]{1,0:T(8,128)(2,1)}, bf16[256,1664]{1,0:T(8,128)(2,1)S(1)}, u32[]{:S(2)}, u32[]{:S(2)}) %collective-permute-start.24) | collective-permute-done | bytes 852000 | tf_op jit(solution)/shard_map/ppermute | solution.py:32
  306.3 20.1 %experts.7 = (bf16[256,1664]{1,0:T(8,128)(2,1)}, bf16[256,1664]{1,0:T(8,128)(2,1)}, bf16[4,2,256,1536]{3,2,1,0:T(8,128)(2,1)}, bf16[512,1024]{1,0:T(8,128)(2,1)}...) custom-call(s32[6]{0:T(128)} %stack.170.info_ref, ...), custom_call_target="tpu_custom_call", output_to_operand_aliasing={{2}: (8, {})} | custom-call | flops 9663676416 | bytes 22020096 | tf_op jit(solution)/shard_map/experts/pallas_call | solution.py:451
  329.8 21.8 %weight_grads.1 = bf16[4,2,1536,256]{3,2,1,0:T(8,128)(2,1)} custom-call(s32[9]{0:T(128)} %stack.181.info_ref, bf16[256,1664]{1,0:T(8,128)(2,1)} %concatenate.58.near_in.refs_0_, bf16[256,1664]{1,0:T(8,128)(2,1)} %collective-permute-done.21.far_in.refs_1_, bf16[256,1664]{1,0:T(8,128)(2,1)} %collective-permute-done.19.near_in.refs_2_, ...), custom_call_target="tpu_custom_call" | custom-call | flops 12884901888 | bytes 20971520 | tf_op jit(solution)/shard_map/weight_grads/pallas_call | solution.py:528
  361.6 12.5 %down_grads.1 = bf16[4,256,1536]{2,1,0:T(8,128)(2,1)} custom-call(s32[9]{0:T(128)} %stack.181.info_ref, bf16[2,4,256,1536]{3,2,1,0:T(8,128)(2,1)} %bitcast.170, bf16[2,4,256,1536]{3,2,1,0:T(8,128)(2,1)} %bitcast.171, bf16[2,4,256,1536]{3,2,1,0:T(8,128)(2,1)} %bitcast.172, bf16[2,4,256,1536]{3,2,1,0:T(8,128)(2,1)} %bitcast.173, ...), custom_call_target="tpu_custom_call" | custom-call | flops 6442450944 | bytes 10485760 | tf_op jit(solution)/shard_map/down_grads/pallas_call | solution.py:573
  379.2 17.9 %collective-permute-done.33 = bf16[256,1664]{1,0:T(8,128)(2,1)} collective-permute-done((bf16[256,1664]{1,0:T(8,128)(2,1)}, bf16[256,1664]{1,0:T(8,128)(2,1)}, u32[]{:S(2)}, u32[]{:S(2)}) %collective-permute-start.33) | collective-permute-done | bytes 852000 | tf_op jit(solution)/shard_map/ppermute | solution.py:32
  419.8 7.2 %collective-permute-done.34 = bf16[256,1536]{1,0:T(8,128)(2,1)} collective-permute-done((bf16[256,1536]{1,0:T(8,128)(2,1)}, bf16[256,1536]{1,0:T(8,128)(2,1)}, u32[]{:S(2)}, u32[]{:S(2)}) %collective-permute-start.34) | collective-permute-done | bytes 786464 | tf_op jit(solution)/shard_map/ppermute | solution.py:32
  431.5 20.0 %attend_back.1 = (f32[768,512]{1,0:T(8,128)S(1)}, bf16[4,2,256,512]{3,2,1,0:T(8,128)(2,1)S(1)}) custom-call(s32[4]{0:T(128)S(1)} %pad_add_fusion.info_ref, bf16[768,512]{1,0:T(8,128)(2,1)S(1)} %copy-done.19, bf16[4,2,256,512]{3,2,1,0:T(8,128)(2,1)} %copy-done.4, bf16[768,512]{1,0:T(8,128)(2,1)S(1)} %copy-done.10, ...), custom_call_target="tpu_custom_call" | custom-call | flops 8053063680 | bytes 8126464 | tf_op jit(solution)/shard_map/attend_back/pallas_call | solution.py:339
  456.2 15.6 %collective-permute-start.38 = (bf16[2,256,512]{2,1,0:T(8,128)(2,1)S(1)}, bf16[2,256,512]{2,1,0:T(8,128)(2,1)S(1)}, u32[]{:S(2)}, u32[]{:S(2)}) collective-permute-start(bf16[2,256,512]{2,1,0:T(8,128)(2,1)S(1)} %fusion.34), channel_id=1, source_target_pairs={{0,4},{4,0},{1,5},{5,1},{2,6},{6,2},{3,7},{7,3},{8,12},{12,8},{9,1... | collective-permute-start | bytes 1572872 | tf_op jit(solution)/shard_map/ppermute | solution.py:28
  472.4 8.5 %collective-permute-start.60 = (bf16[384,384]{1,0:T(8,128)(2,1)S(1)}, bf16[384,384]{1,0:T(8,128)(2,1)S(1)}, u32[]{:S(2)}, u32[]{:S(2)}) collective-permute-start(bf16[384,384]{1,0:T(8,128)(2,1)S(1)} %get-tuple-element.205), channel_id=1, source_target_pairs={{0,16},{8,24},{16,0},{24,8},{1,17},{9,25},{17,1},{25,9},{2,18},{10... | collective-permute-start | bytes 884744 | tf_op jit(solution)/shard_map/ppermute | solution.py:28
  484.1 7.9 %collective-permute-start.61 = (bf16[384,384]{1,0:T(8,128)(2,1)S(1)}, bf16[384,384]{1,0:T(8,128)(2,1)S(1)}, u32[]{:S(2)}, u32[]{:S(2)}) collective-permute-start(bf16[384,384]{1,0:T(8,128)(2,1)S(1)} %get-tuple-element.204), channel_id=1, source_target_pairs={{0,24},{8,0},{16,8},{24,16},{1,25},{9,1},{17,9},{25,17},{2,26},{10... | collective-permute-start | bytes 884744 | tf_op jit(solution)/shard_map/ppermute | solution.py:28
  508.3 35.4 %collective-permute-done.48 = bf16[192,768]{1,0:T(8,128)(2,1)S(1)} collective-permute-done((bf16[192,768]{1,0:T(8,128)(2,1)S(1)}, bf16[192,768]{1,0:T(8,128)(2,1)S(1)}, u32[]{:S(2)}, u32[]{:S(2)}) %collective-permute-start.48) | collective-permute-done | bytes 294944 | tf_op jit(solution)/shard_map/ppermute | solution.py:28
  560.6 16.4 %collective-permute-start.43 = (f32[18,384]{1,0:T(8,128)S(1)}, f32[18,384]{1,0:T(8,128)S(1)}, u32[]{:S(2)}, u32[]{:S(2)}) collective-permute-start(f32[18,384]{1,0:T(8,128)S(1)} %get-tuple-element.222), channel_id=1, source_target_pairs={{0,8},{8,16},{16,24},{24,0},{1,9},{9,17},{17,25},{25,1},{2,10},{10... | collective-permute-start | bytes 82952 | tf_op jit(solution)/shard_map/ppermute | solution.py:28
  641.6 8.2 %place.2 = (f32[4,1536,256]{2,1,0:T(8,128)}, f32[4,1536,256]{2,1,0:T(8,128)}) custom-call(s32[4]{0:T(128)S(1)} %pad_add_fusion.2.info_ref, bf16[2,2,1536,256]{3,2,1,0:T(8,128)(2,1)} %collective-permute-done.66.refs_0_.refs_1_, bf16[2,2,1536,256]{3,2,1,0:T(8,128)(2,1)} %collective-permute-done.66.refs_0_.refs_1_, ...), custom_call_target="tpu_custom_call" | custom-call | bytes 18874368 | tf_op jit(solution)/shard_map/place/pallas_call | solution.py:605
  (405 shorter events, 251.2 us)
Async XLA Ops:
  7.2 239.7 %all-gather.3.cloned.1.call-start = ((), (), s32[]{:S(2)}) async-start(), calls=%async_computation.2 | async-start | bytes 7077888 | tf_op jit(solution)/shard_map/all_gather | solution.py:707
  68.1 562.0 %reduce-scatter.2.cloned.1.call-start = ((), (), s32[]{:S(2)}) async-start(), calls=%async_computation.1 | async-start | bytes 7077888 | tf_op jit(solution)/shard_map/reduce_scatter | solution.py:819
  72.1 28.5 %collective-permute-start.14 = (bf16[192,768]{1,0:T(8,128)(2,1)S(1)}, bf16[192,768]{1,0:T(8,128)(2,1)S(1)}, u32[]{:S(2)}, u32[]{:S(2)}) collective-permute-start(bf16[192,768]{1,0:T(8,128)(2,1)S(1)} %constant_dynamic-slice_fusion.9), channel_id=1, source_target_pairs={{0,8},{8,16},{16,24},{24,0},{1,9},{9,17},{17,25},{25,1},{2,10},{10... | collective-permute-start | bytes 884744 | tf_op jit(solution)/shard_map/ppermute | solution.py:28
  78.8 35.7 %collective-permute-start.15 = (bf16[192,768]{1,0:T(8,128)(2,1)S(1)}, bf16[192,768]{1,0:T(8,128)(2,1)S(1)}, u32[]{:S(2)}, u32[]{:S(2)}) collective-permute-start(bf16[192,768]{1,0:T(8,128)(2,1)S(1)} %constant_dynamic-slice_fusion.9), channel_id=1, source_target_pairs={{0,16},{8,24},{16,0},{24,8},{1,17},{9,25},{17,1},{25,9},{2,18},{10... | collective-permute-start | bytes 884744 | tf_op jit(solution)/shard_map/ppermute | solution.py:28
  81.1 33.4 %collective-permute-start.16 = (bf16[192,768]{1,0:T(8,128)(2,1)S(1)}, bf16[192,768]{1,0:T(8,128)(2,1)S(1)}, u32[]{:S(2)}, u32[]{:S(2)}) collective-permute-start(bf16[192,768]{1,0:T(8,128)(2,1)S(1)} %constant_dynamic-slice_fusion.9), channel_id=1, source_target_pairs={{0,24},{8,0},{16,8},{24,16},{1,25},{9,1},{17,9},{25,17},{2,26},{10... | collective-permute-start | bytes 884744 | tf_op jit(solution)/shard_map/ppermute | solution.py:28
  132.8 32.1 %collective-permute-start.18 = (bf16[256,1536]{1,0:T(8,128)(2,1)}, bf16[256,1536]{1,0:T(8,128)(2,1)}, u32[]{:S(2)}, u32[]{:S(2)}) collective-permute-start(bf16[256,1536]{1,0:T(8,128)(2,1)} %convolution_convert_fusion.3), channel_id=1, source_target_pairs={{0,1},{1,0},{2,3},{3,2},{4,5},{5,4},{6,7},{7,6},{8,9},{9,8},{10,11... | collective-permute-start | bytes 2359304 | tf_op jit(solution)/shard_map/ppermute | solution.py:32
  172.6 49.3 %collective-permute-start.19 = (bf16[256,1664]{1,0:T(8,128)(2,1)}, bf16[256,1664]{1,0:T(8,128)(2,1)}, u32[]{:S(2)}, u32[]{:S(2)}) collective-permute-start(bf16[256,1664]{1,0:T(8,128)(2,1)} %concatenate.58.near_in.refs_0_), channel_id=1, source_target_pairs={{0,8},{8,16},{16,24},{24,0},{1,9},{9,17},{17,25},{25,1},{2,10},{10... | collective-permute-start | bytes 2555912 | tf_op jit(solution)/shard_map/ppermute | solution.py:28
  194.1 28.1 %collective-permute-start.21 = (bf16[256,1664]{1,0:T(8,128)(2,1)}, bf16[256,1664]{1,0:T(8,128)(2,1)}, u32[]{:S(2)}, u32[]{:S(2)}) collective-permute-start(bf16[256,1664]{1,0:T(8,128)(2,1)} %concatenate.58.near_in.refs_0_), channel_id=1, source_target_pairs={{0,1},{1,0},{2,3},{3,2},{4,5},{5,4},{6,7},{7,6},{8,9},{9,8},{10,11... | collective-permute-start | bytes 2555912 | tf_op jit(solution)/shard_map/ppermute | solution.py:32
  268.6 37.8 %collective-permute-start.25 = (bf16[256,1664]{1,0:T(8,128)(2,1)}, bf16[256,1664]{1,0:T(8,128)(2,1)}, u32[]{:S(2)}, u32[]{:S(2)}) collective-permute-start(bf16[256,1664]{1,0:T(8,128)(2,1)} %collective-permute-done.22.near_in.refs_6_), channel_id=1, source_target_pairs={{0,1},{1,0},{2,3},{3,2},{4,5},{5,4},{6,7},{7,6},{8,9},{9,8},{10,11... | collective-permute-start | bytes 2555912 | tf_op jit(solution)/shard_map/ppermute | solution.py:32
  268.9 37.2 %collective-permute-start.24 = (bf16[256,1664]{1,0:T(8,128)(2,1)}, bf16[256,1664]{1,0:T(8,128)(2,1)S(1)}, u32[]{:S(2)}, u32[]{:S(2)}) collective-permute-start(bf16[256,1664]{1,0:T(8,128)(2,1)} %get-tuple-element.118), channel_id=1, source_target_pairs={{0,1},{1,0},{2,3},{3,2},{4,5},{5,4},{6,7},{7,6},{8,9},{9,8},{10,11... | collective-permute-start | bytes 2555912 | tf_op jit(solution)/shard_map/ppermute | solution.py:32
  289.7 37.2 %collective-permute-start.28 = (bf16[256,1664]{1,0:T(8,128)(2,1)}, bf16[256,1664]{1,0:T(8,128)(2,1)S(1)}, u32[]{:S(2)}, u32[]{:S(2)}) collective-permute-start(bf16[256,1664]{1,0:T(8,128)(2,1)} %get-tuple-element.125), channel_id=1, source_target_pairs={{0,1},{1,0},{2,3},{3,2},{4,5},{5,4},{6,7},{7,6},{8,9},{9,8},{10,11... | collective-permute-start | bytes 2555912 | tf_op jit(solution)/shard_map/ppermute | solution.py:32
  326.4 29.0 %collective-permute-start.30 = (bf16[256,1664]{1,0:T(8,128)(2,1)}, bf16[256,1664]{1,0:T(8,128)(2,1)S(1)}, u32[]{:S(2)}, u32[]{:S(2)}) collective-permute-start(bf16[256,1664]{1,0:T(8,128)(2,1)} %get-tuple-element.127), channel_id=1, source_target_pairs={{0,1},{1,0},{2,3},{3,2},{4,5},{5,4},{6,7},{7,6},{8,9},{9,8},{10,11... | collective-permute-start | bytes 2555912 | tf_op jit(solution)/shard_map/ppermute | solution.py:32
  329.2 31.2 %collective-permute-start.29 = (bf16[256,1664]{1,0:T(8,128)(2,1)S(1)}, bf16[256,1664]{1,0:T(8,128)(2,1)S(1)}, u32[]{:S(2)}, u32[]{:S(2)}) collective-permute-start(bf16[256,1664]{1,0:T(8,128)(2,1)S(1)} %add_convert_fusion.3), channel_id=1, source_target_pairs={{0,8},{8,16},{16,24},{24,0},{1,9},{9,17},{17,25},{25,1},{2,10},{10... | collective-permute-start | bytes 2555912 | tf_op jit(solution)/shard_map/ppermute | solution.py:28
  355.4 43.2 %collective-permute-start.32 = (bf16[2,2,1536,256]{3,2,1,0:T(8,128)(2,1)}, bf16[2,2,1536,256]{3,2,1,0:T(8,128)(2,1)}, u32[]{:S(2)}, u32[]{:S(2)}) collective-permute-start(bf16[2,2,1536,256]{3,2,1,0:T(8,128)(2,1)} %slice.135), channel_id=1, source_target_pairs={{0,2},{2,0},{1,3},{3,1},{4,6},{6,4},{5,7},{7,5},{8,10},{10,8},{9,1... | collective-permute-start | bytes 9437192 | tf_op jit(solution)/shard_map/ppermute | solution.py:32
  414.3 84.0 %collective-permute-start.67 = (bf16[1,1,256,1536]{3,2,1,0:T(8,128)(2,1)}, bf16[1,1,256,1536]{3,2,1,0:T(8,128)(2,1)}, u32[]{:S(2)}, u32[]{:S(2)}) collective-permute-start(bf16[1,1,256,1536]{3,2,1,0:T(8,128)(2,1)} %slice.212), channel_id=1, source_target_pairs={{0,4},{4,0},{1,5},{5,1},{2,6},{6,2},{3,7},{7,3},{8,12},{12,8},{9,1... | collective-permute-start | bytes 2359304 | tf_op jit(solution)/shard_map/ppermute | solution.py:32
  418.2 80.1 %collective-permute-start.64 = (bf16[1,2,1536,256]{3,2,1,0:T(8,128)(2,1)}, bf16[1,2,1536,256]{3,2,1,0:T(8,128)(2,1)}, u32[]{:S(2)}, u32[]{:S(2)}) collective-permute-start(bf16[1,2,1536,256]{3,2,1,0:T(8,128)(2,1)} %slice.211), channel_id=1, source_target_pairs={{0,4},{4,0},{1,5},{5,1},{2,6},{6,2},{3,7},{7,3},{8,12},{12,8},{9,1... | collective-permute-start | bytes 4718600 | tf_op jit(solution)/shard_map/ppermute | solution.py:32
  472.4 31.3 %collective-permute-start.60 = (bf16[384,384]{1,0:T(8,128)(2,1)S(1)}, bf16[384,384]{1,0:T(8,128)(2,1)S(1)}, u32[]{:S(2)}, u32[]{:S(2)}) collective-permute-start(bf16[384,384]{1,0:T(8,128)(2,1)S(1)} %get-tuple-element.205), channel_id=1, source_target_pairs={{0,16},{8,24},{16,0},{24,8},{1,17},{9,25},{17,1},{25,9},{2,18},{10... | collective-permute-start | bytes 884744 | tf_op jit(solution)/shard_map/ppermute | solution.py:28
  498.3 45.4 %collective-permute-start.48 = (bf16[192,768]{1,0:T(8,128)(2,1)S(1)}, bf16[192,768]{1,0:T(8,128)(2,1)S(1)}, u32[]{:S(2)}, u32[]{:S(2)}) collective-permute-start(bf16[192,768]{1,0:T(8,128)(2,1)S(1)} %get-tuple-element.208), channel_id=1, source_target_pairs={{0,16},{8,24},{16,0},{24,8},{1,17},{9,25},{17,1},{25,9},{2,18},{10... | collective-permute-start | bytes 884744 | tf_op jit(solution)/shard_map/ppermute | solution.py:28
  498.6 45.1 %collective-permute-start.49 = (bf16[192,768]{1,0:T(8,128)(2,1)S(1)}, bf16[192,768]{1,0:T(8,128)(2,1)S(1)}, u32[]{:S(2)}, u32[]{:S(2)}) collective-permute-start(bf16[192,768]{1,0:T(8,128)(2,1)S(1)} %get-tuple-element.207), channel_id=1, source_target_pairs={{0,24},{8,0},{16,8},{24,16},{1,25},{9,1},{17,9},{25,17},{2,26},{10... | collective-permute-start | bytes 884744 | tf_op jit(solution)/shard_map/ppermute | solution.py:28
  503.7 123.0 %collective-permute-start.39 = (bf16[512,1536]{1,0:T(8,128)(2,1)}, bf16[512,1536]{1,0:T(8,128)(2,1)}, u32[]{:S(2)}, u32[]{:S(2)}) collective-permute-start(bf16[512,1536]{1,0:T(8,128)(2,1)} %get-tuple-element.196), channel_id=1, source_target_pairs={{0,1},{1,0},{2,3},{3,2},{4,5},{5,4},{6,7},{7,6},{8,9},{9,8},{10,11... | collective-permute-start | bytes 4718600 | tf_op jit(solution)/shard_map/ppermute | solution.py:32
  505.1 103.7 %collective-permute-start.65 = (bf16[1,2,1536,256]{3,2,1,0:T(8,128)(2,1)S(1)}, bf16[1,2,1536,256]{3,2,1,0:T(8,128)(2,1)}, u32[]{:S(2)}, u32[]{:S(2)}) collective-permute-start(bf16[1,2,1536,256]{3,2,1,0:T(8,128)(2,1)S(1)} %fusion.18), channel_id=1, source_target_pairs={{0,4},{4,0},{1,5},{5,1},{2,6},{6,2},{3,7},{7,3},{8,12},{12,8},{9,1... | collective-permute-start | bytes 4718600 | tf_op jit(solution)/shard_map/ppermute | solution.py:32
  507.9 48.2 %collective-permute-start.62 = (bf16[1,384,384]{2,1,0:T(8,128)(2,1)S(1)}, bf16[1,384,384]{2,1,0:T(8,128)(2,1)S(1)}, u32[]{:S(2)}, u32[]{:S(2)}) collective-permute-start(bf16[1,384,384]{2,1,0:T(8,128)(2,1)S(1)} %get-tuple-element.181), channel_id=1, source_target_pairs={{0,4},{4,0},{1,5},{5,1},{2,6},{6,2},{3,7},{7,3},{8,12},{12,8},{9,1... | collective-permute-start | bytes 884744 | tf_op jit(solution)/shard_map/ppermute | solution.py:28
  548.7 28.3 %collective-permute-start.50 = (bf16[1,192,768]{2,1,0:T(8,128)(2,1)S(1)}, bf16[1,192,768]{2,1,0:T(8,128)(2,1)S(1)}, u32[]{:S(2)}, u32[]{:S(2)}) collective-permute-start(bf16[1,192,768]{2,1,0:T(8,128)(2,1)S(1)} %get-tuple-element.185), channel_id=1, source_target_pairs={{0,4},{4,0},{1,5},{5,1},{2,6},{6,2},{3,7},{7,3},{8,12},{12,8},{9,1... | collective-permute-start | bytes 884744 | tf_op jit(solution)/shard_map/ppermute | solution.py:28
  612.1 29.5 %collective-permute-start.66 = (bf16[2,2,1536,256]{3,2,1,0:T(8,128)(2,1)}, bf16[2,2,1536,256]{3,2,1,0:T(8,128)(2,1)}, u32[]{:S(2)}, u32[]{:S(2)}) collective-permute-start(bf16[2,2,1536,256]{3,2,1,0:T(8,128)(2,1)} %pad_maximum_fusion.refs_2_.refs_3_), channel_id=1, source_target_pairs={{0,2},{2,0},{1,3},{3,1},{4,6},{6,4},{5,7},{7,5},{8,10},{10,8},{9,1... | collective-permute-start | bytes 9437192 | tf_op jit(solution)/shard_map/ppermute | solution.py:32
  (108 other events, 1189.2 us)
Sparse Core Ops, SparseCore 0:
  68.2 154.9 all-gather.2
  418.4 137.6 reduce-scatter.1

commit v3 on v2

--- a/solution.py
+++ b/solution.py
@@ -43,6 +43,20 @@
 
 def after(v, *others):
     return lax.optimization_barrier((v,) + others)[0]
+
+
+def anchor_kernel(in_ref, out_ref):
+    out_ref[...] = in_ref[...]
+
+
+def anchor(*others):
+    token = after(jnp.zeros((8, 128), F32), *others)
+    return pl.pallas_call(
+        anchor_kernel,
+        name="anchor",
+        out_shape=jax.ShapeDtypeStruct((8, 128), F32),
+        cost_estimate=pl.CostEstimate(flops=10**11, transcendentals=0, bytes_accessed=8192),
+    )(token)
 
 
 def direct_reduce(part, axis, n):
@@ -139,17 +153,19 @@
 
 
 def assemble(info_ref, own_ref, got_ref, other_ref, full_ref):
-    z, core = info_ref[0], info_ref[1]
+    z, core, cx = info_ref[0], info_ref[1], info_ref[2]
     rows = own_ref.shape[0]
-    piece = rows // 2
-    n_z = got_ref.shape[0] + 1
+    chips, steps, piece, _ = got_ref.shape
+    n_z = steps + 1
     full_ref[pl.ds(pl.multiple_of(z * rows, piece), rows), :] = own_ref[...]
-    for s in range(1, n_z):
-        start = ((z + n_z - s) % n_z) * rows
-        mine = pl.multiple_of(start + core * piece, piece)
-        theirs = pl.multiple_of(start + (1 - core) * piece, piece)
-        full_ref[pl.ds(mine, piece), :] = got_ref[s - 1]
-        full_ref[pl.ds(theirs, piece), :] = other_ref[s - 1]
+    for k in range(chips):
+        chip = (cx + chips - k) % chips
+        for s in range(1, n_z):
+            start = ((z + n_z - s) % n_z) * rows + chip * 2 * piece
+            mine = pl.multiple_of(start + core * piece, piece)
+            theirs = pl.multiple_of(start + (1 - core) * piece, piece)
+            full_ref[pl.ds(mine, piece), :] = got_ref[k, s - 1]
+            full_ref[pl.ds(theirs, piece), :] = other_ref[k, s - 1]
 
 
 def project_kernel(turned, scale, info_ref, own_ref, got_ref, other_ref, x_ref, cos_ref, sin_ref, out_ref, full_ref):
@@ -194,7 +210,7 @@
 
 def assembled(info, own, got, other):
     rows, columns = own.shape
-    full = (rows * (got.shape[0] + 1), columns)
+    full = (rows * (got.shape[1] + 1), columns)
     return pl.pallas_call(
         assemble,
         name="assembled",
@@ -364,9 +380,7 @@
     )(info, q, kv, o, do, lse)
 
 
-def expert_kernel(aliased, info_ref, near_in, far_in, near_do, far_do, gate_ref, up_ref, down_ref, *refs):
-    if aliased:
-        refs = refs[1:]
+def expert_kernel(info_ref, near_in, far_in, near_do, far_do, gate_ref, up_ref, down_ref, *refs):
     near_out, far_out, mix_out, act_out, dg_out, du_out = refs[:6]
     rows_x, rows_do, shares_in, mix_sum, back_sum, shares_out = refs[6:]
     e = pl.program_id(0)
@@ -431,12 +445,10 @@
         near_out[:, width:] = shares_out[:half, :].astype(BF)
         far_out[:, :width] = back_sum[half:, :].astype(BF)
         far_out[:, width:] = shares_out[half:, :].astype(BF)
-        tp = info_ref[1]
-        mix_out[0, tp] = mix_sum[:half, :].astype(BF)
-        mix_out[0, 1 - tp] = mix_sum[half:, :].astype(BF)
-
-
-def experts(info, near, far, do_near, do_far, n_z, gate, up, down, mix_all):
+        mix_out[...] = mix_sum[...].astype(BF)
+
+
+def experts(info, near, far, do_near, do_far, gate, up, down, weight):
     half, wide = near.shape
     width = do_near.shape[3]
     held, _, hidden = gate.shape
@@ -447,9 +459,8 @@
     column = pl.BlockSpec((rows, per * hidden), lambda e, i: (0, e))
     mid = jax.ShapeDtypeStruct((rows, held * hidden), BF)
     message = jax.ShapeDtypeStruct((half, wide), BF)
-    aliased = mix_all is not None
     return pl.pallas_call(
-        functools.partial(expert_kernel, aliased),
+        expert_kernel,
         name="experts",
         grid_spec=pltpu.PrefetchScalarGridSpec(
             num_scalar_prefetch=1,
@@ -462,12 +473,11 @@
                 each((width, hidden)),
                 each((width, hidden)),
                 each((hidden, width)),
-            ]
-            + [pl.BlockSpec(memory_space=pl.ANY)] * aliased,
+            ],
             out_specs=[
                 whole((half, wide)),
                 whole((half, wide)),
-                pl.BlockSpec((1, 2, half, width), lambda e, i: (i[2], 0, 0, 0)),
+                whole((rows, width)),
                 column,
                 column,
                 column,
@@ -484,139 +494,125 @@
         out_shape=[
             message,
             message,
-            jax.ShapeDtypeStruct((n_z, 2, half, width), BF),
+            jax.ShapeDtypeStruct((rows, width), BF),
             mid,
             mid,
             mid,
         ],
-        input_output_aliases={8: 2} if aliased else {},
         compiler_params=pltpu.CompilerParams(vmem_limit_bytes=56 << 20),
         cost_estimate=pl.CostEstimate(
-            flops=12 * rows * width * held * hidden,
+            flops=12 * weight * rows * width * held * hidden,
             transcendentals=rows * held * hidden,
             bytes_accessed=6 * held * hidden * width + 16 * rows * width,
         ),
-    )(info, near, far, do_near, do_far, gate, up, down, *([mix_all] if aliased else []))
-
-
-def weight_grad_kernel(count, info_ref, *refs):
-    lefts = refs[:count]
-    rights = refs[count:-2]
-    out, turned = refs[-2:]
-    size = lefts[0].shape[0]
-
-    @pl.when(pl.program_id(0) == 0)
-    def _():
-        for i, left in enumerate(lefts):
-            turned[:, i * size : (i + 1) * size] = left[:, : turned.shape[0]].T
-
-    half = len(rights) // 2
-    for i, blocks in enumerate((rights[:half], rights[half:])):
-        out[0, i] = jnp.dot(
-            turned[...],
-            jnp.concatenate([block[...] for block in blocks], axis=0),
-            preferred_element_type=F32,
-        ).astype(BF)
-
-
-def weight_grads(info, chunks, firsts, seconds, held, width):
-    size, wide = chunks[0].shape
-    rows, mid = firsts[0].shape
-    hidden = mid // held
-    at = 1 + len(firsts)
-    column = pl.BlockSpec((rows, hidden), lambda e, i: (0, i[at + e]))
-    return pl.pallas_call(
-        functools.partial(weight_grad_kernel, len(chunks)),
-        name="weight_grads",
-        grid_spec=pltpu.PrefetchScalarGridSpec(
-            num_scalar_prefetch=1,
-            grid=(held,),
-            in_specs=[
-                pl.BlockSpec((size, wide), lambda e, i: (0, 0), pipeline_mode=pl.Buffered(1))
-                for _ in chunks
-            ]
-            + [column for _ in firsts + seconds],
-            out_specs=pl.BlockSpec((1, 2, width, hidden), lambda e, i: (e, 0, 0, 0)),
-            scratch_shapes=[pltpu.VMEM((width, size * len(chunks)), BF)],
-        ),
-        out_shape=jax.ShapeDtypeStruct((held, 2, width, hidden), BF),
-        compiler_params=pltpu.CompilerParams(vmem_limit_bytes=58 << 20),
-        cost_estimate=pl.CostEstimate(
-            flops=4 * len(firsts) * rows * width * mid,
-            transcendentals=0,
-            bytes_accessed=4 * len(firsts) * rows * (width + mid),
-        ),
-    )(info, *chunks, *firsts, *seconds)
-
-
-def down_grad_kernel(count, info_ref, *refs):
-    rights = refs[: 2 * count]
-    lefts = refs[2 * count : 3 * count]
-    total = None
-    for i, left in enumerate(lefts):
-        right = jnp.concatenate([rights[2 * i][0, 0], rights[2 * i + 1][0, 0]], axis=0)
-        term = dot(left[...], right, 0, 0)
-        total = term if total is None else total + term
-    refs[-1][0] = total.astype(BF)
-
-
-def down_grads(info, do_all, acts, held):
-    _, n_z, size, width = do_all.shape
+    )(info, near, far, do_near, do_far, gate, up, down)
+
+
+def expert_grad_kernel(count, info_ref, *refs):
+    rows_x, rows_do = refs[: 2 * count], refs[2 * count : 4 * count]
+    acts, dgs, dus = (refs[(4 + k) * count : (5 + k) * count] for k in range(3))
+    out = refs[-1]
+    width = rows_do[0].shape[-1]
+    hidden = acts[0].shape[1]
+    down = both = None
+    for s in range(count):
+        do = jnp.concatenate([rows_do[2 * s][0, 0], rows_do[2 * s + 1][0, 0]], axis=0)
+        x = jnp.concatenate([rows_x[2 * s][:, :width], rows_x[2 * s + 1][:, :width]], axis=0)
+        dgu = jnp.concatenate([dgs[s][...], dus[s][...]], axis=1)
+        first, second = dot(acts[s][...], do, 0, 0), dot(dgu, x, 0, 0)
+        down = first if down is None else down + first
+        both = second if both is None else both + second
+    out[0, 0] = down.astype(BF)
+    out[0, 1] = both[:hidden].astype(BF)
+    out[0, 2] = both[hidden:].astype(BF)
+
+
+def expert_grads(info, chunks, do_all, acts, dgs, dus, held, start, count):
+    n_z = len(acts)
+    if n_z > 4:
+        total = 0.0
+        for b in range(0, n_z, 4):
+            part = slice(b, b + 4)
+            here = jnp.concatenate([info[:1], info[1 + b : 5 + b], info[1 + n_z :]])
+            total = total + expert_grads(
+                here,
+                chunks[2 * b : 2 * b + 8],
+                do_all,
+                acts[part],
+                dgs[part],
+                dus[part],
+                held,
+                start,
+                count,
+            ).astype(F32)
+        return total.astype(BF)
+    size, width = do_all.shape[2:]
+    wide = chunks[0].shape[1]
     rows, mid = acts[0].shape
     hidden = mid // held
-    at = 1 + n_z
-    chunk = lambda other, s: pl.BlockSpec(
+    at = 1 + n_z + start
+    chunk = pl.BlockSpec((size, wide), lambda e, i: (0, 0), pipeline_mode=pl.Buffered(1))
+    do_chunk = lambda other, s: pl.BlockSpec(
         (1, 1, size, width),
         lambda e, i: ((1 - i[0]) if other else i[0], i[1 + s], 0, 0),
         pipeline_mode=pl.Buffered(1),
     )
+    column = pl.BlockSpec((rows, hidden), lambda e, i: (0, i[at + e]))
     return pl.pallas_call(
-        functools.partial(down_grad_kernel, n_z),
-        name="down_grads",
+        functools.partial(expert_grad_kernel, n_z),
+        name="expert_grads",
         grid_spec=pltpu.PrefetchScalarGridSpec(
             num_scalar_prefetch=1,
-            grid=(held,),
-            in_specs=[chunk(other, s) for s in range(n_z) for other in (False, True)]
-            + [pl.BlockSpec((rows, hidden), lambda e, i: (0, i[at + e])) for _ in acts],
-            out_specs=pl.BlockSpec((1, hidden, width), lambda e, i: (e, 0, 0)),
-        ),
-        out_shape=jax.ShapeDtypeStruct((held, hidden, width), BF),
-        compiler_params=pltpu.CompilerParams(vmem_limit_bytes=56 << 20),
+            grid=(count,),
+            in_specs=[chunk for _ in chunks]
+            + [do_chunk(other, s) for s in range(n_z) for other in (False, True)]
+            + [column] * (3 * n_z),
+            out_specs=pl.BlockSpec((1, 3, hidden, width), lambda e, i: (e, 0, 0, 0)),
+        ),
+        out_shape=jax.ShapeDtypeStruct((count, 3, hidden, width), BF),
+        compiler_params=pltpu.CompilerParams(vmem_limit_bytes=58 << 20),
         cost_estimate=pl.CostEstimate(
-            flops=2 * len(acts) * rows * width * mid,
+            flops=60 * n_z * rows * width * hidden * count,
             transcendentals=0,
-            bytes_accessed=2 * len(acts) * rows * (width + mid),
-        ),
-    )(info, *([do_all] * (2 * n_z)), *acts)
+            bytes_accessed=4 * n_z * rows * (width + hidden * count),
+        ),
+    )(info, *chunks, *([do_all] * (2 * n_z)), *acts, *dgs, *dus)
 
 
 def place_kernel(count, info_ref, *refs):
+    down, gate, up = refs[count:]
     for i, ref in enumerate(refs[:count]):
 
         @pl.when(pl.program_id(0) == i)
         def _():
-            for k, out in enumerate(refs[count:]):
-                out[0] = ref[0, k].astype(F32)
+            down[0] = ref[0, 0].astype(F32)
+            gate[0] = ref[0, 1].astype(F32).T
+            up[0] = ref[0, 2].astype(F32).T
 
 
 def place(info, parts):
-    kinds = parts[0][0].shape[1]
-    shape = parts[0][0].shape[2:]
+    hidden, width = parts[0][0].shape[2:]
+    count = len(parts)
+    out = lambda *shape: pl.BlockSpec((1,) + shape, lambda e, i: (i[e], 0, 0))
     return pl.pallas_call(
-        functools.partial(place_kernel, len(parts)),
+        functools.partial(place_kernel, count),
         name="place",
         grid_spec=pltpu.PrefetchScalarGridSpec(
             num_scalar_prefetch=1,
-            grid=(len(parts),),
+            grid=(count,),
             in_specs=[
-                pl.BlockSpec((1, kinds) + shape, lambda e, i, k=k: (k, 0, 0, 0)) for _, k in parts
+                pl.BlockSpec((1, 3, hidden, width), lambda e, i, k=k: (k, 0, 0, 0)) for _, k in parts
             ],
-            out_specs=[pl.BlockSpec((1,) + shape, lambda e, i: (i[e], 0, 0))] * kinds,
-        ),
-        out_shape=[jax.ShapeDtypeStruct((len(parts),) + shape, F32)] * kinds,
+            out_specs=[out(hidden, width), out(width, hidden), out(width, hidden)],
+        ),
+        out_shape=[
+            jax.ShapeDtypeStruct((count, hidden, width), F32),
+            jax.ShapeDtypeStruct((count, width, hidden), F32),
+            jax.ShapeDtypeStruct((count, width, hidden), F32),
+        ],
         compiler_params=pltpu.CompilerParams(vmem_limit_bytes=48 << 20),
         cost_estimate=pl.CostEstimate(
-            flops=0, transcendentals=0, bytes_accessed=6 * kinds * len(parts) * math.prod(shape)
+            flops=0, transcendentals=0, bytes_accessed=18 * count * hidden * width
         ),
     )(info, *[array for array, _ in parts])
 
@@ -673,23 +669,27 @@
     grad_half = (pick(cotangent[0], tp, 2, 0).astype(F32) * pick(valid, tp, 2, 0)).astype(BF)
     grad_other = swap(grad_half, "tp")
 
-    def bring(own):
-        piece = pick(own, core, 2, 0)
+    wide_split = n_cx == 2 and (shard // 4) % 16 == 0
+
+    def bring(own, over_chips):
+        piece = pick(own, ctx, n_ctx, 0) if over_chips else pick(own, core, 2, 0)
         return own, [shift(piece, "fsdp", n_z, s) for s in range(1, n_z)]
 
-    def spread(own, got):
-        got = jnp.stack(got)
+    def spread(own, got, over_chips):
+        got = jnp.stack(got)[None]
+        if over_chips:
+            got = jnp.concatenate([got, swap(got, "cx")], axis=0)
         return own, got, swap(got, "core")
 
-    kv_pieces = spread(*bring(jnp.concatenate([key_matrix, value_matrix], axis=1)))
-    q_own, q_got = bring(after(query_weight, kv_pieces[1]))
-    here = jnp.stack([z, core]).astype(jnp.int32)
+    kv_pieces = spread(*bring(jnp.concatenate([key_matrix, value_matrix], axis=1), False), False)
+    q_own, q_got = bring(after(query_weight, kv_pieces[1]), wide_split)
+    here = jnp.stack([z, core, cx]).astype(jnp.int32)
 
     routed, kept = keep_plan(routes[0], visit_order[0, 0], live)
 
     inputs = tokens[0].astype(F32)
     inverse_one, normed_one = normalize(inputs)
-    hidden_one = (normed_one * gain_first).astype(BF)
+    hidden_one = after((normed_one * gain_first).astype(BF), grad_other)
     frequency = jnp.exp(
         jnp.arange(HEAD // 2, dtype=F32) * (-2.0 * math.log(10000.0) / HEAD)
     )
@@ -702,9 +702,10 @@
     for s in range(1, n_cx):
         near_kv.append(shift(near_kv[-1], "cx", n_cx))
     near_kv = jnp.concatenate(near_kv, axis=0)
-    q_pieces = spread(q_own, [after(v, near_kv) for v in q_got])
-    o_own, o_got = bring(after(output_weight.T, q_pieces[1]))
-    grad_all = lax.all_gather(after(grad_half, q_pieces[1]), ("tp", "fsdp"))
+    q_got = [after(v, near_kv) for v in q_got]
+    q_pieces = spread(q_own, q_got, wide_split)
+    o_own, o_got = bring(after(output_weight.T, *q_got), wide_split)
+    grad_all = lax.all_gather(after(grad_half, *q_got), ("tp", "fsdp"))
     grad_all = grad_all.reshape(2, n_z, half, width)
     query, w_q = project(here, *q_pieces, hidden_one, cos, sin, q_width, scale)
     kv = jnp.concatenate([near_kv, swap(near_kv, "core")], axis=0)
@@ -713,7 +714,7 @@
     kv_heads = kv_width // HEAD
     split = [(0, kv_heads // 2), (kv_heads // 2, kv_heads - kv_heads // 2)]
     early, early_lse = attend(after(query, grad_other), kv, info, group, *split[0])
-    o_pieces = spread(o_own, [after(v, early) for v in o_got])
+    o_pieces = spread(o_own, [after(v, early) for v in o_got], wide_split)
     later, later_lse = attend(after(query, early), kv, info, group, *split[1])
     attended = jnp.concatenate([early, later], axis=0)
     lse = jnp.concatenate([early_lse, later_lse], axis=0)
@@ -743,7 +744,7 @@
     near = [message]
     far = [swap(message, "tp")]
     coming = shift(message, "fsdp", n_z)
-    done, mix_all, moving, joined = [], None, None, ()
+    done, moving, joined = [], None, ()
     for s in range(n_z):
         first = near[s]
         if s + 1 < n_z:
@@ -765,14 +766,12 @@
                 first,
                 far[s],
                 *rows_do,
-                n_z,
                 gate_weight,
                 up_weight,
                 down_weight,
-                mix_all,
+                10 if s else 1,
             )
         )
-        mix_all = done[s][2]
         if s > 1:
             part = done[s - 1][0].astype(F32) + swap(done[s - 1][1], "tp").astype(F32)
             if s > 2:
@@ -780,48 +779,37 @@
             moving = part.astype(BF)
             joined = (moving,)
     last = swap(done[-1][1], "tp")
-    by_ctx = held == n_ctx and n_cx == 2
-    if by_ctx:
-        slots = [(1 - core) * 2 + 1 - cx, (1 - core) * 2 + cx, core * 2 + 1 - cx, core * 2 + cx]
-    else:
-        slots = list(range(held))
+    by_core = held % 2 == 0
+    first_slot = held // 2 if by_core else 0
+    slots = [((1 - core) * first_slot + k) % held for k in range(first_slot)]
+    slots += [core * first_slot + k for k in range(held - first_slot)]
     order = jnp.stack([jnp.asarray(v, jnp.int32) for v in [tp] + blocks + slots])
-    grad_pair = weight_grads(
-        order,
+    grad_args = (
         [v for s in range(n_z) for v in (near[s], far[s])],
+        grad_all,
+        [done[s][3] for s in range(n_z)],
         [done[s][4] for s in range(n_z)],
-        [after(done[s][5], moving) for s in range(n_z)],
+        [done[s][5] for s in range(n_z)],
         held,
-        width,
-    )
-    part = done[-1][0].astype(F32) + after(last, grad_pair).astype(F32)
+    )
+    theirs = expert_grads(after(order, moving), *grad_args, 0, first_slot) if by_core else None
+    mix_moving = shift(done[1][2], "fsdp", n_z)
+    part = done[-1][0].astype(F32) + after(last, theirs if by_core else moving).astype(F32)
     moving = (shift(moving, "fsdp", n_z).astype(F32) + part).astype(BF)
     own = done[0][0].astype(F32) + swap(after(done[0][1], last), "tp").astype(F32)
-    grad_down = down_grads(
-        order, grad_all, [after(done[s][3], moving) for s in range(n_z)], held
-    )[:, None]
+    mine = expert_grads(after(order, moving), *grad_args, first_slot, held - first_slot)
     back = shift(moving, "fsdp", n_z)
 
-    half_held = held // 2
-
-    def core_stage(v, *others):
-        both = v[half_held:].astype(F32) + after(swap(v[:half_held], "core"), *others).astype(F32)
-        return both, both[:1].astype(BF)
-
-    if by_ctx:
-        pair_half, pair_far = core_stage(grad_pair, grad_down)
-        back, own = after(back, pair_far), after(own, pair_far)
-        pair_far = swap(pair_far, "cx")
+    if by_core:
+        expert_half = mine.astype(F32) + after(swap(theirs, "core"), mine).astype(F32)
+        expert_half = expert_half.astype(BF)
+        expert_sum = lax.psum(expert_half, "cx")
+        back, own = after(back, expert_half), after(own, expert_half)
+    else:
+        expert_sum = lax.psum(mine, ("cx", "core"))
     back = back.astype(F32) + own
     hidden_grad = back[:, :width]
     gate_grad = back[:, width : width + E] * kept_half
-
-    mixture = lax.psum_scatter(
-        after(mix_all, back).reshape(2 * n_z * half, width),
-        ("fsdp", "tp"),
-        scatter_dimension=0,
-        tiled=True,
-    )
 
     logit_grad = (
         gates * (gate_grad - jnp.sum(gates * gate_grad, axis=1, keepdims=True))
@@ -834,28 +822,57 @@
     ).astype(BF)
     lead = tp == 0
     branch_other = swap(branch_half, "tp")
-    if by_ctx:
-        down_half, down_far = core_stage(grad_down)
-        branch_other = after(branch_other, down_far)
-        down_far = swap(down_far, "cx")
     branch = jnp.concatenate(
         [jnp.where(lead, branch_half, branch_other), jnp.where(lead, branch_other, branch_half)],
         axis=0,
     )
 
     attended_grad = dot(o_full, branch, 0, 1).astype(BF)
-    grad_output = dot(attended, branch, 1, 0).astype(BF)
+    grad_output = dot(branch, attended, 0, 1).astype(BF)
     attended_grad = after(attended_grad, grad_output)
 
     grad_query_rot, grad_kv = attend_back(
         query, kv, attended, attended_grad, lse, info, group
     )
+    def mix_step(arrived, s, *others):
+        return (after(arrived, *others).astype(F32) + done[s][2].astype(F32)).astype(BF)
+
+    for s in range(2, n_z):
+        mix_moving = mix_step(mix_moving, s, *((theirs,) if s == 2 and by_core else (grad_kv,)))
+        mix_moving = shift(mix_moving, "fsdp", n_z)
     kv_sum = grad_kv[:n_cx].astype(F32) + swap(grad_kv[n_cx:], "core").astype(F32)
     kv_moving = kv_sum[1].astype(BF)
     for s in range(2, n_cx):
         kv_moving = (shift(kv_moving, "cx", n_cx).astype(F32) + kv_sum[s]).astype(BF)
-    kv_grad = shift(kv_moving, "cx", n_cx).astype(F32) + kv_sum[0]
+    kv_far = shift(kv_moving, "cx", n_cx)
     query_grad = (rotate(grad_query_rot, cos, sin, True) * scale).astype(BF)
+
+    def by_core_halves(v):
+        blocks = v.reshape(n_z, v.shape[0] // n_z, v.shape[1])
+        theirs = pick(blocks, 1 - core, 2, 1)
+        return pick(blocks, core, 2, 1).astype(F32), theirs, swap(theirs, "core")
+
+    def by_fsdp(mine, came, *others):
+        half = (mine + after(came, *others).astype(F32)).astype(BF)
+        return half, lax.all_to_all(half, "fsdp", 0, 0)
+
+    def by_chip(came, *others):
+        total = jnp.sum(after(came, *others).astype(F32), axis=0).astype(BF)
+        return total, ring_gather(total[None], "cx", n_cx, 0)
+
+    def whole_of(came, *others):
+        total = jnp.sum(after(came, *others).astype(F32), axis=0).astype(BF)
+        return core_join(total, 0).astype(F32)
+
+    grad_q = dot(hidden_one, query_grad, 0, 1).astype(BF)
+    o_mine, o_theirs, o_came = by_core_halves(grad_output)
+    q_mine, q_theirs, q_came = by_core_halves(grad_q)
+    started = anchor(kv_moving, o_theirs, q_theirs)
+    o_half, o_came = by_fsdp(o_mine, o_came, started)
+    q_half, q_came = by_fsdp(q_mine, q_came, started)
+    started = anchor(started, o_half, q_half)
+
+    kv_grad = after(kv_far, started).astype(F32) + kv_sum[0]
     key_grad = rotate(kv_grad[0], cos, sin, True).astype(BF)
     value_grad = kv_grad[1].astype(BF)
     grad_both = jnp.concatenate([key_grad, value_grad], axis=0)
@@ -863,67 +880,48 @@
     grad_first = jnp.sum(first_part * normed_one, axis=0, keepdims=True)
     first_low = first_part.astype(BF)
     first_other = swap(first_low, "tp")
-    if by_ctx:
-        down_total = (down_half[1:] + after(down_far, first_low).astype(F32)).astype(BF)
-        pair_total = (pair_half[1:] + after(pair_far, first_low).astype(F32)).astype(BF)
-    grad_q = dot(hidden_one, query_grad, 0, 1).astype(BF)
+    small_grad = jnp.concatenate([grad_first, grad_second, grad_router], axis=0)
+    small_other = swap(small_grad, "tp")
     grad_kv_w = dot(hidden_one, grad_both, 0, 1).astype(BF)
-
-    def owned(v, dim, *others):
-        if dim:
-            mine = core_halves(v, 0).astype(BF)
-            part = lambda j: pick(mine, j, n_z, 1)
-        else:
-            mine = core_halves(v.reshape(n_z, v.shape[0] // n_z, v.shape[1]), 1).astype(BF)
-            part = lambda j: lax.dynamic_index_in_dim(mine, j, 0, False)
-        total = part(z).astype(F32)
-        for s in range(1, n_z):
-            total = total + after(shift(part((z + s) % n_z), "fsdp", n_z, s), *others).astype(F32)
-        everyone = ring_gather(total.astype(BF)[None], "cx", n_cx, 0)
-        return core_join(jnp.sum(everyone.astype(F32), axis=0).astype(BF), 0)
-
-    grad_q = owned(grad_q, 0, first_low).astype(F32)
-    grad_kv_w = owned(grad_kv_w, 0).astype(F32)
-    grad_output = owned(grad_output, 1, first_low).astype(F32)
-
-    valid_half = pick(valid, tp, 2, 0)
-    out_half = (valid_half * (residual + after(mixture, grad_kv).astype(F32))).astype(BF)
+    kv_mine, kv_theirs, kv_came = by_core_halves(grad_kv_w)
+    started = anchor(first_low, small_grad, kv_theirs)
+    kv_half, kv_came = by_fsdp(kv_mine, kv_came, started)
+    small_grad = small_grad + after(small_other, started)
+    small_other = swap(small_grad, "core")
+    started = anchor(kv_half, small_grad)
+
+    mixed = mix_step(mix_moving, 0, started)
+    mix_other = swap(mixed[half:], "tp")
+    o_total, o_came = by_chip(o_came, started)
+    q_total, q_came = by_chip(q_came, started)
+    small_grad = small_grad + after(small_other, started)
+    everyone = ring_gather(small_grad[None], "cx", n_cx, 0)
+    started = anchor(mixed, o_total, q_total, small_grad)
+
+    first_grad = first_low.astype(F32) + after(first_other, started).astype(F32)
+    grad_inputs = branch.astype(F32) + norm_backward(
+        first_grad, gain_first, inverse_one, normed_one
+    )
+    mixture = mixed[:half].astype(F32) + after(mix_other, first_grad).astype(F32)
+    out_half = (pick(valid, tp, 2, 0) * (residual + mixture)).astype(BF)
     out_other = swap(out_half, "tp")
+    kv_total, kv_came = by_chip(kv_came, started)
+    total = jnp.sum(after(everyone, started), axis=0)
+    small_mine = jnp.sum(
+        lax.all_to_all(total, "fsdp", 1, 0, tiled=True).reshape(n_z, 2 + E, shard), axis=0
+    )
+    parts = [(expert_sum, k) for k in range(held - first_slot)]
+    if by_core:
+        others = swap(after(expert_sum, started), "core")
+        parts = [(others, k) for k in range(first_slot)] + parts
+    grad_q = whole_of(q_came, started)
+    grad_output = whole_of(o_came, started).T
+    started = anchor(out_half, kv_total)
+    grad_down, grad_gate, grad_up = place(order[1 + n_z :], parts)
+    grad_kv_w = whole_of(kv_came, started)
+    out_other = after(out_other, started)
     layer_out = jnp.concatenate(
         [jnp.where(lead, out_half, out_other), jnp.where(lead, out_other, out_half)], axis=0
-    )
-
-    def ctx_sum_generic(v):
-        kinds, a, b = v.shape[1:]
-        total = ctx_total(v.reshape(-1, b), n_cx).reshape(v.shape).astype(F32)
-        return [total[:, k] for k in range(kinds)]
-
-    def ctx_sum_end(total):
-        both = jnp.concatenate([swap(total, "cx"), total], axis=0)
-        others = swap(both, "core")
-        return place(
-            jnp.stack(slots).astype(jnp.int32), [(others, 0), (others, 1), (both, 0), (both, 1)]
-        )
-
-    if by_ctx:
-        (grad_down,) = ctx_sum_end(down_total)
-        grad_gate, grad_up = ctx_sum_end(pair_total)
-    else:
-        (grad_down,) = ctx_sum_generic(grad_down)
-        grad_gate, grad_up = ctx_sum_generic(grad_pair)
-
-    small_grad = jnp.concatenate([grad_first, grad_second, grad_router], axis=0)
-    small_grad = small_grad + swap(small_grad, "tp")
-    small_grad = small_grad + swap(small_grad, "core")
-    everyone = ring_gather(small_grad[None], "cx", n_cx, 0)
-    total = jnp.sum(everyone, axis=0)
-    small_mine = pick(total, z, n_z, 1)
-    for s in range(1, n_z):
-        small_mine = small_mine + shift(pick(total, (z + s) % n_z, n_z, 1), "fsdp", n_z, s)
-
-    first_grad = first_low.astype(F32) + after(first_other, small_mine).astype(F32)
-    grad_inputs = branch.astype(F32) + norm_backward(
-        first_grad, gain_first, inverse_one, normed_one
     )
 
     return (

time: 669 us -> 625 us (0.934)
  starting transfers between devices: 150 us -> 110 us
  waiting for transfers between devices: 197 us -> 174 us
  other arithmetic: 61.4 us -> 75.7 us
    ppermute x36 -> x27, starting transfers between devices: 116 us -> 60.1 us  [shift(): return lax.ppermute(v, axis, [(i, (i + by) % n) for i in range(n)])]
    ppermute x36 -> x27, waiting for transfers between devices: 124 us -> 76.4 us  [shift(): return lax.ppermute(v, axis, [(i, (i + by) % n) for i in range(n)])]
    all_to_all x0 -> x4, starting transfers between devices: none -> 16.9 us  [the longest x3 13.5 us: by_fsdp(): return (half, lax.all_to_all(half, 'fsdp', 0, 0))]
    convert_element_type x10 -> x11, other arithmetic: 12.7 us -> 26.7 us  [the longest x3 8.13 us: mix_step(): (after(arrived, *others).astype(F32) + done[s][2].astype(F32)).astype(BF)]
    all_to_all x0 -> x4, waiting for transfers between devices: none -> 13.7 us  [the longest x3 13.7 us: by_fsdp(): return (half, lax.all_to_all(half, 'fsdp', 0, 0))]
    ppermute x34 -> x31, waiting for transfers between devices: 73.3 us -> 84 us  [swap(): return lax.ppermute(v, axis, [(0, 1), (1, 0)])]
    slice x4 -> x1, local copies, waits for them, and re-layouts: 8.89 us -> 0.93 us  [local(): mix_other = swap(mixed[half:], 'tp')]
    pallas_call x8 -> x7, Pallas kernels: 125 us -> 127 us  [the longest x4 78.7 us: experts(): pl.pallas_call(expert_kernel, name='experts', grid_spec=pltpu.PrefetchSca...]
  transfers between devices with their start and end apart: 72 -> 64, of which waited for: 20 -> 21; matrix products, arithmetic and copies ran while one was open for 15% -> 19% of each run, Pallas kernels for 25% -> 26%
where the time goes in v3:
time: 625 us; the launch traced here: 616 us
  waiting for transfers between devices  174 us (28%)
  Pallas kernels  174 us (28%)
  starting transfers between devices  110 us (18%)
  other arithmetic  75.7 us (12%)
  local copies, waits for them, and re-layouts  47.5 us (8%)
  matrix products  18.2 us (3%)
  between operations  16.6 us (3%)
    ppermute x31, waiting for transfers between devices, swap(): return lax.ppermute(v, axis, [(0, 1), (1, 0)])  84 us
    pallas_call x4, Pallas kernels, experts(): pl.pallas_call(expert_kernel, name='experts', grid_spec=pltpu.PrefetchSca...  78.7 us
    ppermute x27, waiting for transfers between devices, shift(): return lax.ppermute(v, axis, [(i, (i + by) % n) for i in range(n)])  76.4 us
    ppermute x27, starting transfers between devices, shift(): return lax.ppermute(v, axis, [(i, (i + by) % n) for i in range(n)])  60.1 us
    pallas_call x2, Pallas kernels, expert_grads(): pl.pallas_call(functools.partial(expert_grad_kernel, n_z), name='expert_g...  37.2 us
    ppermute x31, starting transfers between devices, swap(): return lax.ppermute(v, axis, [(0, 1), (1, 0)])  33.3 us
    unnamed x164, local copies, waits for them, and re-layouts  21.8 us
    pallas_call x1, Pallas kernels, attend_back(): pl.pallas_call(functools.partial(attend_back_kernel, group), name='attend...  20.3 us
  transfers between devices with their start and end apart: 64, of which 21 were waited for; matrix products, arithmetic and copies ran while one was open for 19% of the time, Pallas kernels for 26%

profile of v3, /device:TPU:1, one launch (start us, length us, event | category | flops | bytes accessed | tf_op | source)
XLA Modules:
  0.0 616.2 jit_solution(15371496048349307303)
XLA Ops:
  39.1 10.4 %collective-permute-done.8 = bf16[256,1536]{1,0:T(8,128)(2,1)S(1)} collective-permute-done((bf16[256,1536]{1,0:T(8,128)(2,1)S(1)}, bf16[256,1536]{1,0:T(8,128)(2,1)S(1)}, u32[]{:S(2)}, u32[]{:S(2)}) %collective-permute-start.8) | collective-permute-done | bytes 786464 | tf_op jit(solution)/shard_map/ppermute | solution.py:32
  70.9 9.2 %collective-permute-done.12 = bf16[1,3,96,768]{3,2,1,0:T(8,128)(2,1)S(1)} collective-permute-done((bf16[1,3,96,768]{3,2,1,0:T(8,128)(2,1)S(1)}, bf16[1,3,96,768]{3,2,1,0:T(8,128)(2,1)S(1)}, u32[]{:S(2)}, u32[]{:S(2)}) %collective-permute-start.12) | collective-permute-done | bytes 442400 | tf_op jit(solution)/shard_map/ppermute | solution.py:32
  96.7 9.3 %attend.2 = (bf16[384,512]{1,0:T(8,128)(2,1)S(1)}, f32[2,8,512]{2,1,0:T(8,128)S(1)}) custom-call(s32[4]{0:T(128)S(1)} %pad_add_fusion.info_ref, bf16[768,512]{1,0:T(8,128)(2,1)S(1)} %get-tuple-element.111.q_ref, bf16[4,2,256,512]{3,2,1,0:T(8,128)(2,1)S(1)} %pad_maximum_fusion.kv_ref), custom_call_target="tpu_custom_call" | custom-call | flops 1610612736 | bytes 1835008 | tf_op jit(solution)/shard_map/attend/pallas_call | solution.py:277
  106.0 13.2 %collective-permute-done.16 = bf16[96,768]{1,0:T(8,128)(2,1)S(1)} collective-permute-done((bf16[96,768]{1,0:T(8,128)(2,1)S(1)}, bf16[96,768]{1,0:T(8,128)(2,1)S(1)}, u32[]{:S(2)}, u32[]{:S(2)}) %collective-permute-start.16) | collective-permute-done | bytes 147488 | tf_op jit(solution)/shard_map/ppermute | solution.py:28
  120.6 10.0 %collective-permute-done.18 = bf16[1,3,96,768]{3,2,1,0:T(8,128)(2,1)S(1)} collective-permute-done((bf16[1,3,96,768]{3,2,1,0:T(8,128)(2,1)S(1)}, bf16[1,3,96,768]{3,2,1,0:T(8,128)(2,1)S(1)}, u32[]{:S(2)}, u32[]{:S(2)}) %collective-permute-start.18) | collective-permute-done | bytes 442400 | tf_op jit(solution)/shard_map/ppermute | solution.py:32
  136.4 9.2 %attend.3 = (bf16[384,512]{1,0:T(8,128)(2,1)S(1)}, f32[2,8,512]{2,1,0:T(8,128)S(1)}) custom-call(s32[4]{0:T(128)S(1)} %pad_add_fusion.info_ref, bf16[768,512]{1,0:T(8,128)(2,1)S(1)} %copy-done.20, bf16[4,2,256,512]{3,2,1,0:T(8,128)(2,1)S(1)} %copy-done.7), custom_call_target="tpu_custom_call" | custom-call | flops 1610612736 | bytes 1835008 | tf_op jit(solution)/shard_map/attend/pallas_call | solution.py:277
  154.7 23.6 %collective-permute-done.20 = bf16[256,1536]{1,0:T(8,128)(2,1)} collective-permute-done((bf16[256,1536]{1,0:T(8,128)(2,1)}, bf16[256,1536]{1,0:T(8,128)(2,1)}, u32[]{:S(2)}, u32[]{:S(2)}) %collective-permute-start.20) | collective-permute-done | bytes 786464 | tf_op jit(solution)/shard_map/ppermute | solution.py:32
  189.5 28.7 %collective-permute-done.21.near_in.refs_2_ = bf16[256,1664]{1,0:T(8,128)(2,1)} collective-permute-done((bf16[256,1664]{1,0:T(8,128)(2,1)}, bf16[256,1664]{1,0:T(8,128)(2,1)}, u32[]{:S(2)}, u32[]{:S(2)}) %collective-permute-start.21) | collective-permute-done | bytes 852000 | tf_op jit(solution)/shard_map/ppermute | solution.py:28
  218.5 19.7 %experts.4 = (bf16[256,1664]{1,0:T(8,128)(2,1)}, bf16[256,1664]{1,0:T(8,128)(2,1)}, bf16[512,1536]{1,0:T(8,128)(2,1)}, bf16[512,1024]{1,0:T(8,128)(2,1)}, bf16[5...) custom-call(s32[6]{0:T(128)} %stack.166.info_ref, bf16[256,1664]{1,0:T(8,128)(2,1)} %concatenate.61.near_in.refs_0_, ...), custom_call_target="tpu_custom_call" | custom-call | flops 9663676416 | bytes 22020096 | tf_op jit(solution)/shard_map/experts/pallas_call | solution.py:462
  241.6 19.5 %experts.5 = (bf16[256,1664]{1,0:T(8,128)(2,1)}, bf16[256,1664]{1,0:T(8,128)(2,1)}, bf16[512,1536]{1,0:T(8,128)(2,1)}, bf16[512,1024]{1,0:T(8,128)(2,1)}, bf16[5...) custom-call(s32[6]{0:T(128)} %stack.164.info_ref, bf16[256,1664]{1,0:T(8,128)(2,1)} %collective-permute-done.21.near_in.refs_2_, ...), custom_call_target="tpu_custom_call" | custom-call | flops 96636764160 | bytes 22020096 | tf_op jit(solution)/shard_map/experts/pallas_call | solution.py:462
  263.0 20.1 %experts.6 = (bf16[256,1664]{1,0:T(8,128)(2,1)}, bf16[256,1664]{1,0:T(8,128)(2,1)}, bf16[512,1536]{1,0:T(8,128)(2,1)}, bf16[512,1024]{1,0:T(8,128)(2,1)}, bf16[5...) custom-call(s32[6]{0:T(128)} %stack.174.info_ref, bf16[256,1664]{1,0:T(8,128)(2,1)} %copy-done.76, ...), custom_call_target="tpu_custom_call" | custom-call | flops 96636764160 | bytes 22020096 | tf_op jit(solution)/shard_map/experts/pallas_call | solution.py:462
  283.8 14.5 %collective-permute-done.26 = bf16[256,1664]{1,0:T(8,128)(2,1)S(1)} collective-permute-done((bf16[256,1664]{1,0:T(8,128)(2,1)}, bf16[256,1664]{1,0:T(8,128)(2,1)S(1)}, u32[]{:S(2)}, u32[]{:S(2)}) %collective-permute-start.26) | collective-permute-done | bytes 852000 | tf_op jit(solution)/shard_map/ppermute | solution.py:32
  299.6 19.5 %experts.7 = (bf16[256,1664]{1,0:T(8,128)(2,1)}, bf16[256,1664]{1,0:T(8,128)(2,1)}, bf16[512,1536]{1,0:T(8,128)(2,1)}, bf16[512,1024]{1,0:T(8,128)(2,1)}, bf16[5...) custom-call(s32[6]{0:T(128)} %stack.175.info_ref, bf16[256,1664]{1,0:T(8,128)(2,1)} %collective-permute-done.28.near_in.refs_6_, ...), custom_call_target="tpu_custom_call" | custom-call | flops 96636764160 | bytes 22020096 | tf_op jit(solution)/shard_map/experts/pallas_call | solution.py:462
  323.5 18.6 %expert_grads.2 = bf16[2,3,256,1536]{3,2,1,0:T(8,128)(2,1)} custom-call(s32[9]{0:T(128)} %stack.173.info_ref, bf16[256,1664]{1,0:T(8,128)(2,1)} %concatenate.61.near_in.refs_0_, bf16[256,1664]{1,0:T(8,128)(2,1)} %collective-permute-done.23.far_in.refs_1_, bf16[256,1664]{1,0:T(8,128)(2,1)} %collective-permute-done.21.near_in.refs_2_, ...), custom_call_target="tpu_custom_call" | custom-call | flops 96636764160 | bytes 16777216 | tf_op jit(solution)/shard_map/expert_grads/pallas_call | solution.py:561
  351.4 18.6 %expert_grads.3 = bf16[2,3,256,1536]{3,2,1,0:T(8,128)(2,1)} custom-call(s32[9]{0:T(128)} %stack.173.info_ref, bf16[256,1664]{1,0:T(8,128)(2,1)} %concatenate.61.near_in.refs_0_, bf16[256,1664]{1,0:T(8,128)(2,1)} %collective-permute-done.23.far_in.refs_1_, bf16[256,1664]{1,0:T(8,128)(2,1)} %collective-permute-done.21.near_in.refs_2_, ...), custom_call_target="tpu_custom_call" | custom-call | flops 96636764160 | bytes 16777216 | tf_op jit(solution)/shard_map/expert_grads/pallas_call | solution.py:561
  371.4 7.4 %add_convert_fusion = bf16[2,3,256,1536]{3,2,1,0:T(8,128)(2,1)} fusion(bf16[2,3,256,1536]{3,2,1,0:T(8,128)(2,1)} %collective-permute-done.36, bf16[2,3,256,1536]{3,2,1,0:T(8,128)(2,1)} %expert_grads.3), kind=kLoop, calls=%fused_computation.1 | loop fusion | flops 9437184 | bytes 14155776 | tf_op jit(solution)/shard_map/convert_element_type | solution.py:805
  390.6 12.3 %collective-permute-done.38 = bf16[256,1536]{1,0:T(8,128)(2,1)} collective-permute-done((bf16[256,1536]{1,0:T(8,128)(2,1)}, bf16[256,1536]{1,0:T(8,128)(2,1)}, u32[]{:S(2)}, u32[]{:S(2)}) %collective-permute-start.38) | collective-permute-done | bytes 786464 | tf_op jit(solution)/shard_map/ppermute | solution.py:32
  408.2 20.3 %attend_back.1 = (f32[768,512]{1,0:T(8,128)S(1)}, bf16[4,2,256,512]{3,2,1,0:T(8,128)(2,1)S(1)}) custom-call(s32[4]{0:T(128)S(1)} %pad_add_fusion.info_ref, bf16[768,512]{1,0:T(8,128)(2,1)S(1)} %copy-done.21, bf16[4,2,256,512]{3,2,1,0:T(8,128)(2,1)} %copy-done.6, bf16[768,512]{1,0:T(8,128)(2,1)S(1)} %copy-done.15, ...), custom_call_target="tpu_custom_call" | custom-call | flops 8053063680 | bytes 8126464 | tf_op jit(solution)/shard_map/attend_back/pallas_call | solution.py:355
  441.5 11.1 %collective-permute-start.41 = (bf16[2,256,512]{2,1,0:T(8,128)(2,1)}, bf16[2,256,512]{2,1,0:T(8,128)(2,1)}, u32[]{:S(2)}, u32[]{:S(2)}) collective-permute-start(bf16[2,256,512]{2,1,0:T(8,128)(2,1)} %fusion.21), channel_id=1, source_target_pairs={{0,4},{4,0},{1,5},{5,1},{2,6},{6,2},{3,7},{7,3},{8,12},{12,8},{9,1... | collective-permute-start | bytes 1572872 | tf_op jit(solution)/shard_map/ppermute | solution.py:28
  461.5 11.5 %collective-permute-done.41 = bf16[2,256,512]{2,1,0:T(8,128)(2,1)} collective-permute-done((bf16[2,256,512]{2,1,0:T(8,128)(2,1)}, bf16[2,256,512]{2,1,0:T(8,128)(2,1)}, u32[]{:S(2)}, u32[]{:S(2)}) %collective-permute-start.41) | collective-permute-done | bytes 524320 | tf_op jit(solution)/shard_map/ppermute | solution.py:28
  502.9 10.4 %collective-permute-start.50 = (f32[1,18,1536]{2,1,0:T(8,128)S(1)}, f32[1,18,1536]{2,1,0:T(8,128)S(1)}, u32[]{:S(2)}, u32[]{:S(2)}) collective-permute-start(f32[1,18,1536]{2,1,0:T(8,128)S(1)} %bitcast.141), channel_id=1, source_target_pairs={{0,4},{4,0},{1,5},{5,1},{2,6},{6,2},{3,7},{7,3},{8,12},{12,8},{9,1... | collective-permute-start | bytes 331784 | tf_op jit(solution)/shard_map/ppermute | solution.py:28
  519.5 9.3 %all-to-all-done.1 = bf16[4,192,768]{2,1,0:T(8,128)(2,1)} async-done(((bf16[4,192,768]{2,1,0:T(8,128)(2,1)}), bf16[4,192,768]{2,1,0:T(8,128)(2,1)}, u32[]{:S(2)}, u32[]{:S(2)}) %all-to-all-start.1) | async-done | bytes 1179680 | tf_op jit(solution)/shard_map/all_to_all | solution.py:857
  538.3 10.5 %collective-permute-start.51 = (bf16[1,192,768]{2,1,0:T(8,128)(2,1)}, bf16[1,192,768]{2,1,0:T(8,128)(2,1)}, u32[]{:S(2)}, u32[]{:S(2)}) collective-permute-start(bf16[1,192,768]{2,1,0:T(8,128)(2,1)} %bitcast.126), channel_id=1, source_target_pairs={{0,4},{4,0},{1,5},{5,1},{2,6},{6,2},{3,7},{7,3},{8,12},{12,8},{9,1... | collective-permute-start | bytes 884744 | tf_op jit(solution)/shard_map/ppermute | solution.py:28
  597.4 11.4 %place.1 = (f32[4,256,1536]{2,1,0:T(8,128)}, f32[4,1536,256]{2,1,0:T(8,128)}, f32[4,1536,256]{2,1,0:T(8,128)}) custom-call(s32[4]{0:T(128)S(1)} %pad_add_fusion.2.info_ref, bf16[2,3,256,1536]{3,2,1,0:T(8,128)(2,1)} %collective-permute-done.57.refs_0_.refs_1_, bf16[2,3,256,1536]{3,2,1,0:T(8,128)(2,1)} %collective-permute-done.57.refs_0_.refs_1_, ...), custom_call_target="tpu_custom_call" | custom-call | bytes 28311552 | tf_op jit(solution)/shard_map/place/pallas_call | solution.py:597
  (426 shorter events, 251.4 us)
Async XLA Ops:
  7.2 233.5 %all-gather.3.cloned.1.call-start = ((), (), s32[]{:S(2)}) async-start(), calls=%async_computation.5 | async-start | bytes 7077888 | tf_op jit(solution)/shard_map/all_gather | solution.py:708
  69.2 513.6 %all-reduce.2.cloned.1.call-start = ((), (), s32[]{:S(2)}) async-start(), calls=%async_computation.4 | async-start | bytes 9437184 | tf_op jit(solution)/shard_map/psum | solution.py:806
  87.1 32.1 %collective-permute-start.16 = (bf16[96,768]{1,0:T(8,128)(2,1)S(1)}, bf16[96,768]{1,0:T(8,128)(2,1)S(1)}, u32[]{:S(2)}, u32[]{:S(2)}) collective-permute-start(bf16[96,768]{1,0:T(8,128)(2,1)S(1)} %constant_dynamic-slice_fusion.3), channel_id=1, source_target_pairs={{0,16},{8,24},{16,0},{24,8},{1,17},{9,25},{17,1},{25,9},{2,18},{10... | collective-permute-start | bytes 442376 | tf_op jit(solution)/shard_map/ppermute | solution.py:28
  89.7 29.5 %collective-permute-start.15 = (bf16[96,768]{1,0:T(8,128)(2,1)S(1)}, bf16[96,768]{1,0:T(8,128)(2,1)S(1)}, u32[]{:S(2)}, u32[]{:S(2)}) collective-permute-start(bf16[96,768]{1,0:T(8,128)(2,1)S(1)} %constant_dynamic-slice_fusion.3), channel_id=1, source_target_pairs={{0,8},{8,16},{16,24},{24,0},{1,9},{9,17},{17,25},{25,1},{2,10},{10... | collective-permute-start | bytes 442376 | tf_op jit(solution)/shard_map/ppermute | solution.py:28
  150.5 27.8 %collective-permute-start.20 = (bf16[256,1536]{1,0:T(8,128)(2,1)}, bf16[256,1536]{1,0:T(8,128)(2,1)}, u32[]{:S(2)}, u32[]{:S(2)}) collective-permute-start(bf16[256,1536]{1,0:T(8,128)(2,1)} %convolution_convert_fusion.3), channel_id=1, source_target_pairs={{0,1},{1,0},{2,3},{3,2},{4,5},{5,4},{6,7},{7,6},{8,9},{9,8},{10,11... | collective-permute-start | bytes 2359304 | tf_op jit(solution)/shard_map/ppermute | solution.py:32
  183.8 34.4 %collective-permute-start.21 = (bf16[256,1664]{1,0:T(8,128)(2,1)}, bf16[256,1664]{1,0:T(8,128)(2,1)}, u32[]{:S(2)}, u32[]{:S(2)}) collective-permute-start(bf16[256,1664]{1,0:T(8,128)(2,1)} %concatenate.61.near_in.refs_0_), channel_id=1, source_target_pairs={{0,8},{8,16},{16,24},{24,0},{1,9},{9,17},{17,25},{25,1},{2,10},{10... | collective-permute-start | bytes 2555912 | tf_op jit(solution)/shard_map/ppermute | solution.py:28
  185.3 33.2 %collective-permute-start.23 = (bf16[256,1664]{1,0:T(8,128)(2,1)}, bf16[256,1664]{1,0:T(8,128)(2,1)}, u32[]{:S(2)}, u32[]{:S(2)}) collective-permute-start(bf16[256,1664]{1,0:T(8,128)(2,1)} %concatenate.61.near_in.refs_0_), channel_id=1, source_target_pairs={{0,1},{1,0},{2,3},{3,2},{4,5},{5,4},{6,7},{7,6},{8,9},{9,8},{10,11... | collective-permute-start | bytes 2555912 | tf_op jit(solution)/shard_map/ppermute | solution.py:32
  261.5 37.2 %collective-permute-start.31 = (bf16[256,1664]{1,0:T(8,128)(2,1)}, bf16[256,1664]{1,0:T(8,128)(2,1)S(1)}, u32[]{:S(2)}, u32[]{:S(2)}) collective-permute-start(bf16[256,1664]{1,0:T(8,128)(2,1)} %collective-permute-done.28.near_in.refs_6_), channel_id=1, source_target_pairs={{0,1},{1,0},{2,3},{3,2},{4,5},{5,4},{6,7},{7,6},{8,9},{9,8},{10,11... | collective-permute-start | bytes 2555912 | tf_op jit(solution)/shard_map/ppermute | solution.py:32
  262.3 36.0 %collective-permute-start.26 = (bf16[256,1664]{1,0:T(8,128)(2,1)}, bf16[256,1664]{1,0:T(8,128)(2,1)S(1)}, u32[]{:S(2)}, u32[]{:S(2)}) collective-permute-start(bf16[256,1664]{1,0:T(8,128)(2,1)} %get-tuple-element.127), channel_id=1, source_target_pairs={{0,1},{1,0},{2,3},{3,2},{4,5},{5,4},{6,7},{7,6},{8,9},{9,8},{10,11... | collective-permute-start | bytes 2555912 | tf_op jit(solution)/shard_map/ppermute | solution.py:32
  263.0 84.4 %collective-permute-start.25 = (bf16[512,1536]{1,0:T(8,128)(2,1)}, bf16[512,1536]{1,0:T(8,128)(2,1)}, u32[]{:S(2)}, u32[]{:S(2)}) collective-permute-start(bf16[512,1536]{1,0:T(8,128)(2,1)} %get-tuple-element.125), channel_id=1, source_target_pairs={{0,8},{8,16},{16,24},{24,0},{1,9},{9,17},{17,25},{25,1},{2,10},{10... | collective-permute-start | bytes 4718600 | tf_op jit(solution)/shard_map/ppermute | solution.py:28
  283.0 37.4 %collective-permute-start.30 = (bf16[256,1664]{1,0:T(8,128)(2,1)}, bf16[256,1664]{1,0:T(8,128)(2,1)S(1)}, u32[]{:S(2)}, u32[]{:S(2)}) collective-permute-start(bf16[256,1664]{1,0:T(8,128)(2,1)} %get-tuple-element.131), channel_id=1, source_target_pairs={{0,1},{1,0},{2,3},{3,2},{4,5},{5,4},{6,7},{7,6},{8,9},{9,8},{10,11... | collective-permute-start | bytes 2555912 | tf_op jit(solution)/shard_map/ppermute | solution.py:32
  319.1 28.3 %collective-permute-start.34 = (bf16[256,1664]{1,0:T(8,128)(2,1)}, bf16[256,1664]{1,0:T(8,128)(2,1)S(1)}, u32[]{:S(2)}, u32[]{:S(2)}) collective-permute-start(bf16[256,1664]{1,0:T(8,128)(2,1)} %get-tuple-element.149), channel_id=1, source_target_pairs={{0,1},{1,0},{2,3},{3,2},{4,5},{5,4},{6,7},{7,6},{8,9},{9,8},{10,11... | collective-permute-start | bytes 2555912 | tf_op jit(solution)/shard_map/ppermute | solution.py:32
  342.1 29.3 %collective-permute-start.36 = (bf16[2,3,256,1536]{3,2,1,0:T(8,128)(2,1)}, bf16[2,3,256,1536]{3,2,1,0:T(8,128)(2,1)}, u32[]{:S(2)}, u32[]{:S(2)}) collective-permute-start(bf16[2,3,256,1536]{3,2,1,0:T(8,128)(2,1)} %expert_grads.2), channel_id=1, source_target_pairs={{0,2},{2,0},{1,3},{3,1},{4,6},{6,4},{5,7},{7,5},{8,10},{10,8},{9,1... | collective-permute-start | bytes 14155784 | tf_op jit(solution)/shard_map/ppermute | solution.py:32
  349.9 28.9 %collective-permute-start.35 = (bf16[256,1664]{1,0:T(8,128)(2,1)}, bf16[256,1664]{1,0:T(8,128)(2,1)S(1)}, u32[]{:S(2)}, u32[]{:S(2)}) collective-permute-start(bf16[256,1664]{1,0:T(8,128)(2,1)} %add_convert_fusion.6), channel_id=1, source_target_pairs={{0,8},{8,16},{16,24},{24,0},{1,9},{9,17},{17,25},{25,1},{2,10},{10... | collective-permute-start | bytes 2555912 | tf_op jit(solution)/shard_map/ppermute | solution.py:28
  388.2 40.4 %collective-permute-start.32 = (bf16[512,1536]{1,0:T(8,128)(2,1)}, bf16[512,1536]{1,0:T(8,128)(2,1)}, u32[]{:S(2)}, u32[]{:S(2)}) collective-permute-start(bf16[512,1536]{1,0:T(8,128)(2,1)} %add_convert_fusion.3), channel_id=1, source_target_pairs={{0,8},{8,16},{16,24},{24,0},{1,9},{9,17},{17,25},{25,1},{2,10},{10... | collective-permute-start | bytes 4718600 | tf_op jit(solution)/shard_map/ppermute | solution.py:28
  432.8 67.7 %collective-permute-start.39 = (bf16[512,1536]{1,0:T(8,128)(2,1)}, bf16[512,1536]{1,0:T(8,128)(2,1)}, u32[]{:S(2)}, u32[]{:S(2)}) collective-permute-start(bf16[512,1536]{1,0:T(8,128)(2,1)} %add_convert_fusion.2), channel_id=1, source_target_pairs={{0,8},{8,16},{16,24},{24,0},{1,9},{9,17},{17,25},{25,1},{2,10},{10... | collective-permute-start | bytes 4718600 | tf_op jit(solution)/shard_map/ppermute | solution.py:28
  441.5 31.5 %collective-permute-start.41 = (bf16[2,256,512]{2,1,0:T(8,128)(2,1)}, bf16[2,256,512]{2,1,0:T(8,128)(2,1)}, u32[]{:S(2)}, u32[]{:S(2)}) collective-permute-start(bf16[2,256,512]{2,1,0:T(8,128)(2,1)} %fusion.21), channel_id=1, source_target_pairs={{0,4},{4,0},{1,5},{5,1},{2,6},{6,2},{3,7},{7,3},{8,12},{12,8},{9,1... | collective-permute-start | bytes 1572872 | tf_op jit(solution)/shard_map/ppermute | solution.py:28
  453.8 42.4 %all-to-all-start = ((bf16[4,192,768]{2,1,0:T(8,128)(2,1)}), bf16[4,192,768]{2,1,0:T(8,128)(2,1)}, u32[]{:S(2)}, u32[]{:S(2)}) async-start(bf16[4,192,768]{2,1,0:T(8,128)(2,1)} %add_convert_fusion.5), calls=%async_computation | async-start | bytes 2359296 | tf_op jit(solution)/shard_map/all_to_all | solution.py:857
  485.3 77.6 %collective-permute-start.45 = (bf16[512,1536]{1,0:T(8,128)(2,1)}, bf16[512,1536]{1,0:T(8,128)(2,1)}, u32[]{:S(2)}, u32[]{:S(2)}) collective-permute-start(bf16[512,1536]{1,0:T(8,128)(2,1)} %get-tuple-element.268), channel_id=1, source_target_pairs={{0,1},{1,0},{2,3},{3,2},{4,5},{5,4},{6,7},{7,6},{8,9},{9,8},{10,11... | collective-permute-start | bytes 4718600 | tf_op jit(solution)/shard_map/ppermute | solution.py:32
  496.3 32.5 %all-to-all-start.1 = ((bf16[4,192,768]{2,1,0:T(8,128)(2,1)}), bf16[4,192,768]{2,1,0:T(8,128)(2,1)}, u32[]{:S(2)}, u32[]{:S(2)}) async-start(bf16[4,192,768]{2,1,0:T(8,128)(2,1)} %add_convert_fusion.4), calls=%async_computation.1 | async-start | bytes 2359296 | tf_op jit(solution)/shard_map/all_to_all | solution.py:857
  517.6 42.3 %collective-permute-start.44 = (bf16[256,1536]{1,0:T(8,128)(2,1)}, bf16[256,1536]{1,0:T(8,128)(2,1)}, u32[]{:S(2)}, u32[]{:S(2)}) collective-permute-start(bf16[256,1536]{1,0:T(8,128)(2,1)} %slice.116), channel_id=1, source_target_pairs={{0,1},{1,0},{2,3},{3,2},{4,5},{5,4},{6,7},{7,6},{8,9},{9,8},{10,11... | collective-permute-start | bytes 2359304 | tf_op jit(solution)/shard_map/ppermute | solution.py:32
  538.3 27.4 %collective-permute-start.51 = (bf16[1,192,768]{2,1,0:T(8,128)(2,1)}, bf16[1,192,768]{2,1,0:T(8,128)(2,1)}, u32[]{:S(2)}, u32[]{:S(2)}) collective-permute-start(bf16[1,192,768]{2,1,0:T(8,128)(2,1)} %bitcast.126), channel_id=1, source_target_pairs={{0,4},{4,0},{1,5},{5,1},{2,6},{6,2},{3,7},{7,3},{8,12},{12,8},{9,1... | collective-permute-start | bytes 884744 | tf_op jit(solution)/shard_map/ppermute | solution.py:28
  554.0 27.5 %all-to-all-start.2 = ((bf16[4,192,512]{2,1,0:T(8,128)(2,1)}), bf16[4,192,512]{2,1,0:T(8,128)(2,1)}, u32[]{:S(2)}, u32[]{:S(2)}) async-start(bf16[4,192,512]{2,1,0:T(8,128)(2,1)} %add_convert_fusion.9), calls=%async_computation.2 | async-start | bytes 1572864 | tf_op jit(solution)/shard_map/all_to_all | solution.py:857
  562.5 32.2 %collective-permute-start.49 = (bf16[256,1536]{1,0:T(8,128)(2,1)}, bf16[256,1536]{1,0:T(8,128)(2,1)}, u32[]{:S(2)}, u32[]{:S(2)}) collective-permute-start(bf16[256,1536]{1,0:T(8,128)(2,1)} %multiply_convert_fusion), channel_id=1, source_target_pairs={{0,1},{1,0},{2,3},{3,2},{4,5},{5,4},{6,7},{7,6},{8,9},{9,8},{10,11... | collective-permute-start | bytes 2359304 | tf_op jit(solution)/shard_map/ppermute | solution.py:32
  (120 other events, 1625.7 us)
Sparse Core Ops, SparseCore 0:
  69.3 133.4 all-gather.2
  388.5 128.4 all-reduce.1

commit v4 on v3

--- a/solution.py
+++ b/solution.py
@@ -656,19 +656,6 @@
     live = positions < length
     valid = live.astype(F32)[:, None]
 
-    small = jnp.concatenate(
-        [first_gain[None], second_gain[None], router_weight.T], axis=0
-    )
-    small_full = put(jnp.zeros((2 + E, width), BF), small, z * shard, 1)
-    for s in range(1, n_z):
-        small_full = put(small_full, shift(small, "fsdp", n_z, s), ((z + n_z - s) % n_z) * shard, 1)
-    gain_first = small_full[0:1].astype(F32)
-    gain_second = small_full[1:2].astype(F32)
-    router = small_full[2:]
-
-    grad_half = (pick(cotangent[0], tp, 2, 0).astype(F32) * pick(valid, tp, 2, 0)).astype(BF)
-    grad_other = swap(grad_half, "tp")
-
     wide_split = n_cx == 2 and (shard // 4) % 16 == 0
 
     def bring(own, over_chips):
@@ -681,8 +668,22 @@
             got = jnp.concatenate([got, swap(got, "cx")], axis=0)
         return own, got, swap(got, "core")
 
-    kv_pieces = spread(*bring(jnp.concatenate([key_matrix, value_matrix], axis=1), False), False)
-    q_own, q_got = bring(after(query_weight, kv_pieces[1]), wide_split)
+    kv_own, kv_got = bring(jnp.concatenate([key_matrix, value_matrix], axis=1), False)
+
+    small = jnp.concatenate([first_gain[None], second_gain[None], router_weight.T], axis=0)
+    small_full = lax.all_to_all(jnp.broadcast_to(small[None], (n_z, 2 + E, shard)), "fsdp", 0, 0)
+    small_full = jnp.transpose(small_full, (1, 0, 2)).reshape(2 + E, width)
+    gain_first = small_full[0:1].astype(F32)
+    gain_second = small_full[1:2].astype(F32)
+    router = small_full[2:]
+
+    grad_half = (pick(cotangent[0], tp, 2, 0).astype(F32) * pick(valid, tp, 2, 0)).astype(BF)
+    grad_other = swap(grad_half, "tp")
+
+    kv_pieces = spread(kv_own, kv_got, False)
+    q_own, q_got = bring(after(query_weight, *kv_got), wide_split)
+    started = anchor(*kv_got)
+    kv_pieces = (kv_own, kv_pieces[1], after(kv_pieces[2], started))
     here = jnp.stack([z, core, cx]).astype(jnp.int32)
 
     routed, kept = keep_plan(routes[0], visit_order[0, 0], live)
@@ -701,8 +702,9 @@
     near_kv = [kv_mine]
     for s in range(1, n_cx):
         near_kv.append(shift(near_kv[-1], "cx", n_cx))
-    near_kv = jnp.concatenate(near_kv, axis=0)
-    q_got = [after(v, near_kv) for v in q_got]
+    near_kv = jnp.concatenate([near_kv[0]] + [after(v, anchor(kv_mine)) for v in near_kv[1:]], axis=0)
+    started = anchor(kv_mine)
+    q_got = [after(v, started) for v in q_got]
     q_pieces = spread(q_own, q_got, wide_split)
     o_own, o_got = bring(after(output_weight.T, *q_got), wide_split)
     grad_all = lax.all_gather(after(grad_half, *q_got), ("tp", "fsdp"))

time: 625 us -> 594 us (0.950)
  waiting for transfers between devices: 174 us -> 133 us
  starting transfers between devices: 110 us -> 122 us
    ppermute x31, waiting for transfers between devices: 84 us -> 62.2 us  [swap(): return lax.ppermute(v, axis, [(0, 1), (1, 0)])]
    ppermute x27 -> x24, waiting for transfers between devices: 76.4 us -> 55.7 us  [shift(): return lax.ppermute(v, axis, [(i, (i + by) % n) for i in range(n)])]
    all_to_all x0 -> x1, waiting for transfers between devices: none -> 6.61 us  [local(): lax.all_to_all(jnp.broadcast_to(small[None], (n_z, 2 + E, shard)), 'fsdp'...]
    ppermute x27 -> x24, starting transfers between devices: 60.1 us -> 65.2 us  [shift(): return lax.ppermute(v, axis, [(i, (i + by) % n) for i in range(n)])]
    unnamed x164 -> x165, local copies, waits for them, and re-layouts: 21.8 us -> 21.1 us
  transfers between devices with their start and end apart: 64 -> 62, of which waited for: 21 -> 17; matrix products, arithmetic and copies ran while one was open for 19% -> 20% of each run, Pallas kernels for 26% -> 27%
where the time goes in v4:
time: 594 us; the launch traced here: 586 us
  Pallas kernels  173 us (29%)
  waiting for transfers between devices  133 us (22%)
  starting transfers between devices  122 us (21%)
  other arithmetic  79.7 us (13%)
  local copies, waits for them, and re-layouts  45.2 us (8%)
  matrix products  17.3 us (3%)
  between operations  16.5 us (3%)
    pallas_call x4, Pallas kernels, experts(): pl.pallas_call(expert_kernel, name='experts', grid_spec=pltpu.PrefetchSca...  77.9 us
    ppermute x24, starting transfers between devices, shift(): return lax.ppermute(v, axis, [(i, (i + by) % n) for i in range(n)])  65.2 us
    ppermute x31, waiting for transfers between devices, swap(): return lax.ppermute(v, axis, [(0, 1), (1, 0)])  62.2 us
    ppermute x24, waiting for transfers between devices, shift(): return lax.ppermute(v, axis, [(i, (i + by) % n) for i in range(n)])  55.7 us
    pallas_call x2, Pallas kernels, expert_grads(): pl.pallas_call(functools.partial(expert_grad_kernel, n_z), name='expert_g...  37.1 us
    ppermute x31, starting transfers between devices, swap(): return lax.ppermute(v, axis, [(0, 1), (1, 0)])  36.8 us
    unnamed x165, local copies, waits for them, and re-layouts  21.1 us
    pallas_call x1, Pallas kernels, attend_back(): pl.pallas_call(functools.partial(attend_back_kernel, group), name='attend...  20.1 us
  transfers between devices with their start and end apart: 62, of which 17 were waited for; matrix products, arithmetic and copies ran while one was open for 20% of the time, Pallas kernels for 27%

profile of v4, /device:TPU:1, one launch (start us, length us, event | category | flops | bytes accessed | tf_op | source)
XLA Modules:
  0.0 586.5 jit_solution(11301472786745475677)
XLA Ops:
  26.5 6.6 %all-to-all-done = bf16[4,18,384]{2,1,0:T(8,128)(2,1)S(1)} async-done(((bf16[4,18,384]{2,1,0:T(8,128)(2,1)}), bf16[4,18,384]{2,1,0:T(8,128)(2,1)S(1)}, u32[]{:S(2)}, u32[]{:S(2)}) %all-to-all-start) | async-done | bytes 55328 | tf_op jit(solution)/shard_map/all_to_all | solution.py:674
  51.8 9.0 %collective-permute-done.10 = bf16[1,2,256,512]{3,2,1,0:T(8,128)(2,1)S(1)} collective-permute-done((bf16[1,2,256,512]{3,2,1,0:T(8,128)(2,1)S(1)}, bf16[1,2,256,512]{3,2,1,0:T(8,128)(2,1)S(1)}, u32[]{:S(2)}, u32[]{:S(2)}) %collective-permute-start.10) | collective-permute-done | bytes 524320 | tf_op jit(solution)/shard_map/ppermute | solution.py:28
  87.1 9.7 %attend.2 = (bf16[384,512]{1,0:T(8,128)(2,1)S(1)}, f32[2,8,512]{2,1,0:T(8,128)S(1)}) custom-call(s32[4]{0:T(128)S(1)} %pad_add_fusion.info_ref, bf16[768,512]{1,0:T(8,128)(2,1)S(1)} %get-tuple-element.115.q_ref, bf16[4,2,256,512]{3,2,1,0:T(8,128)(2,1)S(1)} %pad_maximum_fusion.kv_ref), custom_call_target="tpu_custom_call" | custom-call | flops 1610612736 | bytes 1835008 | tf_op jit(solution)/shard_map/attend/pallas_call | solution.py:277
  101.5 5.7 collective-permute-start.15
  108.9 6.0 %collective-permute-done.15 = bf16[1,3,96,768]{3,2,1,0:T(8,128)(2,1)} collective-permute-done((bf16[1,3,96,768]{3,2,1,0:T(8,128)(2,1)S(1)}, bf16[1,3,96,768]{3,2,1,0:T(8,128)(2,1)}, u32[]{:S(2)}, u32[]{:S(2)}) %collective-permute-start.15) | collective-permute-done | bytes 442400 | tf_op jit(solution)/shard_map/ppermute | solution.py:32
  119.4 9.2 %attend.3 = (bf16[384,512]{1,0:T(8,128)(2,1)S(1)}, f32[2,8,512]{2,1,0:T(8,128)S(1)}) custom-call(s32[4]{0:T(128)S(1)} %pad_add_fusion.info_ref, bf16[768,512]{1,0:T(8,128)(2,1)S(1)} %copy-done.21, bf16[4,2,256,512]{3,2,1,0:T(8,128)(2,1)S(1)} %pad_maximum_fusion.kv_ref), custom_call_target="tpu_custom_call" | custom-call | flops 1610612736 | bytes 1835008 | tf_op jit(solution)/shard_map/attend/pallas_call | solution.py:277
  136.9 19.4 %collective-permute-done.17 = bf16[256,1536]{1,0:T(8,128)(2,1)} collective-permute-done((bf16[256,1536]{1,0:T(8,128)(2,1)}, bf16[256,1536]{1,0:T(8,128)(2,1)}, u32[]{:S(2)}, u32[]{:S(2)}) %collective-permute-start.17) | collective-permute-done | bytes 786464 | tf_op jit(solution)/shard_map/ppermute | solution.py:32
  167.8 15.8 %collective-permute-done.18.near_in.refs_2_ = bf16[256,1664]{1,0:T(8,128)(2,1)} collective-permute-done((bf16[256,1664]{1,0:T(8,128)(2,1)S(1)}, bf16[256,1664]{1,0:T(8,128)(2,1)}, u32[]{:S(2)}, u32[]{:S(2)}) %collective-permute-start.18) | collective-permute-done | bytes 852000 | tf_op jit(solution)/shard_map/ppermute | solution.py:28
  183.8 19.5 %experts.4 = (bf16[256,1664]{1,0:T(8,128)(2,1)}, bf16[256,1664]{1,0:T(8,128)(2,1)}, bf16[512,1536]{1,0:T(8,128)(2,1)}, bf16[512,1024]{1,0:T(8,128)(2,1)}, bf16[5...) custom-call(s32[6]{0:T(128)} %stack.166.info_ref, bf16[256,1664]{1,0:T(8,128)(2,1)} %copy-done.50, ...), custom_call_target="tpu_custom_call" | custom-call | flops 9663676416 | bytes 22020096 | tf_op jit(solution)/shard_map/experts/pallas_call | solution.py:462
  206.8 19.5 %experts.5 = (bf16[256,1664]{1,0:T(8,128)(2,1)}, bf16[256,1664]{1,0:T(8,128)(2,1)}, bf16[512,1536]{1,0:T(8,128)(2,1)}, bf16[512,1024]{1,0:T(8,128)(2,1)}, bf16[5...) custom-call(s32[6]{0:T(128)} %stack.164.info_ref, bf16[256,1664]{1,0:T(8,128)(2,1)} %collective-permute-done.18.near_in.refs_2_, ...), custom_call_target="tpu_custom_call" | custom-call | flops 96636764160 | bytes 22020096 | tf_op jit(solution)/shard_map/experts/pallas_call | solution.py:462
  229.8 19.5 %experts.6 = (bf16[256,1664]{1,0:T(8,128)(2,1)}, bf16[256,1664]{1,0:T(8,128)(2,1)}, bf16[512,1536]{1,0:T(8,128)(2,1)}, bf16[512,1024]{1,0:T(8,128)(2,1)}, bf16[5...) custom-call(s32[6]{0:T(128)} %stack.174.info_ref, bf16[256,1664]{1,0:T(8,128)(2,1)} %copy-done.77, ...), custom_call_target="tpu_custom_call" | custom-call | flops 96636764160 | bytes 22020096 | tf_op jit(solution)/shard_map/experts/pallas_call | solution.py:462
  249.3 14.5 %collective-permute-done.23 = bf16[256,1664]{1,0:T(8,128)(2,1)S(1)} collective-permute-done((bf16[256,1664]{1,0:T(8,128)(2,1)}, bf16[256,1664]{1,0:T(8,128)(2,1)S(1)}, u32[]{:S(2)}, u32[]{:S(2)}) %collective-permute-start.23) | collective-permute-done | bytes 852000 | tf_op jit(solution)/shard_map/ppermute | solution.py:32
  266.8 19.5 %experts.7 = (bf16[256,1664]{1,0:T(8,128)(2,1)}, bf16[256,1664]{1,0:T(8,128)(2,1)}, bf16[512,1536]{1,0:T(8,128)(2,1)}, bf16[512,1024]{1,0:T(8,128)(2,1)}, bf16[5...) custom-call(s32[6]{0:T(128)} %stack.175.info_ref, bf16[256,1664]{1,0:T(8,128)(2,1)} %collective-permute-done.25.near_in.refs_6_, ...), custom_call_target="tpu_custom_call" | custom-call | flops 96636764160 | bytes 22020096 | tf_op jit(solution)/shard_map/experts/pallas_call | solution.py:462
  288.9 18.6 %expert_grads.2 = bf16[2,3,256,1536]{3,2,1,0:T(8,128)(2,1)} custom-call(s32[9]{0:T(128)} %stack.173.info_ref, bf16[256,1664]{1,0:T(8,128)(2,1)} %copy-done.50, bf16[256,1664]{1,0:T(8,128)(2,1)} %collective-permute-done.20.far_in.refs_1_, bf16[256,1664]{1,0:T(8,128)(2,1)} %collective-permute-done.18.near_in.refs_2_, bf16[256,1664]{1,0:T(8,128)(2,1)} %copy-done.78, ...), custom_call_target="tpu_custom_call" | custom-call | flops 96636764160 | bytes 16777216 | tf_op jit(solution)/shard_map/expert_grads/pallas_call | solution.py:561
  317.0 18.5 %expert_grads.3 = bf16[2,3,256,1536]{3,2,1,0:T(8,128)(2,1)} custom-call(s32[9]{0:T(128)} %stack.173.info_ref, bf16[256,1664]{1,0:T(8,128)(2,1)} %copy-done.50, bf16[256,1664]{1,0:T(8,128)(2,1)} %collective-permute-done.20.far_in.refs_1_, bf16[256,1664]{1,0:T(8,128)(2,1)} %collective-permute-done.18.near_in.refs_2_, bf16[256,1664]{1,0:T(8,128)(2,1)} %copy-done.78, ...), custom_call_target="tpu_custom_call" | custom-call | flops 96636764160 | bytes 16777216 | tf_op jit(solution)/shard_map/expert_grads/pallas_call | solution.py:561
  336.8 7.4 %add_convert_fusion = bf16[2,3,256,1536]{3,2,1,0:T(8,128)(2,1)} fusion(bf16[2,3,256,1536]{3,2,1,0:T(8,128)(2,1)} %collective-permute-done.33, bf16[2,3,256,1536]{3,2,1,0:T(8,128)(2,1)} %expert_grads.3), kind=kLoop, calls=%fused_computation.1 | loop fusion | flops 9437184 | bytes 14155776 | tf_op jit(solution)/shard_map/convert_element_type | solution.py:807
  356.2 12.4 %collective-permute-done.35 = bf16[256,1536]{1,0:T(8,128)(2,1)} collective-permute-done((bf16[256,1536]{1,0:T(8,128)(2,1)}, bf16[256,1536]{1,0:T(8,128)(2,1)}, u32[]{:S(2)}, u32[]{:S(2)}) %collective-permute-start.35) | collective-permute-done | bytes 786464 | tf_op jit(solution)/shard_map/ppermute | solution.py:32
  373.9 20.1 %attend_back.1 = (f32[768,512]{1,0:T(8,128)S(1)}, bf16[4,2,256,512]{3,2,1,0:T(8,128)(2,1)S(1)}) custom-call(s32[4]{0:T(128)S(1)} %pad_add_fusion.info_ref, bf16[768,512]{1,0:T(8,128)(2,1)S(1)} %copy-done.22, bf16[4,2,256,512]{3,2,1,0:T(8,128)(2,1)} %copy-done.6, bf16[768,512]{1,0:T(8,128)(2,1)S(1)} %copy-done.14, ...), custom_call_target="tpu_custom_call" | custom-call | flops 8053063680 | bytes 8126464 | tf_op jit(solution)/shard_map/attend_back/pallas_call | solution.py:355
  406.9 16.4 %collective-permute-start.38 = (bf16[2,256,512]{2,1,0:T(8,128)(2,1)}, bf16[2,256,512]{2,1,0:T(8,128)(2,1)}, u32[]{:S(2)}, u32[]{:S(2)}) collective-permute-start(bf16[2,256,512]{2,1,0:T(8,128)(2,1)} %fusion.21), channel_id=1, source_target_pairs={{0,4},{4,0},{1,5},{5,1},{2,6},{6,2},{3,7},{7,3},{8,12},{12,8},{9,1... | collective-permute-start | bytes 1572872 | tf_op jit(solution)/shard_map/ppermute | solution.py:28
  432.2 14.9 %collective-permute-done.38 = bf16[2,256,512]{2,1,0:T(8,128)(2,1)} collective-permute-done((bf16[2,256,512]{2,1,0:T(8,128)(2,1)}, bf16[2,256,512]{2,1,0:T(8,128)(2,1)}, u32[]{:S(2)}, u32[]{:S(2)}) %collective-permute-start.38) | collective-permute-done | bytes 524320 | tf_op jit(solution)/shard_map/ppermute | solution.py:28
  471.3 12.5 %collective-permute-start.47 = (f32[1,18,1536]{2,1,0:T(8,128)S(1)}, f32[1,18,1536]{2,1,0:T(8,128)S(1)}, u32[]{:S(2)}, u32[]{:S(2)}) collective-permute-start(f32[1,18,1536]{2,1,0:T(8,128)S(1)} %bitcast.150), channel_id=1, source_target_pairs={{0,4},{4,0},{1,5},{5,1},{2,6},{6,2},{3,7},{7,3},{8,12},{12,8},{9,1... | collective-permute-start | bytes 331784 | tf_op jit(solution)/shard_map/ppermute | solution.py:28
  489.3 8.4 %all-to-all-done.2 = bf16[4,192,768]{2,1,0:T(8,128)(2,1)} async-done(((bf16[4,192,768]{2,1,0:T(8,128)(2,1)}), bf16[4,192,768]{2,1,0:T(8,128)(2,1)}, u32[]{:S(2)}, u32[]{:S(2)}) %all-to-all-start.2) | async-done | bytes 1179680 | tf_op jit(solution)/shard_map/all_to_all | solution.py:859
  507.3 12.0 %collective-permute-start.48 = (bf16[1,192,768]{2,1,0:T(8,128)(2,1)}, bf16[1,192,768]{2,1,0:T(8,128)(2,1)}, u32[]{:S(2)}, u32[]{:S(2)}) collective-permute-start(bf16[1,192,768]{2,1,0:T(8,128)(2,1)} %bitcast.132), channel_id=1, source_target_pairs={{0,4},{4,0},{1,5},{5,1},{2,6},{6,2},{3,7},{7,3},{8,12},{12,8},{9,1... | collective-permute-start | bytes 884744 | tf_op jit(solution)/shard_map/ppermute | solution.py:28
  568.0 11.4 %place.1 = (f32[4,256,1536]{2,1,0:T(8,128)}, f32[4,1536,256]{2,1,0:T(8,128)}, f32[4,1536,256]{2,1,0:T(8,128)}) custom-call(s32[4]{0:T(128)S(1)} %pad_add_fusion.2.info_ref, bf16[2,3,256,1536]{3,2,1,0:T(8,128)(2,1)} %collective-permute-done.54.refs_0_.refs_1_, bf16[2,3,256,1536]{3,2,1,0:T(8,128)(2,1)} %collective-permute-done.54.refs_0_.refs_1_, ...), custom_call_target="tpu_custom_call" | custom-call | bytes 28311552 | tf_op jit(solution)/shard_map/place/pallas_call | solution.py:597
  (423 shorter events, 243.7 us)
Async XLA Ops:
  9.2 24.5 %collective-permute-start = (bf16[192,512]{1,0:T(8,128)(2,1)S(1)}, bf16[192,512]{1,0:T(8,128)(2,1)S(1)}, u32[]{:S(2)}, u32[]{:S(2)}) collective-permute-start(bf16[192,512]{1,0:T(8,128)(2,1)S(1)} %constant_dynamic-slice_fusion.5), channel_id=1, source_target_pairs={{0,8},{8,16},{16,24},{24,0},{1,9},{9,17},{17,25},{25,1},{2,10},{10... | collective-permute-start | bytes 589832 | tf_op jit(solution)/shard_map/ppermute | solution.py:28
  20.8 185.1 %all-gather.3.cloned.1.call-start = ((), (), s32[]{:S(2)}) async-start(), calls=%async_computation.6 | async-start | bytes 7077888 | tf_op jit(solution)/shard_map/all_gather | solution.py:710
  49.0 504.4 %all-reduce.2.cloned.1.call-start = ((), (), s32[]{:S(2)}) async-start(), calls=%async_computation.5 | async-start | bytes 9437184 | tf_op jit(solution)/shard_map/psum | solution.py:808
  205.8 24.0 %collective-permute-start.26 = (bf16[256,1664]{1,0:T(8,128)(2,1)S(1)}, bf16[256,1664]{1,0:T(8,128)(2,1)}, u32[]{:S(2)}, u32[]{:S(2)}) collective-permute-start(bf16[256,1664]{1,0:T(8,128)(2,1)S(1)} %collective-permute-done.19.near_in.refs_4_), channel_id=1, source_target_pairs={{0,1},{1,0},{2,3},{3,2},{4,5},{5,4},{6,7},{7,6},{8,9},{9,8},{10,11... | collective-permute-start | bytes 2555912 | tf_op jit(solution)/shard_map/ppermute | solution.py:32
  226.9 39.0 %collective-permute-start.28 = (bf16[256,1664]{1,0:T(8,128)(2,1)}, bf16[256,1664]{1,0:T(8,128)(2,1)S(1)}, u32[]{:S(2)}, u32[]{:S(2)}) collective-permute-start(bf16[256,1664]{1,0:T(8,128)(2,1)} %collective-permute-done.25.near_in.refs_6_), channel_id=1, source_target_pairs={{0,1},{1,0},{2,3},{3,2},{4,5},{5,4},{6,7},{7,6},{8,9},{9,8},{10,11... | collective-permute-start | bytes 2555912 | tf_op jit(solution)/shard_map/ppermute | solution.py:32
  227.8 36.0 %collective-permute-start.23 = (bf16[256,1664]{1,0:T(8,128)(2,1)}, bf16[256,1664]{1,0:T(8,128)(2,1)S(1)}, u32[]{:S(2)}, u32[]{:S(2)}) collective-permute-start(bf16[256,1664]{1,0:T(8,128)(2,1)} %get-tuple-element.131), channel_id=1, source_target_pairs={{0,1},{1,0},{2,3},{3,2},{4,5},{5,4},{6,7},{7,6},{8,9},{9,8},{10,11... | collective-permute-start | bytes 2555912 | tf_op jit(solution)/shard_map/ppermute | solution.py:32
  228.4 84.5 %collective-permute-start.22 = (bf16[512,1536]{1,0:T(8,128)(2,1)}, bf16[512,1536]{1,0:T(8,128)(2,1)}, u32[]{:S(2)}, u32[]{:S(2)}) collective-permute-start(bf16[512,1536]{1,0:T(8,128)(2,1)} %get-tuple-element.129), channel_id=1, source_target_pairs={{0,8},{8,16},{16,24},{24,0},{1,9},{9,17},{17,25},{25,1},{2,10},{10... | collective-permute-start | bytes 4718600 | tf_op jit(solution)/shard_map/ppermute | solution.py:28
  249.3 37.3 %collective-permute-start.27 = (bf16[256,1664]{1,0:T(8,128)(2,1)}, bf16[256,1664]{1,0:T(8,128)(2,1)S(1)}, u32[]{:S(2)}, u32[]{:S(2)}) collective-permute-start(bf16[256,1664]{1,0:T(8,128)(2,1)} %get-tuple-element.135), channel_id=1, source_target_pairs={{0,1},{1,0},{2,3},{3,2},{4,5},{5,4},{6,7},{7,6},{8,9},{9,8},{10,11... | collective-permute-start | bytes 2555912 | tf_op jit(solution)/shard_map/ppermute | solution.py:32
  286.3 26.6 %collective-permute-start.31 = (bf16[256,1664]{1,0:T(8,128)(2,1)}, bf16[256,1664]{1,0:T(8,128)(2,1)S(1)}, u32[]{:S(2)}, u32[]{:S(2)}) collective-permute-start(bf16[256,1664]{1,0:T(8,128)(2,1)} %get-tuple-element.153), channel_id=1, source_target_pairs={{0,1},{1,0},{2,3},{3,2},{4,5},{5,4},{6,7},{7,6},{8,9},{9,8},{10,11... | collective-permute-start | bytes 2555912 | tf_op jit(solution)/shard_map/ppermute | solution.py:32
  287.9 26.4 %collective-permute-start.30 = (bf16[256,1664]{1,0:T(8,128)(2,1)}, bf16[256,1664]{1,0:T(8,128)(2,1)S(1)}, u32[]{:S(2)}, u32[]{:S(2)}) collective-permute-start(bf16[256,1664]{1,0:T(8,128)(2,1)} %add_convert_fusion.7), channel_id=1, source_target_pairs={{0,8},{8,16},{16,24},{24,0},{1,9},{9,17},{17,25},{25,1},{2,10},{10... | collective-permute-start | bytes 2555912 | tf_op jit(solution)/shard_map/ppermute | solution.py:28
  307.5 29.3 %collective-permute-start.33 = (bf16[2,3,256,1536]{3,2,1,0:T(8,128)(2,1)}, bf16[2,3,256,1536]{3,2,1,0:T(8,128)(2,1)}, u32[]{:S(2)}, u32[]{:S(2)}) collective-permute-start(bf16[2,3,256,1536]{3,2,1,0:T(8,128)(2,1)} %expert_grads.2), channel_id=1, source_target_pairs={{0,2},{2,0},{1,3},{3,1},{4,6},{6,4},{5,7},{7,5},{8,10},{10,8},{9,1... | collective-permute-start | bytes 14155784 | tf_op jit(solution)/shard_map/ppermute | solution.py:32
  315.5 28.7 %collective-permute-start.32 = (bf16[256,1664]{1,0:T(8,128)(2,1)}, bf16[256,1664]{1,0:T(8,128)(2,1)S(1)}, u32[]{:S(2)}, u32[]{:S(2)}) collective-permute-start(bf16[256,1664]{1,0:T(8,128)(2,1)} %add_convert_fusion.6), channel_id=1, source_target_pairs={{0,8},{8,16},{16,24},{24,0},{1,9},{9,17},{17,25},{25,1},{2,10},{10... | collective-permute-start | bytes 2555912 | tf_op jit(solution)/shard_map/ppermute | solution.py:28
  353.9 40.3 %collective-permute-start.29 = (bf16[512,1536]{1,0:T(8,128)(2,1)}, bf16[512,1536]{1,0:T(8,128)(2,1)}, u32[]{:S(2)}, u32[]{:S(2)}) collective-permute-start(bf16[512,1536]{1,0:T(8,128)(2,1)} %add_convert_fusion.3), channel_id=1, source_target_pairs={{0,8},{8,16},{16,24},{24,0},{1,9},{9,17},{17,25},{25,1},{2,10},{10... | collective-permute-start | bytes 4718600 | tf_op jit(solution)/shard_map/ppermute | solution.py:28
  398.4 70.6 %collective-permute-start.36 = (bf16[512,1536]{1,0:T(8,128)(2,1)}, bf16[512,1536]{1,0:T(8,128)(2,1)}, u32[]{:S(2)}, u32[]{:S(2)}) collective-permute-start(bf16[512,1536]{1,0:T(8,128)(2,1)} %add_convert_fusion.2), channel_id=1, source_target_pairs={{0,8},{8,16},{16,24},{24,0},{1,9},{9,17},{17,25},{25,1},{2,10},{10... | collective-permute-start | bytes 4718600 | tf_op jit(solution)/shard_map/ppermute | solution.py:28
  399.2 24.1 %collective-permute-start.43 = (bf16[4,192,768]{2,1,0:T(8,128)(2,1)S(1)}, bf16[4,192,768]{2,1,0:T(8,128)(2,1)S(1)}, u32[]{:S(2)}, u32[]{:S(2)}) collective-permute-start(bf16[4,192,768]{2,1,0:T(8,128)(2,1)S(1)} %constant_dynamic-slice_fusion.1), channel_id=1, source_target_pairs={{0,2},{2,0},{1,3},{3,1},{4,6},{6,4},{5,7},{7,5},{8,10},{10,8},{9,1... | collective-permute-start | bytes 3538952 | tf_op jit(solution)/shard_map/ppermute | solution.py:32
  403.9 25.3 %collective-permute-start.44 = (bf16[4,192,768]{2,1,0:T(8,128)(2,1)}, bf16[4,192,768]{2,1,0:T(8,128)(2,1)}, u32[]{:S(2)}, u32[]{:S(2)}) collective-permute-start(bf16[4,192,768]{2,1,0:T(8,128)(2,1)} %constant_dynamic-slice_fusion), channel_id=1, source_target_pairs={{0,2},{2,0},{1,3},{3,1},{4,6},{6,4},{5,7},{7,5},{8,10},{10,8},{9,1... | collective-permute-start | bytes 3538952 | tf_op jit(solution)/shard_map/ppermute | solution.py:32
  406.9 40.3 %collective-permute-start.38 = (bf16[2,256,512]{2,1,0:T(8,128)(2,1)}, bf16[2,256,512]{2,1,0:T(8,128)(2,1)}, u32[]{:S(2)}, u32[]{:S(2)}) collective-permute-start(bf16[2,256,512]{2,1,0:T(8,128)(2,1)} %fusion.21), channel_id=1, source_target_pairs={{0,4},{4,0},{1,5},{5,1},{2,6},{6,2},{3,7},{7,3},{8,12},{12,8},{9,1... | collective-permute-start | bytes 1572872 | tf_op jit(solution)/shard_map/ppermute | solution.py:28
  424.7 40.0 %all-to-all-start.1 = ((bf16[4,192,768]{2,1,0:T(8,128)(2,1)}), bf16[4,192,768]{2,1,0:T(8,128)(2,1)}, u32[]{:S(2)}, u32[]{:S(2)}) async-start(bf16[4,192,768]{2,1,0:T(8,128)(2,1)} %add_convert_fusion.5), calls=%async_computation.1 | async-start | bytes 2359296 | tf_op jit(solution)/shard_map/all_to_all | solution.py:859
  456.2 77.2 %collective-permute-start.42 = (bf16[512,1536]{1,0:T(8,128)(2,1)}, bf16[512,1536]{1,0:T(8,128)(2,1)}, u32[]{:S(2)}, u32[]{:S(2)}) collective-permute-start(bf16[512,1536]{1,0:T(8,128)(2,1)} %get-tuple-element.284), channel_id=1, source_target_pairs={{0,1},{1,0},{2,3},{3,2},{4,5},{5,4},{6,7},{7,6},{8,9},{9,8},{10,11... | collective-permute-start | bytes 4718600 | tf_op jit(solution)/shard_map/ppermute | solution.py:32
  464.7 33.0 %all-to-all-start.2 = ((bf16[4,192,768]{2,1,0:T(8,128)(2,1)}), bf16[4,192,768]{2,1,0:T(8,128)(2,1)}, u32[]{:S(2)}, u32[]{:S(2)}) async-start(bf16[4,192,768]{2,1,0:T(8,128)(2,1)} %add_convert_fusion.4), calls=%async_computation.2 | async-start | bytes 2359296 | tf_op jit(solution)/shard_map/all_to_all | solution.py:859
  488.1 42.2 %collective-permute-start.41 = (bf16[256,1536]{1,0:T(8,128)(2,1)}, bf16[256,1536]{1,0:T(8,128)(2,1)}, u32[]{:S(2)}, u32[]{:S(2)}) collective-permute-start(bf16[256,1536]{1,0:T(8,128)(2,1)} %slice.122), channel_id=1, source_target_pairs={{0,1},{1,0},{2,3},{3,2},{4,5},{5,4},{6,7},{7,6},{8,9},{9,8},{10,11... | collective-permute-start | bytes 2359304 | tf_op jit(solution)/shard_map/ppermute | solution.py:32
  507.3 29.0 %collective-permute-start.48 = (bf16[1,192,768]{2,1,0:T(8,128)(2,1)}, bf16[1,192,768]{2,1,0:T(8,128)(2,1)}, u32[]{:S(2)}, u32[]{:S(2)}) collective-permute-start(bf16[1,192,768]{2,1,0:T(8,128)(2,1)} %bitcast.132), channel_id=1, source_target_pairs={{0,4},{4,0},{1,5},{5,1},{2,6},{6,2},{3,7},{7,3},{8,12},{12,8},{9,1... | collective-permute-start | bytes 884744 | tf_op jit(solution)/shard_map/ppermute | solution.py:28
  524.5 27.6 %all-to-all-start.3 = ((bf16[4,192,512]{2,1,0:T(8,128)(2,1)}), bf16[4,192,512]{2,1,0:T(8,128)(2,1)}, u32[]{:S(2)}, u32[]{:S(2)}) async-start(bf16[4,192,512]{2,1,0:T(8,128)(2,1)} %add_convert_fusion.9), calls=%async_computation.3 | async-start | bytes 1572864 | tf_op jit(solution)/shard_map/all_to_all | solution.py:859
  532.9 32.3 %collective-permute-start.46 = (bf16[256,1536]{1,0:T(8,128)(2,1)}, bf16[256,1536]{1,0:T(8,128)(2,1)}, u32[]{:S(2)}, u32[]{:S(2)}) collective-permute-start(bf16[256,1536]{1,0:T(8,128)(2,1)} %multiply_convert_fusion), channel_id=1, source_target_pairs={{0,1},{1,0},{2,3},{3,2},{4,5},{5,4},{6,7},{7,6},{8,9},{9,8},{10,11... | collective-permute-start | bytes 2359304 | tf_op jit(solution)/shard_map/ppermute | solution.py:32
  (118 other events, 1321.1 us)
Sparse Core Ops, SparseCore 0:
  49.1 135.2 all-gather.2
  354.3 130.0 all-reduce.1

commit v5 on v4

--- a/solution.py
+++ b/solution.py
@@ -871,7 +871,7 @@
     q_mine, q_theirs, q_came = by_core_halves(grad_q)
     started = anchor(kv_moving, o_theirs, q_theirs)
     o_half, o_came = by_fsdp(o_mine, o_came, started)
-    q_half, q_came = by_fsdp(q_mine, q_came, started)
+    q_half = (q_mine + after(q_came, started).astype(F32)).astype(BF)
     started = anchor(started, o_half, q_half)
 
     kv_grad = after(kv_far, started).astype(F32) + kv_sum[0]
@@ -887,7 +887,9 @@
     grad_kv_w = dot(hidden_one, grad_both, 0, 1).astype(BF)
     kv_mine, kv_theirs, kv_came = by_core_halves(grad_kv_w)
     started = anchor(first_low, small_grad, kv_theirs)
-    kv_half, kv_came = by_fsdp(kv_mine, kv_came, started)
+    kv_half = (kv_mine + after(kv_came, started).astype(F32)).astype(BF)
+    kv_half = jnp.concatenate([q_half, kv_half], axis=2)
+    kv_came = lax.all_to_all(kv_half, "fsdp", 0, 0)
     small_grad = small_grad + after(small_other, started)
     small_other = swap(small_grad, "core")
     started = anchor(kv_half, small_grad)
@@ -895,10 +897,9 @@
     mixed = mix_step(mix_moving, 0, started)
     mix_other = swap(mixed[half:], "tp")
     o_total, o_came = by_chip(o_came, started)
-    q_total, q_came = by_chip(q_came, started)
     small_grad = small_grad + after(small_other, started)
     everyone = ring_gather(small_grad[None], "cx", n_cx, 0)
-    started = anchor(mixed, o_total, q_total, small_grad)
+    started = anchor(mixed, o_total, small_grad)
 
     first_grad = first_low.astype(F32) + after(first_other, started).astype(F32)
     grad_inputs = branch.astype(F32) + norm_backward(
@@ -916,11 +917,11 @@
     if by_core:
         others = swap(after(expert_sum, started), "core")
         parts = [(others, k) for k in range(first_slot)] + parts
-    grad_q = whole_of(q_came, started)
     grad_output = whole_of(o_came, started).T
     started = anchor(out_half, kv_total)
     grad_down, grad_gate, grad_up = place(order[1 + n_z :], parts)
-    grad_kv_w = whole_of(kv_came, started)
+    grad_kv_w = whole_of(kv_came, started, grad_down)
+    grad_q, grad_kv_w = grad_kv_w[:, :q_width], grad_kv_w[:, q_width:]
     out_other = after(out_other, started)
     layer_out = jnp.concatenate(
         [jnp.where(lead, out_half, out_other), jnp.where(lead, out_other, out_half)], axis=0

time: 594 us -> 586 us (0.987)
  waiting for transfers between devices: 133 us -> 161 us
  starting transfers between devices: 122 us -> 100 us
  other arithmetic: 79.7 us -> 69.9 us
    ppermute x24 -> x23, starting transfers between devices: 65.2 us -> 45.8 us  [shift(): return lax.ppermute(v, axis, [(i, (i + by) % n) for i in range(n)])]
    ppermute x31 -> x30, waiting for transfers between devices: 62.2 us -> 77.3 us  [swap(): return lax.ppermute(v, axis, [(0, 1), (1, 0)])]
    ppermute x24 -> x23, waiting for transfers between devices: 55.7 us -> 65.3 us  [shift(): return lax.ppermute(v, axis, [(i, (i + by) % n) for i in range(n)])]
    all_to_all x0 -> x1, waiting for transfers between devices: none -> 9.24 us  [local(): kv_came = lax.all_to_all(kv_half, 'fsdp', 0, 0)]
    all_to_all x3 -> x1, starting transfers between devices: 13.4 us -> 4.53 us  [by_fsdp(): return (half, lax.all_to_all(half, 'fsdp', 0, 0))]
    all_to_all x3 -> x1, waiting for transfers between devices: 8.44 us -> 0.01 us  [by_fsdp(): return (half, lax.all_to_all(half, 'fsdp', 0, 0))]
    ppermute x31 -> x30, starting transfers between devices: 36.8 us -> 37.9 us  [swap(): return lax.ppermute(v, axis, [(0, 1), (1, 0)])]
  transfers between devices with their start and end apart: 62 -> 59, of which waited for: 17 -> 20; matrix products, arithmetic and copies ran while one was open for 20% -> 18% of each run, Pallas kernels for 27% -> 28%
where the time goes in v5:
time: 586 us; the launch traced here: 582 us
  Pallas kernels  173 us (30%)
  waiting for transfers between devices  161 us (27%)
  starting transfers between devices  100 us (17%)
  other arithmetic  69.9 us (12%)
  local copies, waits for them, and re-layouts  43.1 us (7%)
  matrix products  17.3 us (3%)
  between operations  16.6 us (3%)
    pallas_call x4, Pallas kernels, experts(): pl.pallas_call(expert_kernel, name='experts', grid_spec=pltpu.PrefetchSca...  78.7 us
    ppermute x30, waiting for transfers between devices, swap(): return lax.ppermute(v, axis, [(0, 1), (1, 0)])  77.3 us
    ppermute x23, waiting for transfers between devices, shift(): return lax.ppermute(v, axis, [(i, (i + by) % n) for i in range(n)])  65.3 us
    ppermute x23, starting transfers between devices, shift(): return lax.ppermute(v, axis, [(i, (i + by) % n) for i in range(n)])  45.8 us
    ppermute x30, starting transfers between devices, swap(): return lax.ppermute(v, axis, [(0, 1), (1, 0)])  37.9 us
    pallas_call x2, Pallas kernels, expert_grads(): pl.pallas_call(functools.partial(expert_grad_kernel, n_z), name='expert_g...  37.2 us
    unnamed x165, local copies, waits for them, and re-layouts  23.6 us
    pallas_call x1, Pallas kernels, attend_back(): pl.pallas_call(functools.partial(attend_back_kernel, group), name='attend...  20.2 us
  transfers between devices with their start and end apart: 59, of which 20 were waited for; matrix products, arithmetic and copies ran while one was open for 18% of the time, Pallas kernels for 28%

profile of v5, /device:TPU:1, one launch (start us, length us, event | category | flops | bytes accessed | tf_op | source)
XLA Modules:
  0.0 581.9 jit_solution(10108663146057102979)
XLA Ops:
  26.5 6.6 %all-to-all-done = bf16[4,18,384]{2,1,0:T(8,128)(2,1)S(1)} async-done(((bf16[4,18,384]{2,1,0:T(8,128)(2,1)}), bf16[4,18,384]{2,1,0:T(8,128)(2,1)S(1)}, u32[]{:S(2)}, u32[]{:S(2)}) %all-to-all-start) | async-done | bytes 55328 | tf_op jit(solution)/shard_map/all_to_all | solution.py:674
  51.8 9.0 %collective-permute-done.10 = bf16[1,2,256,512]{3,2,1,0:T(8,128)(2,1)S(1)} collective-permute-done((bf16[1,2,256,512]{3,2,1,0:T(8,128)(2,1)S(1)}, bf16[1,2,256,512]{3,2,1,0:T(8,128)(2,1)S(1)}, u32[]{:S(2)}, u32[]{:S(2)}) %collective-permute-start.10) | collective-permute-done | bytes 524320 | tf_op jit(solution)/shard_map/ppermute | solution.py:28
  87.1 9.3 %attend.2 = (bf16[384,512]{1,0:T(8,128)(2,1)S(1)}, f32[2,8,512]{2,1,0:T(8,128)S(1)}) custom-call(s32[4]{0:T(128)S(1)} %pad_add_fusion.info_ref, bf16[768,512]{1,0:T(8,128)(2,1)S(1)} %get-tuple-element.113.q_ref, bf16[4,2,256,512]{3,2,1,0:T(8,128)(2,1)S(1)} %pad_maximum_fusion.kv_ref), custom_call_target="tpu_custom_call" | custom-call | flops 1610612736 | bytes 1835008 | tf_op jit(solution)/shard_map/attend/pallas_call | solution.py:277
  101.5 5.4 collective-permute-start.15
  108.6 6.3 %collective-permute-done.15 = bf16[1,3,96,768]{3,2,1,0:T(8,128)(2,1)} collective-permute-done((bf16[1,3,96,768]{3,2,1,0:T(8,128)(2,1)S(1)}, bf16[1,3,96,768]{3,2,1,0:T(8,128)(2,1)}, u32[]{:S(2)}, u32[]{:S(2)}) %collective-permute-start.15) | collective-permute-done | bytes 442400 | tf_op jit(solution)/shard_map/ppermute | solution.py:32
  119.4 9.2 %attend.3 = (bf16[384,512]{1,0:T(8,128)(2,1)S(1)}, f32[2,8,512]{2,1,0:T(8,128)S(1)}) custom-call(s32[4]{0:T(128)S(1)} %pad_add_fusion.info_ref, bf16[768,512]{1,0:T(8,128)(2,1)S(1)} %copy-done.21, bf16[4,2,256,512]{3,2,1,0:T(8,128)(2,1)S(1)} %pad_maximum_fusion.kv_ref), custom_call_target="tpu_custom_call" | custom-call | flops 1610612736 | bytes 1835008 | tf_op jit(solution)/shard_map/attend/pallas_call | solution.py:277
  136.9 19.4 %collective-permute-done.17 = bf16[256,1536]{1,0:T(8,128)(2,1)} collective-permute-done((bf16[256,1536]{1,0:T(8,128)(2,1)}, bf16[256,1536]{1,0:T(8,128)(2,1)}, u32[]{:S(2)}, u32[]{:S(2)}) %collective-permute-start.17) | collective-permute-done | bytes 786464 | tf_op jit(solution)/shard_map/ppermute | solution.py:32
  167.1 17.8 %collective-permute-done.18.near_in.refs_2_ = bf16[256,1664]{1,0:T(8,128)(2,1)} collective-permute-done((bf16[256,1664]{1,0:T(8,128)(2,1)}, bf16[256,1664]{1,0:T(8,128)(2,1)}, u32[]{:S(2)}, u32[]{:S(2)}) %collective-permute-start.18) | collective-permute-done | bytes 852000 | tf_op jit(solution)/shard_map/ppermute | solution.py:28
  184.8 19.7 %experts.4 = (bf16[256,1664]{1,0:T(8,128)(2,1)}, bf16[256,1664]{1,0:T(8,128)(2,1)}, bf16[512,1536]{1,0:T(8,128)(2,1)}, bf16[512,1024]{1,0:T(8,128)(2,1)}, bf16[5...) custom-call(s32[6]{0:T(128)} %stack.166.info_ref, bf16[256,1664]{1,0:T(8,128)(2,1)} %concatenate.61.near_in.refs_0_, ...), custom_call_target="tpu_custom_call" | custom-call | flops 9663676416 | bytes 22020096 | tf_op jit(solution)/shard_map/experts/pallas_call | solution.py:462
  207.9 19.5 %experts.5 = (bf16[256,1664]{1,0:T(8,128)(2,1)}, bf16[256,1664]{1,0:T(8,128)(2,1)}, bf16[512,1536]{1,0:T(8,128)(2,1)}, bf16[512,1024]{1,0:T(8,128)(2,1)}, bf16[5...) custom-call(s32[6]{0:T(128)} %stack.164.info_ref, bf16[256,1664]{1,0:T(8,128)(2,1)} %collective-permute-done.18.near_in.refs_2_, ...), custom_call_target="tpu_custom_call" | custom-call | flops 96636764160 | bytes 22020096 | tf_op jit(solution)/shard_map/experts/pallas_call | solution.py:462
  229.6 20.1 %experts.6 = (bf16[256,1664]{1,0:T(8,128)(2,1)}, bf16[256,1664]{1,0:T(8,128)(2,1)}, bf16[512,1536]{1,0:T(8,128)(2,1)}, bf16[512,1024]{1,0:T(8,128)(2,1)}, bf16[5...) custom-call(s32[6]{0:T(128)} %stack.174.info_ref, bf16[256,1664]{1,0:T(8,128)(2,1)} %copy-done.77, ...), custom_call_target="tpu_custom_call" | custom-call | flops 96636764160 | bytes 22020096 | tf_op jit(solution)/shard_map/experts/pallas_call | solution.py:462
  250.5 14.5 %collective-permute-done.23 = bf16[256,1664]{1,0:T(8,128)(2,1)S(1)} collective-permute-done((bf16[256,1664]{1,0:T(8,128)(2,1)}, bf16[256,1664]{1,0:T(8,128)(2,1)S(1)}, u32[]{:S(2)}, u32[]{:S(2)}) %collective-permute-start.23) | collective-permute-done | bytes 852000 | tf_op jit(solution)/shard_map/ppermute | solution.py:32
  266.8 19.5 %experts.7 = (bf16[256,1664]{1,0:T(8,128)(2,1)}, bf16[256,1664]{1,0:T(8,128)(2,1)}, bf16[512,1536]{1,0:T(8,128)(2,1)}, bf16[512,1024]{1,0:T(8,128)(2,1)}, bf16[5...) custom-call(s32[6]{0:T(128)} %stack.175.info_ref, bf16[256,1664]{1,0:T(8,128)(2,1)} %collective-permute-done.25.near_in.refs_6_, ...), custom_call_target="tpu_custom_call" | custom-call | flops 96636764160 | bytes 22020096 | tf_op jit(solution)/shard_map/experts/pallas_call | solution.py:462
  289.2 18.6 %expert_grads.2 = bf16[2,3,256,1536]{3,2,1,0:T(8,128)(2,1)} custom-call(s32[9]{0:T(128)} %stack.173.info_ref, bf16[256,1664]{1,0:T(8,128)(2,1)} %concatenate.61.near_in.refs_0_, bf16[256,1664]{1,0:T(8,128)(2,1)} %collective-permute-done.20.far_in.refs_1_, bf16[256,1664]{1,0:T(8,128)(2,1)} %collective-permute-done.18.near_in.refs_2_, ...), custom_call_target="tpu_custom_call" | custom-call | flops 96636764160 | bytes 16777216 | tf_op jit(solution)/shard_map/expert_grads/pallas_call | solution.py:561
  316.8 18.6 %expert_grads.3 = bf16[2,3,256,1536]{3,2,1,0:T(8,128)(2,1)} custom-call(s32[9]{0:T(128)} %stack.173.info_ref, bf16[256,1664]{1,0:T(8,128)(2,1)} %concatenate.61.near_in.refs_0_, bf16[256,1664]{1,0:T(8,128)(2,1)} %collective-permute-done.20.far_in.refs_1_, bf16[256,1664]{1,0:T(8,128)(2,1)} %collective-permute-done.18.near_in.refs_2_, ...), custom_call_target="tpu_custom_call" | custom-call | flops 96636764160 | bytes 16777216 | tf_op jit(solution)/shard_map/expert_grads/pallas_call | solution.py:561
  336.8 7.4 %add_convert_fusion = bf16[2,3,256,1536]{3,2,1,0:T(8,128)(2,1)} fusion(bf16[2,3,256,1536]{3,2,1,0:T(8,128)(2,1)} %collective-permute-done.33, bf16[2,3,256,1536]{3,2,1,0:T(8,128)(2,1)} %expert_grads.3), kind=kLoop, calls=%fused_computation.1 | loop fusion | flops 9437184 | bytes 14155776 | tf_op jit(solution)/shard_map/convert_element_type | solution.py:807
  356.2 12.4 %collective-permute-done.35 = bf16[256,1536]{1,0:T(8,128)(2,1)} collective-permute-done((bf16[256,1536]{1,0:T(8,128)(2,1)}, bf16[256,1536]{1,0:T(8,128)(2,1)}, u32[]{:S(2)}, u32[]{:S(2)}) %collective-permute-start.35) | collective-permute-done | bytes 786464 | tf_op jit(solution)/shard_map/ppermute | solution.py:32
  374.0 20.2 %attend_back.1 = (f32[768,512]{1,0:T(8,128)S(1)}, bf16[4,2,256,512]{3,2,1,0:T(8,128)(2,1)S(1)}) custom-call(s32[4]{0:T(128)S(1)} %pad_add_fusion.info_ref, bf16[768,512]{1,0:T(8,128)(2,1)S(1)} %copy-done.22, bf16[4,2,256,512]{3,2,1,0:T(8,128)(2,1)} %copy-done.6, bf16[768,512]{1,0:T(8,128)(2,1)S(1)} %copy-done.14, ...), custom_call_target="tpu_custom_call" | custom-call | flops 8053063680 | bytes 8126464 | tf_op jit(solution)/shard_map/attend_back/pallas_call | solution.py:355
  406.6 19.7 %collective-permute-start.39 = (bf16[2,256,512]{2,1,0:T(8,128)(2,1)}, bf16[2,256,512]{2,1,0:T(8,128)(2,1)}, u32[]{:S(2)}, u32[]{:S(2)}) collective-permute-start(bf16[2,256,512]{2,1,0:T(8,128)(2,1)} %fusion.21), channel_id=1, source_target_pairs={{0,4},{4,0},{1,5},{5,1},{2,6},{6,2},{3,7},{7,3},{8,12},{12,8},{9,1... | collective-permute-start | bytes 1572872 | tf_op jit(solution)/shard_map/ppermute | solution.py:28
  435.2 14.8 %collective-permute-done.39 = bf16[2,256,512]{2,1,0:T(8,128)(2,1)} collective-permute-done((bf16[2,256,512]{2,1,0:T(8,128)(2,1)}, bf16[2,256,512]{2,1,0:T(8,128)(2,1)}, u32[]{:S(2)}, u32[]{:S(2)}) %collective-permute-start.39) | collective-permute-done | bytes 524320 | tf_op jit(solution)/shard_map/ppermute | solution.py:28
  500.5 14.6 %collective-permute-done.42 = bf16[256,1536]{1,0:T(8,128)(2,1)} collective-permute-done((bf16[256,1536]{1,0:T(8,128)(2,1)}, bf16[256,1536]{1,0:T(8,128)(2,1)}, u32[]{:S(2)}, u32[]{:S(2)}) %collective-permute-start.42) | collective-permute-done | bytes 786464 | tf_op jit(solution)/shard_map/ppermute | solution.py:32
  532.4 9.2 %all-to-all-done.2 = bf16[4,192,1280]{2,1,0:T(8,128)(2,1)} async-done(((bf16[4,192,1280]{2,1,0:T(8,128)(2,1)}), bf16[4,192,1280]{2,1,0:T(8,128)(2,1)}, u32[]{:S(2)}, u32[]{:S(2)}) %all-to-all-start.2) | async-done | bytes 1966112 | tf_op jit(solution)/shard_map/all_to_all | solution.py:892
  545.7 10.0 %collective-permute-done.48 = bf16[1,192,1280]{2,1,0:T(8,128)(2,1)S(1)} collective-permute-done((bf16[1,192,1280]{2,1,0:T(8,128)(2,1)S(1)}, bf16[1,192,1280]{2,1,0:T(8,128)(2,1)S(1)}, u32[]{:S(2)}, u32[]{:S(2)}) %collective-permute-start.48) | collective-permute-done | bytes 491552 | tf_op jit(solution)/shard_map/ppermute | solution.py:28
  555.8 11.4 %place.1 = (f32[4,256,1536]{2,1,0:T(8,128)}, f32[4,1536,256]{2,1,0:T(8,128)}, f32[4,1536,256]{2,1,0:T(8,128)}) custom-call(s32[4]{0:T(128)S(1)} %pad_add_fusion.2.info_ref, bf16[2,3,256,1536]{3,2,1,0:T(8,128)(2,1)} %collective-permute-done.49.refs_0_.refs_1_, bf16[2,3,256,1536]{3,2,1,0:T(8,128)(2,1)} %collective-permute-done.49.refs_0_.refs_1_, ...), custom_call_target="tpu_custom_call" | custom-call | bytes 28311552 | tf_op jit(solution)/shard_map/place/pallas_call | solution.py:597
  (412 shorter events, 232.1 us)
Async XLA Ops:
  9.2 24.5 %collective-permute-start = (bf16[192,512]{1,0:T(8,128)(2,1)S(1)}, bf16[192,512]{1,0:T(8,128)(2,1)S(1)}, u32[]{:S(2)}, u32[]{:S(2)}) collective-permute-start(bf16[192,512]{1,0:T(8,128)(2,1)S(1)} %constant_dynamic-slice_fusion.5), channel_id=1, source_target_pairs={{0,8},{8,16},{16,24},{24,0},{1,9},{9,17},{17,25},{25,1},{2,10},{10... | collective-permute-start | bytes 589832 | tf_op jit(solution)/shard_map/ppermute | solution.py:28
  20.8 186.2 %all-gather.3.cloned.1.call-start = ((), (), s32[]{:S(2)}) async-start(), calls=%async_computation.5 | async-start | bytes 7077888 | tf_op jit(solution)/shard_map/all_gather | solution.py:710
  49.0 483.4 %all-reduce.2.cloned.1.call-start = ((), (), s32[]{:S(2)}) async-start(), calls=%async_computation.4 | async-start | bytes 9437184 | tf_op jit(solution)/shard_map/psum | solution.py:808
  61.9 23.4 %collective-permute-start.11 = (bf16[2,2,256,512]{3,2,1,0:T(8,128)(2,1)}, bf16[2,2,256,512]{3,2,1,0:T(8,128)(2,1)}, u32[]{:S(2)}, u32[]{:S(2)}) collective-permute-start(bf16[2,2,256,512]{3,2,1,0:T(8,128)(2,1)} %pad_maximum_fusion.3), channel_id=1, source_target_pairs={{0,2},{2,0},{1,3},{3,1},{4,6},{6,4},{5,7},{7,5},{8,10},{10,8},{9,1... | collective-permute-start | bytes 3145736 | tf_op jit(solution)/shard_map/ppermute | solution.py:32
  161.5 23.4 %collective-permute-start.18 = (bf16[256,1664]{1,0:T(8,128)(2,1)}, bf16[256,1664]{1,0:T(8,128)(2,1)}, u32[]{:S(2)}, u32[]{:S(2)}) collective-permute-start(bf16[256,1664]{1,0:T(8,128)(2,1)} %concatenate.61.near_in.refs_0_), channel_id=1, source_target_pairs={{0,8},{8,16},{16,24},{24,0},{1,9},{9,17},{17,25},{25,1},{2,10},{10... | collective-permute-start | bytes 2555912 | tf_op jit(solution)/shard_map/ppermute | solution.py:28
  228.1 37.8 %collective-permute-start.28 = (bf16[256,1664]{1,0:T(8,128)(2,1)}, bf16[256,1664]{1,0:T(8,128)(2,1)S(1)}, u32[]{:S(2)}, u32[]{:S(2)}) collective-permute-start(bf16[256,1664]{1,0:T(8,128)(2,1)} %collective-permute-done.25.near_in.refs_6_), channel_id=1, source_target_pairs={{0,1},{1,0},{2,3},{3,2},{4,5},{5,4},{6,7},{7,6},{8,9},{9,8},{10,11... | collective-permute-start | bytes 2555912 | tf_op jit(solution)/shard_map/ppermute | solution.py:32
  228.9 36.0 %collective-permute-start.23 = (bf16[256,1664]{1,0:T(8,128)(2,1)}, bf16[256,1664]{1,0:T(8,128)(2,1)S(1)}, u32[]{:S(2)}, u32[]{:S(2)}) collective-permute-start(bf16[256,1664]{1,0:T(8,128)(2,1)} %get-tuple-element.129), channel_id=1, source_target_pairs={{0,1},{1,0},{2,3},{3,2},{4,5},{5,4},{6,7},{7,6},{8,9},{9,8},{10,11... | collective-permute-start | bytes 2555912 | tf_op jit(solution)/shard_map/ppermute | solution.py:32
  229.6 83.0 %collective-permute-start.22 = (bf16[512,1536]{1,0:T(8,128)(2,1)}, bf16[512,1536]{1,0:T(8,128)(2,1)}, u32[]{:S(2)}, u32[]{:S(2)}) collective-permute-start(bf16[512,1536]{1,0:T(8,128)(2,1)} %get-tuple-element.127), channel_id=1, source_target_pairs={{0,8},{8,16},{16,24},{24,0},{1,9},{9,17},{17,25},{25,1},{2,10},{10... | collective-permute-start | bytes 4718600 | tf_op jit(solution)/shard_map/ppermute | solution.py:28
  249.6 37.5 %collective-permute-start.27 = (bf16[256,1664]{1,0:T(8,128)(2,1)}, bf16[256,1664]{1,0:T(8,128)(2,1)S(1)}, u32[]{:S(2)}, u32[]{:S(2)}) collective-permute-start(bf16[256,1664]{1,0:T(8,128)(2,1)} %get-tuple-element.133), channel_id=1, source_target_pairs={{0,1},{1,0},{2,3},{3,2},{4,5},{5,4},{6,7},{7,6},{8,9},{9,8},{10,11... | collective-permute-start | bytes 2555912 | tf_op jit(solution)/shard_map/ppermute | solution.py:32
  286.3 26.3 %collective-permute-start.31 = (bf16[256,1664]{1,0:T(8,128)(2,1)}, bf16[256,1664]{1,0:T(8,128)(2,1)S(1)}, u32[]{:S(2)}, u32[]{:S(2)}) collective-permute-start(bf16[256,1664]{1,0:T(8,128)(2,1)} %get-tuple-element.151), channel_id=1, source_target_pairs={{0,1},{1,0},{2,3},{3,2},{4,5},{5,4},{6,7},{7,6},{8,9},{9,8},{10,11... | collective-permute-start | bytes 2555912 | tf_op jit(solution)/shard_map/ppermute | solution.py:32
  287.5 26.9 %collective-permute-start.30 = (bf16[256,1664]{1,0:T(8,128)(2,1)S(1)}, bf16[256,1664]{1,0:T(8,128)(2,1)S(1)}, u32[]{:S(2)}, u32[]{:S(2)}) collective-permute-start(bf16[256,1664]{1,0:T(8,128)(2,1)S(1)} %add_convert_fusion.7), channel_id=1, source_target_pairs={{0,8},{8,16},{16,24},{24,0},{1,9},{9,17},{17,25},{25,1},{2,10},{10... | collective-permute-start | bytes 2555912 | tf_op jit(solution)/shard_map/ppermute | solution.py:28
  307.8 29.0 %collective-permute-start.33 = (bf16[2,3,256,1536]{3,2,1,0:T(8,128)(2,1)}, bf16[2,3,256,1536]{3,2,1,0:T(8,128)(2,1)}, u32[]{:S(2)}, u32[]{:S(2)}) collective-permute-start(bf16[2,3,256,1536]{3,2,1,0:T(8,128)(2,1)} %expert_grads.2), channel_id=1, source_target_pairs={{0,2},{2,0},{1,3},{3,1},{4,6},{6,4},{5,7},{7,5},{8,10},{10,8},{9,1... | collective-permute-start | bytes 14155784 | tf_op jit(solution)/shard_map/ppermute | solution.py:32
  315.6 28.7 %collective-permute-start.32 = (bf16[256,1664]{1,0:T(8,128)(2,1)}, bf16[256,1664]{1,0:T(8,128)(2,1)S(1)}, u32[]{:S(2)}, u32[]{:S(2)}) collective-permute-start(bf16[256,1664]{1,0:T(8,128)(2,1)} %add_convert_fusion.6), channel_id=1, source_target_pairs={{0,8},{8,16},{16,24},{24,0},{1,9},{9,17},{17,25},{25,1},{2,10},{10... | collective-permute-start | bytes 2555912 | tf_op jit(solution)/shard_map/ppermute | solution.py:28
  353.9 40.5 %collective-permute-start.29 = (bf16[512,1536]{1,0:T(8,128)(2,1)}, bf16[512,1536]{1,0:T(8,128)(2,1)}, u32[]{:S(2)}, u32[]{:S(2)}) collective-permute-start(bf16[512,1536]{1,0:T(8,128)(2,1)} %add_convert_fusion.3), channel_id=1, source_target_pairs={{0,8},{8,16},{16,24},{24,0},{1,9},{9,17},{17,25},{25,1},{2,10},{10... | collective-permute-start | bytes 4718600 | tf_op jit(solution)/shard_map/ppermute | solution.py:28
  398.7 69.0 %collective-permute-start.36 = (bf16[512,1536]{1,0:T(8,128)(2,1)}, bf16[512,1536]{1,0:T(8,128)(2,1)}, u32[]{:S(2)}, u32[]{:S(2)}) collective-permute-start(bf16[512,1536]{1,0:T(8,128)(2,1)} %add_convert_fusion.2), channel_id=1, source_target_pairs={{0,8},{8,16},{16,24},{24,0},{1,9},{9,17},{17,25},{25,1},{2,10},{10... | collective-permute-start | bytes 4718600 | tf_op jit(solution)/shard_map/ppermute | solution.py:28
  402.8 23.5 %collective-permute-start.37 = (bf16[4,192,768]{2,1,0:T(8,128)(2,1)S(1)}, bf16[4,192,768]{2,1,0:T(8,128)(2,1)S(1)}, u32[]{:S(2)}, u32[]{:S(2)}) collective-permute-start(bf16[4,192,768]{2,1,0:T(8,128)(2,1)S(1)} %constant_dynamic-slice_fusion.2), channel_id=1, source_target_pairs={{0,2},{2,0},{1,3},{3,1},{4,6},{6,4},{5,7},{7,5},{8,10},{10,8},{9,1... | collective-permute-start | bytes 3538952 | tf_op jit(solution)/shard_map/ppermute | solution.py:32
  406.6 43.4 %collective-permute-start.39 = (bf16[2,256,512]{2,1,0:T(8,128)(2,1)}, bf16[2,256,512]{2,1,0:T(8,128)(2,1)}, u32[]{:S(2)}, u32[]{:S(2)}) collective-permute-start(bf16[2,256,512]{2,1,0:T(8,128)(2,1)} %fusion.21), channel_id=1, source_target_pairs={{0,4},{4,0},{1,5},{5,1},{2,6},{6,2},{3,7},{7,3},{8,12},{12,8},{9,1... | collective-permute-start | bytes 1572872 | tf_op jit(solution)/shard_map/ppermute | solution.py:28
  428.6 50.7 %all-to-all-start.1 = ((bf16[4,192,768]{2,1,0:T(8,128)(2,1)}), bf16[4,192,768]{2,1,0:T(8,128)(2,1)}, u32[]{:S(2)}, u32[]{:S(2)}) async-start(bf16[4,192,768]{2,1,0:T(8,128)(2,1)} %add_convert_fusion.4), calls=%async_computation.1 | async-start | bytes 2359296 | tf_op jit(solution)/shard_map/all_to_all | solution.py:859
  460.3 58.5 %collective-permute-start.43 = (bf16[512,1536]{1,0:T(8,128)(2,1)}, bf16[512,1536]{1,0:T(8,128)(2,1)}, u32[]{:S(2)}, u32[]{:S(2)}) collective-permute-start(bf16[512,1536]{1,0:T(8,128)(2,1)} %get-tuple-element.256), channel_id=1, source_target_pairs={{0,1},{1,0},{2,3},{3,2},{4,5},{5,4},{6,7},{7,6},{8,9},{9,8},{10,11... | collective-permute-start | bytes 4718600 | tf_op jit(solution)/shard_map/ppermute | solution.py:32
  475.0 40.2 %collective-permute-start.42 = (bf16[256,1536]{1,0:T(8,128)(2,1)}, bf16[256,1536]{1,0:T(8,128)(2,1)}, u32[]{:S(2)}, u32[]{:S(2)}) collective-permute-start(bf16[256,1536]{1,0:T(8,128)(2,1)} %slice.129), channel_id=1, source_target_pairs={{0,1},{1,0},{2,3},{3,2},{4,5},{5,4},{6,7},{7,6},{8,9},{9,8},{10,11... | collective-permute-start | bytes 2359304 | tf_op jit(solution)/shard_map/ppermute | solution.py:32
  487.2 34.6 %collective-permute-start.51 = (bf16[1,192,768]{2,1,0:T(8,128)(2,1)}, bf16[1,192,768]{2,1,0:T(8,128)(2,1)}, u32[]{:S(2)}, u32[]{:S(2)}) collective-permute-start(bf16[1,192,768]{2,1,0:T(8,128)(2,1)} %bitcast.130), channel_id=1, source_target_pairs={{0,4},{4,0},{1,5},{5,1},{2,6},{6,2},{3,7},{7,3},{8,12},{12,8},{9,1... | collective-permute-start | bytes 884744 | tf_op jit(solution)/shard_map/ppermute | solution.py:28
  492.0 49.7 %all-to-all-start.2 = ((bf16[4,192,1280]{2,1,0:T(8,128)(2,1)}), bf16[4,192,1280]{2,1,0:T(8,128)(2,1)}, u32[]{:S(2)}, u32[]{:S(2)}) async-start(bf16[4,192,1280]{2,1,0:T(8,128)(2,1)} %pad_maximum_fusion.1), calls=%async_computation.2 | async-start | bytes 3932160 | tf_op jit(solution)/shard_map/all_to_all | solution.py:892
  517.7 28.0 %collective-permute-start.46 = (bf16[256,1536]{1,0:T(8,128)(2,1)}, bf16[256,1536]{1,0:T(8,128)(2,1)}, u32[]{:S(2)}, u32[]{:S(2)}) collective-permute-start(bf16[256,1536]{1,0:T(8,128)(2,1)} %multiply_convert_fusion), channel_id=1, source_target_pairs={{0,1},{1,0},{2,3},{3,2},{4,5},{5,4},{6,7},{7,6},{8,9},{9,8},{10,11... | collective-permute-start | bytes 2359304 | tf_op jit(solution)/shard_map/ppermute | solution.py:32
  532.4 23.4 %collective-permute-start.49 = (bf16[2,3,256,1536]{3,2,1,0:T(8,128)(2,1)}, bf16[2,3,256,1536]{3,2,1,0:T(8,128)(2,1)}, u32[]{:S(2)}, u32[]{:S(2)}) collective-permute-start(bf16[2,3,256,1536]{3,2,1,0:T(8,128)(2,1)} %all-reduce.2.cloned.1.call-done.refs_2_.refs_3_), channel_id=1, source_target_pairs={{0,2},{2,0},{1,3},{3,1},{4,6},{6,4},{5,7},{7,5},{8,10},{10,8},{9,1... | collective-permute-start | bytes 14155784 | tf_op jit(solution)/shard_map/ppermute | solution.py:32
  (115 other events, 1239.7 us)
Sparse Core Ops, SparseCore 0:
  49.1 118.6 all-gather.2
  354.2 135.6 all-reduce.1

commit v6 on v5

--- a/solution.py
+++ b/solution.py
@@ -910,9 +910,9 @@
     out_other = swap(out_half, "tp")
     kv_total, kv_came = by_chip(kv_came, started)
     total = jnp.sum(after(everyone, started), axis=0)
-    small_mine = jnp.sum(
-        lax.all_to_all(total, "fsdp", 1, 0, tiled=True).reshape(n_z, 2 + E, shard), axis=0
-    )
+    small_mine = pick(total, z, n_z, 1)
+    for s in range(1, n_z):
+        small_mine = small_mine + shift(pick(total, (z + s) % n_z, n_z, 1), "fsdp", n_z, s)
     parts = [(expert_sum, k) for k in range(held - first_slot)]
     if by_core:
         others = swap(after(expert_sum, started), "core")

time: 586 us -> 597 us (1.019)
  waiting for transfers between devices: 161 us -> 173 us
    ppermute x23 -> x26, waiting for transfers between devices: 65.3 us -> 104 us  [shift(): return lax.ppermute(v, axis, [(i, (i + by) % n) for i in range(n)])]
    ppermute x30, waiting for transfers between devices: 77.3 us -> 62.2 us  [swap(): return lax.ppermute(v, axis, [(0, 1), (1, 0)])]
    all_to_all x1, waiting for transfers between devices: 9.24 us -> 0.01 us  [local(): kv_came = lax.all_to_all(kv_half, 'fsdp', 0, 0)]
    ppermute x23 -> x26, starting transfers between devices: 45.8 us -> 47.7 us  [shift(): return lax.ppermute(v, axis, [(i, (i + by) % n) for i in range(n)])]
    unnamed x165 -> x169, local copies, waits for them, and re-layouts: 23.6 us -> 23.3 us
  transfers between devices with their start and end apart: 59 -> 61, of which waited for: 20 -> 19; matrix products, arithmetic and copies ran while one was open for 18% -> 17% of each run, Pallas kernels for 28% -> 27%
where the time goes in v6:
time: 597 us; the launch traced here: 591 us
  waiting for transfers between devices  173 us (29%)
  Pallas kernels  173 us (29%)
  starting transfers between devices  98.8 us (17%)
  other arithmetic  72.4 us (12%)
  local copies, waits for them, and re-layouts  40.4 us (7%)
  matrix products  17.3 us (3%)
  between operations  16.5 us (3%)
    ppermute x26, waiting for transfers between devices, shift(): return lax.ppermute(v, axis, [(i, (i + by) % n) for i in range(n)])  104 us
    pallas_call x4, Pallas kernels, experts(): pl.pallas_call(expert_kernel, name='experts', grid_spec=pltpu.PrefetchSca...  78.1 us
    ppermute x30, waiting for transfers between devices, swap(): return lax.ppermute(v, axis, [(0, 1), (1, 0)])  62.2 us
    ppermute x26, starting transfers between devices, shift(): return lax.ppermute(v, axis, [(i, (i + by) % n) for i in range(n)])  47.7 us
    ppermute x30, starting transfers between devices, swap(): return lax.ppermute(v, axis, [(0, 1), (1, 0)])  38.5 us
    pallas_call x2, Pallas kernels, expert_grads(): pl.pallas_call(functools.partial(expert_grad_kernel, n_z), name='expert_g...  37 us
    unnamed x169, local copies, waits for them, and re-layouts  23.3 us
    pallas_call x1, Pallas kernels, attend_back(): pl.pallas_call(functools.partial(attend_back_kernel, group), name='attend...  20.1 us
  transfers between devices with their start and end apart: 61, of which 19 were waited for; matrix products, arithmetic and copies ran while one was open for 17% of the time, Pallas kernels for 27%

profile of v6, /device:TPU:1, one launch (start us, length us, event | category | flops | bytes accessed | tf_op | source)
XLA Modules:
  0.0 591.0 jit_solution(3131199608465406866)
XLA Ops:
  26.4 6.6 %all-to-all-done = bf16[4,18,384]{2,1,0:T(8,128)(2,1)S(1)} async-done(((bf16[4,18,384]{2,1,0:T(8,128)(2,1)}), bf16[4,18,384]{2,1,0:T(8,128)(2,1)S(1)}, u32[]{:S(2)}, u32[]{:S(2)}) %all-to-all-start) | async-done | bytes 55328 | tf_op jit(solution)/shard_map/all_to_all | solution.py:674
  51.8 9.0 %collective-permute-done.10 = bf16[1,2,256,512]{3,2,1,0:T(8,128)(2,1)S(1)} collective-permute-done((bf16[1,2,256,512]{3,2,1,0:T(8,128)(2,1)S(1)}, bf16[1,2,256,512]{3,2,1,0:T(8,128)(2,1)S(1)}, u32[]{:S(2)}, u32[]{:S(2)}) %collective-permute-start.10) | collective-permute-done | bytes 524320 | tf_op jit(solution)/shard_map/ppermute | solution.py:28
  87.1 9.7 %attend.2 = (bf16[384,512]{1,0:T(8,128)(2,1)S(1)}, f32[2,8,512]{2,1,0:T(8,128)S(1)}) custom-call(s32[4]{0:T(128)S(1)} %pad_add_fusion.info_ref, bf16[768,512]{1,0:T(8,128)(2,1)S(1)} %get-tuple-element.113.q_ref, bf16[4,2,256,512]{3,2,1,0:T(8,128)(2,1)S(1)} %pad_maximum_fusion.kv_ref), custom_call_target="tpu_custom_call" | custom-call | flops 1610612736 | bytes 1835008 | tf_op jit(solution)/shard_map/attend/pallas_call | solution.py:277
  101.5 5.7 collective-permute-start.15
  108.9 6.0 %collective-permute-done.15 = bf16[1,3,96,768]{3,2,1,0:T(8,128)(2,1)} collective-permute-done((bf16[1,3,96,768]{3,2,1,0:T(8,128)(2,1)S(1)}, bf16[1,3,96,768]{3,2,1,0:T(8,128)(2,1)}, u32[]{:S(2)}, u32[]{:S(2)}) %collective-permute-start.15) | collective-permute-done | bytes 442400 | tf_op jit(solution)/shard_map/ppermute | solution.py:32
  119.4 9.2 %attend.3 = (bf16[384,512]{1,0:T(8,128)(2,1)S(1)}, f32[2,8,512]{2,1,0:T(8,128)S(1)}) custom-call(s32[4]{0:T(128)S(1)} %pad_add_fusion.info_ref, bf16[768,512]{1,0:T(8,128)(2,1)S(1)} %copy-done.21, bf16[4,2,256,512]{3,2,1,0:T(8,128)(2,1)S(1)} %pad_maximum_fusion.kv_ref), custom_call_target="tpu_custom_call" | custom-call | flops 1610612736 | bytes 1835008 | tf_op jit(solution)/shard_map/attend/pallas_call | solution.py:277
  136.9 19.4 %collective-permute-done.17 = bf16[256,1536]{1,0:T(8,128)(2,1)} collective-permute-done((bf16[256,1536]{1,0:T(8,128)(2,1)}, bf16[256,1536]{1,0:T(8,128)(2,1)}, u32[]{:S(2)}, u32[]{:S(2)}) %collective-permute-start.17) | collective-permute-done | bytes 786464 | tf_op jit(solution)/shard_map/ppermute | solution.py:32
  167.6 20.9 %collective-permute-done.18.near_in.refs_2_ = bf16[256,1664]{1,0:T(8,128)(2,1)} collective-permute-done((bf16[256,1664]{1,0:T(8,128)(2,1)S(1)}, bf16[256,1664]{1,0:T(8,128)(2,1)}, u32[]{:S(2)}, u32[]{:S(2)}) %collective-permute-start.18) | collective-permute-done | bytes 852000 | tf_op jit(solution)/shard_map/ppermute | solution.py:28
  188.8 19.5 %experts.4 = (bf16[256,1664]{1,0:T(8,128)(2,1)}, bf16[256,1664]{1,0:T(8,128)(2,1)}, bf16[512,1536]{1,0:T(8,128)(2,1)}, bf16[512,1024]{1,0:T(8,128)(2,1)}, bf16[5...) custom-call(s32[6]{0:T(128)} %stack.166.info_ref, bf16[256,1664]{1,0:T(8,128)(2,1)} %copy-done.52, ...), custom_call_target="tpu_custom_call" | custom-call | flops 9663676416 | bytes 22020096 | tf_op jit(solution)/shard_map/experts/pallas_call | solution.py:462
  211.8 19.5 %experts.5 = (bf16[256,1664]{1,0:T(8,128)(2,1)}, bf16[256,1664]{1,0:T(8,128)(2,1)}, bf16[512,1536]{1,0:T(8,128)(2,1)}, bf16[512,1024]{1,0:T(8,128)(2,1)}, bf16[5...) custom-call(s32[6]{0:T(128)} %stack.164.info_ref, bf16[256,1664]{1,0:T(8,128)(2,1)} %collective-permute-done.18.near_in.refs_2_, ...), custom_call_target="tpu_custom_call" | custom-call | flops 96636764160 | bytes 22020096 | tf_op jit(solution)/shard_map/experts/pallas_call | solution.py:462
  233.6 19.6 %experts.6 = (bf16[256,1664]{1,0:T(8,128)(2,1)}, bf16[256,1664]{1,0:T(8,128)(2,1)}, bf16[512,1536]{1,0:T(8,128)(2,1)}, bf16[512,1024]{1,0:T(8,128)(2,1)}, bf16[5...) custom-call(s32[6]{0:T(128)} %stack.174.info_ref, bf16[256,1664]{1,0:T(8,128)(2,1)} %copy-done.79, ...), custom_call_target="tpu_custom_call" | custom-call | flops 96636764160 | bytes 22020096 | tf_op jit(solution)/shard_map/experts/pallas_call | solution.py:462
  254.1 14.7 %collective-permute-done.23 = bf16[256,1664]{1,0:T(8,128)(2,1)S(1)} collective-permute-done((bf16[256,1664]{1,0:T(8,128)(2,1)}, bf16[256,1664]{1,0:T(8,128)(2,1)S(1)}, u32[]{:S(2)}, u32[]{:S(2)}) %collective-permute-start.23) | collective-permute-done | bytes 852000 | tf_op jit(solution)/shard_map/ppermute | solution.py:32
  270.0 19.5 %experts.7 = (bf16[256,1664]{1,0:T(8,128)(2,1)}, bf16[256,1664]{1,0:T(8,128)(2,1)}, bf16[512,1536]{1,0:T(8,128)(2,1)}, bf16[512,1024]{1,0:T(8,128)(2,1)}, bf16[5...) custom-call(s32[6]{0:T(128)} %stack.175.info_ref, bf16[256,1664]{1,0:T(8,128)(2,1)} %collective-permute-done.25.near_in.refs_6_, ...), custom_call_target="tpu_custom_call" | custom-call | flops 96636764160 | bytes 22020096 | tf_op jit(solution)/shard_map/experts/pallas_call | solution.py:462
  294.1 18.6 %expert_grads.2 = bf16[2,3,256,1536]{3,2,1,0:T(8,128)(2,1)} custom-call(s32[9]{0:T(128)} %stack.173.info_ref, bf16[256,1664]{1,0:T(8,128)(2,1)} %copy-done.52, bf16[256,1664]{1,0:T(8,128)(2,1)} %collective-permute-done.20.far_in.refs_1_, bf16[256,1664]{1,0:T(8,128)(2,1)} %collective-permute-done.18.near_in.refs_2_, bf16[256,1664]{1,0:T(8,128)(2,1)} %copy-done.80, ...), custom_call_target="tpu_custom_call" | custom-call | flops 96636764160 | bytes 16777216 | tf_op jit(solution)/shard_map/expert_grads/pallas_call | solution.py:561
  321.9 18.5 %expert_grads.3 = bf16[2,3,256,1536]{3,2,1,0:T(8,128)(2,1)} custom-call(s32[9]{0:T(128)} %stack.173.info_ref, bf16[256,1664]{1,0:T(8,128)(2,1)} %copy-done.52, bf16[256,1664]{1,0:T(8,128)(2,1)} %collective-permute-done.20.far_in.refs_1_, bf16[256,1664]{1,0:T(8,128)(2,1)} %collective-permute-done.18.near_in.refs_2_, bf16[256,1664]{1,0:T(8,128)(2,1)} %copy-done.80, ...), custom_call_target="tpu_custom_call" | custom-call | flops 96636764160 | bytes 16777216 | tf_op jit(solution)/shard_map/expert_grads/pallas_call | solution.py:561
  341.8 7.4 %add_convert_fusion = bf16[2,3,256,1536]{3,2,1,0:T(8,128)(2,1)} fusion(bf16[2,3,256,1536]{3,2,1,0:T(8,128)(2,1)} %collective-permute-done.33, bf16[2,3,256,1536]{3,2,1,0:T(8,128)(2,1)} %expert_grads.3), kind=kLoop, calls=%fused_computation.1 | loop fusion | flops 9437184 | bytes 14155776 | tf_op jit(solution)/shard_map/convert_element_type | solution.py:807
  361.2 12.4 %collective-permute-done.35 = bf16[256,1536]{1,0:T(8,128)(2,1)} collective-permute-done((bf16[256,1536]{1,0:T(8,128)(2,1)}, bf16[256,1536]{1,0:T(8,128)(2,1)}, u32[]{:S(2)}, u32[]{:S(2)}) %collective-permute-start.35) | collective-permute-done | bytes 786464 | tf_op jit(solution)/shard_map/ppermute | solution.py:32
  378.9 20.1 %attend_back.1 = (f32[768,512]{1,0:T(8,128)S(1)}, bf16[4,2,256,512]{3,2,1,0:T(8,128)(2,1)S(1)}) custom-call(s32[4]{0:T(128)S(1)} %pad_add_fusion.info_ref, bf16[768,512]{1,0:T(8,128)(2,1)S(1)} %copy-done.22, bf16[4,2,256,512]{3,2,1,0:T(8,128)(2,1)} %copy-done.6, bf16[768,512]{1,0:T(8,128)(2,1)S(1)} %copy-done.14, ...), custom_call_target="tpu_custom_call" | custom-call | flops 8053063680 | bytes 8126464 | tf_op jit(solution)/shard_map/attend_back/pallas_call | solution.py:355
  411.5 14.6 %collective-permute-start.39 = (bf16[2,256,512]{2,1,0:T(8,128)(2,1)}, bf16[2,256,512]{2,1,0:T(8,128)(2,1)}, u32[]{:S(2)}, u32[]{:S(2)}) collective-permute-start(bf16[2,256,512]{2,1,0:T(8,128)(2,1)} %fusion.21), channel_id=1, source_target_pairs={{0,4},{4,0},{1,5},{5,1},{2,6},{6,2},{3,7},{7,3},{8,12},{12,8},{9,1... | collective-permute-start | bytes 1572872 | tf_op jit(solution)/shard_map/ppermute | solution.py:28
  435.2 14.5 %collective-permute-done.39 = bf16[2,256,512]{2,1,0:T(8,128)(2,1)} collective-permute-done((bf16[2,256,512]{2,1,0:T(8,128)(2,1)}, bf16[2,256,512]{2,1,0:T(8,128)(2,1)}, u32[]{:S(2)}, u32[]{:S(2)}) %collective-permute-start.39) | collective-permute-done | bytes 524320 | tf_op jit(solution)/shard_map/ppermute | solution.py:28
  493.3 22.3 %collective-permute-done.50 = f32[18,384]{1,0:T(8,128)S(1)} collective-permute-done((f32[18,384]{1,0:T(8,128)S(1)}, f32[18,384]{1,0:T(8,128)S(1)}, u32[]{:S(2)}, u32[]{:S(2)}) %collective-permute-start.50) | collective-permute-done | bytes 27680 | tf_op jit(solution)/shard_map/ppermute | solution.py:28
  519.0 12.5 %collective-permute-done.49 = f32[18,384]{1,0:T(8,128)S(1)} collective-permute-done((f32[18,384]{1,0:T(8,128)S(1)}, f32[18,384]{1,0:T(8,128)S(1)}, u32[]{:S(2)}, u32[]{:S(2)}) %collective-permute-start.49) | collective-permute-done | bytes 27680 | tf_op jit(solution)/shard_map/ppermute | solution.py:28
  555.2 11.1 %collective-permute-done.51 = bf16[1,192,1280]{2,1,0:T(8,128)(2,1)S(1)} collective-permute-done((bf16[1,192,1280]{2,1,0:T(8,128)(2,1)S(1)}, bf16[1,192,1280]{2,1,0:T(8,128)(2,1)S(1)}, u32[]{:S(2)}, u32[]{:S(2)}) %collective-permute-start.51) | collective-permute-done | bytes 491552 | tf_op jit(solution)/shard_map/ppermute | solution.py:28
  566.3 11.4 %place.1 = (f32[4,256,1536]{2,1,0:T(8,128)}, f32[4,1536,256]{2,1,0:T(8,128)}, f32[4,1536,256]{2,1,0:T(8,128)}) custom-call(s32[4]{0:T(128)S(1)} %pad_add_fusion.2.info_ref, bf16[2,3,256,1536]{3,2,1,0:T(8,128)(2,1)} %collective-permute-done.52.refs_0_.refs_1_, bf16[2,3,256,1536]{3,2,1,0:T(8,128)(2,1)} %collective-permute-done.52.refs_0_.refs_1_, ...), custom_call_target="tpu_custom_call" | custom-call | bytes 28311552 | tf_op jit(solution)/shard_map/place/pallas_call | solution.py:597
  (419 shorter events, 232.0 us)
Async XLA Ops:
  9.2 24.5 %collective-permute-start = (bf16[192,512]{1,0:T(8,128)(2,1)S(1)}, bf16[192,512]{1,0:T(8,128)(2,1)S(1)}, u32[]{:S(2)}, u32[]{:S(2)}) collective-permute-start(bf16[192,512]{1,0:T(8,128)(2,1)S(1)} %constant_dynamic-slice_fusion.8), channel_id=1, source_target_pairs={{0,8},{8,16},{16,24},{24,0},{1,9},{9,17},{17,25},{25,1},{2,10},{10... | collective-permute-start | bytes 589832 | tf_op jit(solution)/shard_map/ppermute | solution.py:28
  20.8 190.0 %all-gather.3.cloned.1.call-start = ((), (), s32[]{:S(2)}) async-start(), calls=%async_computation.4 | async-start | bytes 7077888 | tf_op jit(solution)/shard_map/all_gather | solution.py:710
  49.0 500.7 %all-reduce.2.cloned.1.call-start = ((), (), s32[]{:S(2)}) async-start(), calls=%async_computation.3 | async-start | bytes 9437184 | tf_op jit(solution)/shard_map/psum | solution.py:808
  160.7 27.8 %collective-permute-start.18 = (bf16[256,1664]{1,0:T(8,128)(2,1)S(1)}, bf16[256,1664]{1,0:T(8,128)(2,1)}, u32[]{:S(2)}, u32[]{:S(2)}) collective-permute-start(bf16[256,1664]{1,0:T(8,128)(2,1)S(1)} %concatenate.61.near_in.refs_0_), channel_id=1, source_target_pairs={{0,8},{8,16},{16,24},{24,0},{1,9},{9,17},{17,25},{25,1},{2,10},{10... | collective-permute-start | bytes 2555912 | tf_op jit(solution)/shard_map/ppermute | solution.py:28
  161.7 27.1 %collective-permute-start.20 = (bf16[256,1664]{1,0:T(8,128)(2,1)S(1)}, bf16[256,1664]{1,0:T(8,128)(2,1)}, u32[]{:S(2)}, u32[]{:S(2)}) collective-permute-start(bf16[256,1664]{1,0:T(8,128)(2,1)S(1)} %concatenate.61.near_in.refs_0_), channel_id=1, source_target_pairs={{0,1},{1,0},{2,3},{3,2},{4,5},{5,4},{6,7},{7,6},{8,9},{9,8},{10,11... | collective-permute-start | bytes 2555912 | tf_op jit(solution)/shard_map/ppermute | solution.py:32
  231.9 37.2 %collective-permute-start.28 = (bf16[256,1664]{1,0:T(8,128)(2,1)}, bf16[256,1664]{1,0:T(8,128)(2,1)S(1)}, u32[]{:S(2)}, u32[]{:S(2)}) collective-permute-start(bf16[256,1664]{1,0:T(8,128)(2,1)} %collective-permute-done.25.near_in.refs_6_), channel_id=1, source_target_pairs={{0,1},{1,0},{2,3},{3,2},{4,5},{5,4},{6,7},{7,6},{8,9},{9,8},{10,11... | collective-permute-start | bytes 2555912 | tf_op jit(solution)/shard_map/ppermute | solution.py:32
  232.7 36.0 %collective-permute-start.23 = (bf16[256,1664]{1,0:T(8,128)(2,1)}, bf16[256,1664]{1,0:T(8,128)(2,1)S(1)}, u32[]{:S(2)}, u32[]{:S(2)}) collective-permute-start(bf16[256,1664]{1,0:T(8,128)(2,1)} %get-tuple-element.129), channel_id=1, source_target_pairs={{0,1},{1,0},{2,3},{3,2},{4,5},{5,4},{6,7},{7,6},{8,9},{9,8},{10,11... | collective-permute-start | bytes 2555912 | tf_op jit(solution)/shard_map/ppermute | solution.py:32
  233.4 84.1 %collective-permute-start.22 = (bf16[512,1536]{1,0:T(8,128)(2,1)}, bf16[512,1536]{1,0:T(8,128)(2,1)}, u32[]{:S(2)}, u32[]{:S(2)}) collective-permute-start(bf16[512,1536]{1,0:T(8,128)(2,1)} %get-tuple-element.127), channel_id=1, source_target_pairs={{0,8},{8,16},{16,24},{24,0},{1,9},{9,17},{17,25},{25,1},{2,10},{10... | collective-permute-start | bytes 4718600 | tf_op jit(solution)/shard_map/ppermute | solution.py:28
  253.2 37.7 %collective-permute-start.27 = (bf16[256,1664]{1,0:T(8,128)(2,1)}, bf16[256,1664]{1,0:T(8,128)(2,1)S(1)}, u32[]{:S(2)}, u32[]{:S(2)}) collective-permute-start(bf16[256,1664]{1,0:T(8,128)(2,1)} %get-tuple-element.133), channel_id=1, source_target_pairs={{0,1},{1,0},{2,3},{3,2},{4,5},{5,4},{6,7},{7,6},{8,9},{9,8},{10,11... | collective-permute-start | bytes 2555912 | tf_op jit(solution)/shard_map/ppermute | solution.py:32
  289.5 28.0 %collective-permute-start.31 = (bf16[256,1664]{1,0:T(8,128)(2,1)}, bf16[256,1664]{1,0:T(8,128)(2,1)S(1)}, u32[]{:S(2)}, u32[]{:S(2)}) collective-permute-start(bf16[256,1664]{1,0:T(8,128)(2,1)} %get-tuple-element.151), channel_id=1, source_target_pairs={{0,1},{1,0},{2,3},{3,2},{4,5},{5,4},{6,7},{7,6},{8,9},{9,8},{10,11... | collective-permute-start | bytes 2555912 | tf_op jit(solution)/shard_map/ppermute | solution.py:32
  292.2 27.1 %collective-permute-start.30 = (bf16[256,1664]{1,0:T(8,128)(2,1)}, bf16[256,1664]{1,0:T(8,128)(2,1)S(1)}, u32[]{:S(2)}, u32[]{:S(2)}) collective-permute-start(bf16[256,1664]{1,0:T(8,128)(2,1)} %add_convert_fusion.7), channel_id=1, source_target_pairs={{0,8},{8,16},{16,24},{24,0},{1,9},{9,17},{17,25},{25,1},{2,10},{10... | collective-permute-start | bytes 2555912 | tf_op jit(solution)/shard_map/ppermute | solution.py:28
  312.7 29.0 %collective-permute-start.33 = (bf16[2,3,256,1536]{3,2,1,0:T(8,128)(2,1)}, bf16[2,3,256,1536]{3,2,1,0:T(8,128)(2,1)}, u32[]{:S(2)}, u32[]{:S(2)}) collective-permute-start(bf16[2,3,256,1536]{3,2,1,0:T(8,128)(2,1)} %expert_grads.2), channel_id=1, source_target_pairs={{0,2},{2,0},{1,3},{3,1},{4,6},{6,4},{5,7},{7,5},{8,10},{10,8},{9,1... | collective-permute-start | bytes 14155784 | tf_op jit(solution)/shard_map/ppermute | solution.py:32
  320.5 28.7 %collective-permute-start.32 = (bf16[256,1664]{1,0:T(8,128)(2,1)}, bf16[256,1664]{1,0:T(8,128)(2,1)S(1)}, u32[]{:S(2)}, u32[]{:S(2)}) collective-permute-start(bf16[256,1664]{1,0:T(8,128)(2,1)} %add_convert_fusion.6), channel_id=1, source_target_pairs={{0,8},{8,16},{16,24},{24,0},{1,9},{9,17},{17,25},{25,1},{2,10},{10... | collective-permute-start | bytes 2555912 | tf_op jit(solution)/shard_map/ppermute | solution.py:28
  358.8 40.3 %collective-permute-start.29 = (bf16[512,1536]{1,0:T(8,128)(2,1)}, bf16[512,1536]{1,0:T(8,128)(2,1)}, u32[]{:S(2)}, u32[]{:S(2)}) collective-permute-start(bf16[512,1536]{1,0:T(8,128)(2,1)} %add_convert_fusion.3), channel_id=1, source_target_pairs={{0,8},{8,16},{16,24},{24,0},{1,9},{9,17},{17,25},{25,1},{2,10},{10... | collective-permute-start | bytes 4718600 | tf_op jit(solution)/shard_map/ppermute | solution.py:28
  403.4 63.9 %collective-permute-start.36 = (bf16[512,1536]{1,0:T(8,128)(2,1)}, bf16[512,1536]{1,0:T(8,128)(2,1)}, u32[]{:S(2)}, u32[]{:S(2)}) collective-permute-start(bf16[512,1536]{1,0:T(8,128)(2,1)} %add_convert_fusion.2), channel_id=1, source_target_pairs={{0,8},{8,16},{16,24},{24,0},{1,9},{9,17},{17,25},{25,1},{2,10},{10... | collective-permute-start | bytes 4718600 | tf_op jit(solution)/shard_map/ppermute | solution.py:28
  411.5 38.2 %collective-permute-start.39 = (bf16[2,256,512]{2,1,0:T(8,128)(2,1)}, bf16[2,256,512]{2,1,0:T(8,128)(2,1)}, u32[]{:S(2)}, u32[]{:S(2)}) collective-permute-start(bf16[2,256,512]{2,1,0:T(8,128)(2,1)} %fusion.21), channel_id=1, source_target_pairs={{0,4},{4,0},{1,5},{5,1},{2,6},{6,2},{3,7},{7,3},{8,12},{12,8},{9,1... | collective-permute-start | bytes 1572872 | tf_op jit(solution)/shard_map/ppermute | solution.py:28
  428.4 50.4 %all-to-all-start.1 = ((bf16[4,192,768]{2,1,0:T(8,128)(2,1)}), bf16[4,192,768]{2,1,0:T(8,128)(2,1)}, u32[]{:S(2)}, u32[]{:S(2)}) async-start(bf16[4,192,768]{2,1,0:T(8,128)(2,1)} %add_convert_fusion.4), calls=%async_computation.1 | async-start | bytes 2359296 | tf_op jit(solution)/shard_map/all_to_all | solution.py:859
  459.7 76.6 %collective-permute-start.43 = (bf16[512,1536]{1,0:T(8,128)(2,1)}, bf16[512,1536]{1,0:T(8,128)(2,1)}, u32[]{:S(2)}, u32[]{:S(2)}) collective-permute-start(bf16[512,1536]{1,0:T(8,128)(2,1)} %get-tuple-element.244), channel_id=1, source_target_pairs={{0,1},{1,0},{2,3},{3,2},{4,5},{5,4},{6,7},{7,6},{8,9},{9,8},{10,11... | collective-permute-start | bytes 4718600 | tf_op jit(solution)/shard_map/ppermute | solution.py:32
  474.5 58.3 %collective-permute-start.42 = (bf16[256,1536]{1,0:T(8,128)(2,1)}, bf16[256,1536]{1,0:T(8,128)(2,1)}, u32[]{:S(2)}, u32[]{:S(2)}) collective-permute-start(bf16[256,1536]{1,0:T(8,128)(2,1)} %slice.129), channel_id=1, source_target_pairs={{0,1},{1,0},{2,3},{3,2},{4,5},{5,4},{6,7},{7,6},{8,9},{9,8},{10,11... | collective-permute-start | bytes 2359304 | tf_op jit(solution)/shard_map/ppermute | solution.py:32
  478.8 71.0 %all-to-all-start.2 = ((bf16[4,192,1280]{2,1,0:T(8,128)(2,1)}), bf16[4,192,1280]{2,1,0:T(8,128)(2,1)}, u32[]{:S(2)}, u32[]{:S(2)}) async-start(bf16[4,192,1280]{2,1,0:T(8,128)(2,1)} %pad_maximum_fusion.1), calls=%async_computation.2 | async-start | bytes 3932160 | tf_op jit(solution)/shard_map/all_to_all | solution.py:892
  486.6 28.9 %collective-permute-start.50 = (f32[18,384]{1,0:T(8,128)S(1)}, f32[18,384]{1,0:T(8,128)S(1)}, u32[]{:S(2)}, u32[]{:S(2)}) collective-permute-start(f32[18,384]{1,0:T(8,128)S(1)} %get-tuple-element.260), channel_id=1, source_target_pairs={{0,24},{8,0},{16,8},{24,16},{1,25},{9,1},{17,9},{25,17},{2,26},{10... | collective-permute-start | bytes 82952 | tf_op jit(solution)/shard_map/ppermute | solution.py:28
  489.9 41.6 %collective-permute-start.49 = (f32[18,384]{1,0:T(8,128)S(1)}, f32[18,384]{1,0:T(8,128)S(1)}, u32[]{:S(2)}, u32[]{:S(2)}) collective-permute-start(f32[18,384]{1,0:T(8,128)S(1)} %get-tuple-element.261), channel_id=1, source_target_pairs={{0,16},{8,24},{16,0},{24,8},{1,17},{9,25},{17,1},{25,9},{2,18},{10... | collective-permute-start | bytes 82952 | tf_op jit(solution)/shard_map/ppermute | solution.py:28
  489.9 41.6 %collective-permute-start.48 = (f32[18,384]{1,0:T(8,128)S(1)}, f32[18,384]{1,0:T(8,128)S(1)}, u32[]{:S(2)}, u32[]{:S(2)}) collective-permute-start(f32[18,384]{1,0:T(8,128)S(1)} %get-tuple-element.259), channel_id=1, source_target_pairs={{0,8},{8,16},{16,24},{24,0},{1,9},{9,17},{17,25},{25,1},{2,10},{10... | collective-permute-start | bytes 82952 | tf_op jit(solution)/shard_map/ppermute | solution.py:28
  515.6 23.6 %collective-permute-start.54 = (bf16[1,192,768]{2,1,0:T(8,128)(2,1)}, bf16[1,192,768]{2,1,0:T(8,128)(2,1)S(1)}, u32[]{:S(2)}, u32[]{:S(2)}) collective-permute-start(bf16[1,192,768]{2,1,0:T(8,128)(2,1)} %bitcast.130), channel_id=1, source_target_pairs={{0,4},{4,0},{1,5},{5,1},{2,6},{6,2},{3,7},{7,3},{8,12},{12,8},{9,1... | collective-permute-start | bytes 884744 | tf_op jit(solution)/shard_map/ppermute | solution.py:28
  (119 other events, 1344.0 us)
Sparse Core Ops, SparseCore 0:
  49.1 119.2 all-gather.2
  359.3 133.3 all-reduce.1
